TPU v7x, 32 devices: a whole 2x2x4 slice. The times are simulated.
32 devices in a mesh: gx: 2 (over y), gy: 16 (over z, x, core).
Axes of the slice: x: 2, y: 2, z: 4, core: 2. Of those that a mesh axis runs over, the one named last changes fastest.
Arguments:
- start_state: float32 [14, 8, 128, 256], P(None, None, 'gy', 'gx'), may hold values from -5 to 5, as said below
- final_adjoint: float32 [14, 8, 128, 256], P(None, None, 'gy', 'gx'), may hold values from -46 to 46
- face_words: int32 [2, 2, 2, 128, 256], P(None, None, None, 'gy', 'gx'), may hold values from 0 to 65535
- terrain: int32 [128, 256], P('gy', 'gx'), may hold values from 0 to 23
- drag_coef: float32 [24], replicated, may hold values from 0.05 to 1
Outputs:
- start_adjoint: float32 [14, 8, 128, 256], P(None, None, 'gy', 'gx')
- drag_grad: float32 [24], replicated
Inputs may be any that keep to these rules, and one draw needn't show every extreme that they name: `start_state`: fields 0, 5, 8 and 11 are masses between 0.5 and 3.5.
All inputs are finite; a program needn't handle non-finite values.
Results may differ from a plain program's by a relative error of at most 0.0003.
Values sent between devices are 32-bit elements; how exact they have to be, the bound alone decides.
No kernel may reach another device: no remote copies, remote signals or barrier semaphores. Data moves between devices by JAX's collectives and lax.ppermute only.
A program may use at most 64 MiB of HBM per device.

v0:
```python
import math

import jax
import jax.numpy as jnp
from jax import lax
from jax.experimental import pallas as pl
from jax.experimental.pallas import tpu as pltpu
from jax.sharding import PartitionSpec as P

LEV = 8
NCLASS = 24
FIELDS = 14
ROWS = 8
LANES = 128
PHASES = ((0, 5), (5, 3), (8, 3), (11, 3))
FACE = 0.3 * 0.5 * 0.5
COUPLING = 0.5
DRAG_STEP = 0.5


def roll(v, shift):
    return pltpu.roll(v, shift % LANES if isinstance(shift, int) else shift, 1)


def lane_ids():
    return lax.broadcasted_iota(jnp.int32, (8, LANES), 1)


def strip_pos():
    return lane_ids() % 16


def strip_row():
    return lane_ids() // 16


def level_bits():
    levels = lax.broadcasted_iota(jnp.int32, (8, LANES), 0)
    return [jnp.left_shift(jnp.ones_like(levels), levels + LEV * k) for k in range(2)]


def edge_lanes():
    lanes = lane_ids()
    return (lanes < 2) | (lanes >= LANES - 2)


def spread(ref, index):
    return jnp.broadcast_to(ref[pl.ds(index, 1), :], (8, LANES))


def plane(step, direction, pair):
    return step * 4 + direction * 2 + pair


def position(axis):
    return lax.axis_index(axis), lax.axis_size(axis)


def into_slots(values):
    pos = strip_pos() // 4
    total = jnp.zeros((8, LANES), jnp.float32)
    for slot, value in enumerate(values):
        total = jnp.where(pos == slot, value, total)
    return total


def add_edges(edges_ref, values, row):
    mine = strip_row() == row
    for f, value in enumerate(values):
        edges_ref[f] = jnp.where(mine, roll(value, 16 * row + 4), edges_ref[f])


def zero_edges(edges_ref, count=FIELDS):
    for f in range(count):
        edges_ref[f] = jnp.zeros((8, LANES), edges_ref.dtype)


def edge_payload(edges_ref, out_ref):
    for g in range(4):
        fields = range(4 * g, min(4 * g + 4, FIELDS))
        out_ref[g] = into_slots([roll(edges_ref[f], 4 * (f % 4) - 2) for f in fields])


def side_payloads(even_ref, odd_ref):
    index, _ = position("gx")
    is_even = index % 2 == 0

    def pick(k):
        a = even_ref[k]
        b = jnp.zeros_like(a) if odd_ref is None else odd_ref[k]
        return jnp.where(is_even, b, a), jnp.where(is_even, a, b)

    return pick


def build_strip(edges_ref, pick, strip_ref):
    pos = strip_pos()
    for g in range(4):
        left, right = pick(g)
        for f in range(4 * g, min(4 * g + 4, FIELDS)):
            q = f % 4
            own = edges_ref[f]
            value = jnp.where(pos < 4, own, roll(right, 2 - 4 * q))
            value = jnp.where(pos < 6, value, roll(left, 6 - 4 * q))
            value = jnp.where(pos < 8, value, roll(own, 4))
            strip_ref[f] = jnp.where(pos < 12, value, 0.0)


def strip_words(edge_words_ref, left_words, which):
    pos = strip_pos()
    own = spread(edge_words_ref, which)
    left = jnp.broadcast_to(left_words[which : which + 1], (8, LANES))
    value = jnp.where(pos < 4, own, roll(own, 4))
    return jnp.where(pos == 7, roll(left, 4), value)


def face_walls():
    gx, nx = position("gx")
    pos = strip_pos()
    shut = ((pos == 7) & (gx == 0)) | ((pos == 3) & (gx == nx - 1))
    return jnp.where(shut, 0.0, FACE)


def row_wall(j):
    gy, ny = position("gy")
    shut = ((j == 0) & (gy == 0)) | ((j == ROWS) & (gy == ny - 1))
    return jnp.where(shut, 0.0, FACE)


def inverse_root(mass):
    return lax.rsqrt(mass * mass + 1.0)


def gather_edges(v):
    pos = strip_pos()
    return jnp.where((pos == 4) | (pos == 5), roll(v, -4), v)


def face_values(behind, here, ahead, beyond, flag):
    return jnp.where(flag, 3.0 * here - behind, 3.0 * ahead - beyond)


def forward_strip(step, strip, edge_words, left_words, sfv, su, sdx):
    bits = level_bits()
    walls = face_walls()
    for p, (lead, members) in enumerate(PHASES):
        word = strip_words(edge_words, left_words, plane(step, 0, p // 2))
        flag = (word & bits[p % 2]) != 0
        u = strip[lead + 1] * inverse_root(strip[lead])
        speed = walls * (u + roll(u, -1))
        su[p] = speed
        for f in range(lead, lead + members):
            c = strip[f]
            ahead = roll(c, -1)
            value = face_values(roll(c, 1), c, ahead, roll(c, -2), flag)
            sfv[f] = value
            flux = speed * value
            sdx[f] = gather_edges(flux - roll(flux, 1))


def forward_rows(step, ext, words, low_words, fvy, vy):
    bits = level_bits()

    def face(j, carry):
        wall = row_wall(j)
        for p, (lead, members) in enumerate(PHASES):
            here = spread(words, plane(step, 1, p // 2) * ROWS + jnp.maximum(j - 1, 0))
            low = jnp.broadcast_to(low_words[plane(step, 1, p // 2)][None], (8, LANES))
            word = jnp.where(j == 0, low, here)
            flag = (word & bits[p % 2]) != 0
            v_low = ext[lead + 2, j + 1] * inverse_root(ext[lead, j + 1])
            v_high = ext[lead + 2, j + 2] * inverse_root(ext[lead, j + 2])
            vy[p, j] = wall * (v_low + v_high)
            for f in range(lead, lead + members):
                fvy[f, j] = face_values(ext[f, j], ext[f, j + 1], ext[f, j + 2], ext[f, j + 3], flag)
        return carry

    lax.fori_loop(0, ROWS + 1, face, 0)


def carried_row(step, r, ext, words, sdx, fvx, ux, fvy, vy):
    bits = level_bits()
    edges = edge_lanes()
    carried = []
    for p, (lead, members) in enumerate(PHASES):
        word = spread(words, plane(step, 0, p // 2) * ROWS + r)
        flag = (word & bits[p % 2]) != 0
        u = ext[lead + 1, r + 2] * inverse_root(ext[lead, r + 2])
        speed = FACE * (u + roll(u, -1))
        ux[p, r] = speed
        below, above = vy[p, r], vy[p, r + 1]
        for f in range(lead, lead + members):
            c = ext[f, r + 2]
            value = face_values(roll(c, 1), c, roll(c, -1), roll(c, -2), flag)
            fvx[f, r] = value
            flux = speed * value
            along_x = jnp.where(edges, roll(sdx[f], 124 - 16 * r), flux - roll(flux, 1))
            along_y = above * fvy[f, r + 1] - below * fvy[f, r]
            carried.append(c - along_x - along_y)
    return carried


def coupled(c):
    s = inverse_root(c[0])
    u, v = c[1] * s, c[2] * s
    gas_x, gas_y = c[1], c[2]
    out = [None] * FIELDS
    for lead, _ in PHASES[1:]:
        pull_x = COUPLING * (c[lead] * u - c[lead + 1])
        pull_y = COUPLING * (c[lead] * v - c[lead + 2])
        gas_x, gas_y = gas_x - pull_x, gas_y - pull_y
        out[lead] = c[lead]
        out[lead + 1], out[lead + 2] = c[lead + 1] + pull_x, c[lead + 2] + pull_y
    out[0], out[1], out[2], out[3], out[4] = c[0], gas_x, gas_y, c[3], c[4]
    return out, s, u, v


def stepped(c, drag):
    q, _, _, _ = coupled(c)
    for lead, _ in PHASES:
        s = inverse_root(q[lead])
        u, v = q[lead + 1] * s, q[lead + 2] * s
        factor = 1.0 - drag * jnp.sqrt(u * u + v * v + 1.0)
        q[lead + 1], q[lead + 2] = q[lead + 1] * factor, q[lead + 2] * factor
    return q


def stepped_back(c, drag, a):
    q, s0, gas_u, gas_v = coupled(c)
    a = list(a)
    drag_terms = jnp.zeros((8, LANES), jnp.float32)
    for lead, _ in PHASES:
        m, x, y = q[lead], q[lead + 1], q[lead + 2]
        s = s0 if lead == 0 else inverse_root(m)
        u, v = x * s, y * s
        energy = u * u + v * v
        root = lax.rsqrt(energy + 1.0)
        w = (energy + 1.0) * root
        dot = a[lead + 1] * x + a[lead + 2] * y
        drag_terms = drag_terms - w * dot
        k = drag * dot * root
        factor = 1.0 - drag * w
        ks = k * s
        a[lead + 1] = a[lead + 1] * factor - ks * u
        a[lead + 2] = a[lead + 2] * factor - ks * v
        a[lead] = a[lead] + k * energy * m * (s * s)
    du = jnp.zeros_like(drag_terms)
    dv = jnp.zeros_like(drag_terms)
    for lead, _ in PHASES[1:]:
        rx, ry = COUPLING * (a[lead + 1] - a[1]), COUPLING * (a[lead + 2] - a[2])
        a[lead] = a[lead] + rx * gas_u + ry * gas_v
        du, dv = du + c[lead] * rx, dv + c[lead] * ry
        a[lead + 1], a[lead + 2] = a[lead + 1] - rx, a[lead + 2] - ry
    a[1], a[2] = a[1] + du * s0, a[2] + dv * s0
    a[0] = a[0] - (gas_u * du + gas_v * dv) * c[0] * (s0 * s0)
    return a, drag_terms


def add_speed_terms(total, state, lead, du, dv):
    m, x, y = state
    s = inverse_root(m)
    pull = None
    if du is not None:
        total[lead + 1] = total[lead + 1] + s * du
        pull = x * s * du
    if dv is not None:
        total[lead + 2] = total[lead + 2] + s * dv
        pull = y * s * dv if pull is None else pull + y * s * dv
    total[lead] = total[lead] - pull * m * (s * s)


def scatter_x(a, value, speed, flag):
    ahead = roll(a, -1) - a
    g = speed * ahead
    low = jnp.where(flag, g, 0.0)
    high = roll(g - low, 1)
    return 3.0 * (low + high) - roll(low, -1) - roll(high, 1), value * ahead


def expand_edges(own):
    pos = strip_pos()
    value = jnp.where(pos < 4, own, jnp.where((pos >= 8) & (pos < 12), roll(own, 4), 0.0))
    return value


def backward_strip(step, strip, edges_a, edge_words, left_words, sfv, su, sdc, sdu, out_c):
    bits = level_bits()
    walls = face_walls()
    ghosts = []
    for p, (lead, members) in enumerate(PHASES):
        word = strip_words(edge_words, left_words, plane(step, 0, p // 2))
        flag = (word & bits[p % 2]) != 0
        speed = su[p]
        du = jnp.zeros((8, LANES), jnp.float32)
        total = {}
        for f in range(lead, lead + members):
            total[f], term = scatter_x(expand_edges(edges_a[f]), sfv[f], speed, flag)
            sdc[f] = gather_edges(total[f])
            du = du + term
        du = walls * du
        du = du + roll(du, 1)
        sdu[p] = gather_edges(du)
        add_speed_terms(total, (strip[lead], strip[lead + 1], strip[lead + 2]), lead, du, None)
        ghosts.extend(total[f] for f in range(lead, lead + members))
    for g in range(4):
        fields = range(4 * g, min(4 * g + 4, FIELDS))
        out_c[g] = into_slots([roll(ghosts[f], 4 * (f % 4) - 4) for f in fields])


def backward_fluxes(step, ext, words, low_words, a_ext, fvx, ux, fvy, vy, sdc, sdu, gl, gh, dvy, put):
    bits = level_bits()
    edges = edge_lanes()
    zero = jnp.zeros((8, LANES), jnp.float32)
    for k in (0, 1, 2, 12, 13, 14):
        for f in range(FIELDS):
            gl[f, k] = zero
            gh[f, k] = zero
        for p in range(4):
            dvy[p, k] = zero

    def face(j, carry):
        wall = row_wall(j)
        for p, (lead, members) in enumerate(PHASES):
            here = spread(words, plane(step, 1, p // 2) * ROWS + jnp.maximum(j - 1, 0))
            low_word = jnp.broadcast_to(low_words[plane(step, 1, p // 2)][None], (8, LANES))
            word = jnp.where(j == 0, low_word, here)
            flag = (word & bits[p % 2]) != 0
            speed = vy[p, j]
            dv = jnp.zeros((8, LANES), jnp.float32)
            for f in range(lead, lead + members):
                ahead = a_ext[f, j + 1] - a_ext[f, j]
                g = speed * ahead
                low = jnp.where(flag, g, 0.0)
                gl[f, j + 3] = low
                gh[f, j + 3] = g - low
                dv = dv + fvy[f, j] * ahead
            dvy[p, j + 3] = wall * dv
        return carry

    lax.fori_loop(0, ROWS + 1, face, 0)

    def along_y(f, i):
        return 3.0 * (gl[f, i + 4] + gh[f, i + 3]) - gl[f, i + 5] - gh[f, i + 2]

    def own(r, carry):
        total = [None] * FIELDS
        for p, (lead, members) in enumerate(PHASES):
            word = spread(words, plane(step, 0, p // 2) * ROWS + r)
            flag = (word & bits[p % 2]) != 0
            speed = ux[p, r]
            du = jnp.zeros((8, LANES), jnp.float32)
            for f in range(lead, lead + members):
                a = a_ext[f, r + 1]
                part, term = scatter_x(a, fvx[f, r], speed, flag)
                part = jnp.where(edges, roll(sdc[f], 124 - 16 * r), part)
                total[f] = a + part + along_y(f, r)
                du = du + term
            du = FACE * (du + roll(du, 1))
            du = jnp.where(edges, roll(sdu[p], 124 - 16 * r), du)
            dv = dvy[p, r + 4] + dvy[p, r + 3]
            state = (ext[lead, r + 2], ext[lead + 1, r + 2], ext[lead + 2, r + 2])
            add_speed_terms(total, state, lead, du, dv)
        put(r, total)
        return carry

    lax.fori_loop(0, ROWS, own, 0)

    def ghost(t, carry):
        i = jnp.where(t < 2, t - 2, t + 6)
        total = [along_y(f, i) for f in range(FIELDS)]
        for p, (lead, members) in enumerate(PHASES):
            dv = dvy[p, i + 4] + dvy[p, i + 3]
            state = (ext[lead, i + 2], ext[lead + 1, i + 2], ext[lead + 2, i + 2])
            add_speed_terms(total, state, lead, None, dv)
        put(i, total)
        return carry

    lax.fori_loop(0, 4, ghost, 0)


def drag_row(drag_ref, r):
    levels = lax.broadcasted_iota(jnp.int32, (8, LANES), 0)
    weight = jnp.full((8, LANES), DRAG_STEP, jnp.float32)
    for k in range(3):
        weight = jnp.where((levels // 2**k) % 2 == 1, weight * 0.5 ** (2**k), weight)
    return weight, weight * spread(drag_ref, r)


def drag_table(terrain, coef, drag_ref):
    classes = terrain[...]
    drag = jnp.zeros((8, LANES), jnp.float32)
    for k in range(NCLASS):
        drag = jnp.where(classes == k, coef[k], drag)
    drag_ref[...] = drag


def row_bases():
    gy, _ = position("gy")
    is_even = gy % 2 == 0
    return is_even


def fill_ghost_rows(ext, from_a, from_b):
    is_even = row_bases()
    a_row = jnp.where(is_even, ROWS + 2, 0)
    b_row = jnp.where(is_even, 0, ROWS + 2)
    for f in range(FIELDS):
        for j in range(2):
            ext[f, a_row + j] = from_a[2 * f + j]
            ext[f, b_row + j] = from_b[2 * f + j]


def put_edge_rows(source, offset, to_a, to_b):
    is_even = row_bases()
    a_row = jnp.where(is_even, ROWS - 2, 0) + offset
    b_row = jnp.where(is_even, 0, ROWS - 2) + offset
    for f in range(FIELDS):
        for j in range(2):
            to_a[2 * f + j] = source[f, a_row + j]
            to_b[2 * f + j] = source[f, b_row + j]


def pack_kernel(start, words, rows, edges, edge_words, to_a, to_b, to_c):
    zero_edges(edges)
    edge_words[...] = jnp.zeros((8, LANES), jnp.int32)

    def one_row(r, carry):
        values = [start[f, pl.ds(r, 8, stride=8), :] for f in range(FIELDS)]
        for f in range(FIELDS):
            rows[f, r] = values[f]
        add_edges(edges, values, r)
        mine = strip_row() == r
        edge_words[...] = jnp.where(mine, roll(words[pl.ds(r, 8, stride=8), :], 16 * r + 4), edge_words[...])
        return carry

    lax.fori_loop(0, ROWS, one_row, 0)
    put_edge_rows(rows, 0, to_a, to_b)
    top = words[pl.ds(ROWS - 1, 8, stride=8), :].astype(jnp.float32)
    to_a[2 * FIELDS] = top
    to_b[2 * FIELDS] = top
    edge_payload(edges, to_c)
    to_c[4] = edge_words[...].astype(jnp.float32)


def neighbour_words(from_a, from_b, pick):
    low = jnp.where(row_bases(), from_b[2 * FIELDS], from_a[2 * FIELDS]).astype(jnp.int32)
    left, _ = pick(4)
    return low, left.astype(jnp.int32)


def first_kernel(has_odd):
    def kernel(*refs):
        rows, edges, edge_words, words, terrain, coef, from_a, from_b, from_c = refs[:9]
        from_d = refs[9] if has_odd else None
        outs = refs[9 + has_odd :]
        (ext, strip, carried_ref, fvx, ux, fvy, vy, sfv, su, drag_ref, low_ref, left_ref) = outs[:12]
        middle, middle_edges, to_a, to_b, to_c = outs[12:17]
        (sdx,) = outs[17:]
        pick = side_payloads(from_c, from_d)

        def copy_row(r, carry):
            for f in range(FIELDS):
                ext[f, r + 2] = rows[f, r]
            return carry

        lax.fori_loop(0, ROWS, copy_row, 0)
        fill_ghost_rows(ext, from_a, from_b)
        build_strip(edges, pick, strip)
        low_words, left_words = neighbour_words(from_a, from_b, pick)
        low_ref[...] = low_words
        left_ref[...] = left_words
        drag_table(terrain, coef, drag_ref)
        forward_strip(0, strip, edge_words, left_words, sfv, su, sdx)
        forward_rows(0, ext, words, low_words, fvy, vy)
        zero_edges(middle_edges)

        def one_row(r, carry):
            c = carried_row(0, r, ext, words, sdx, fvx, ux, fvy, vy)
            for f in range(FIELDS):
                carried_ref[f, r] = c[f]
            _, drag = drag_row(drag_ref, r)
            q = stepped(c, drag)
            for f in range(FIELDS):
                middle[f, r] = q[f]
            add_edges(middle_edges, q, r)
            return carry

        lax.fori_loop(0, ROWS, one_row, 0)
        put_edge_rows(middle, 0, to_a, to_b)
        edge_payload(middle_edges, to_c)

    return kernel


def ghost_rows_out(part, to_a, to_b):
    is_even = row_bases()
    a_row = jnp.where(is_even, ROWS + 2, 0)
    b_row = jnp.where(is_even, 0, ROWS + 2)
    for f in range(FIELDS):
        for j in range(2):
            to_a[2 * f + j] = part[f, a_row + j]
            to_b[2 * f + j] = part[f, b_row + j]


def second_kernel(has_odd):
    def kernel(*refs):
        middle, middle_edges, edge_words, words, drag_ref, low_ref, left_ref, adjoint = refs[:8]
        from_a, from_b, from_c = refs[8:11]
        from_d = refs[11] if has_odd else None
        outs = refs[11 + has_odd :]
        part, to_a, to_b, to_c, grad_cells = outs[:5]
        (ext, strip, fvx, ux, fvy, vy, sfv, su, sdx, a_ext, edges_a, sdc, sdu, gl, gh, dvy) = outs[5:]
        pick = side_payloads(from_c, from_d)
        low_words, left_words = low_ref[...], left_ref[...]

        def copy_row(r, carry):
            for f in range(FIELDS):
                ext[f, r + 2] = middle[f, r]
            return carry

        lax.fori_loop(0, ROWS, copy_row, 0)
        fill_ghost_rows(ext, from_a, from_b)
        build_strip(middle_edges, pick, strip)
        forward_strip(1, strip, edge_words, left_words, sfv, su, sdx)
        forward_rows(1, ext, words, low_words, fvy, vy)
        zero_edges(edges_a)
        for f in range(FIELDS):
            a_ext[f, 0] = jnp.zeros((8, LANES), jnp.float32)
            a_ext[f, ROWS + 1] = jnp.zeros((8, LANES), jnp.float32)

        def one_row(r, carry):
            c = carried_row(1, r, ext, words, sdx, fvx, ux, fvy, vy)
            weight, drag = drag_row(drag_ref, r)
            a = [adjoint[f, pl.ds(r, 8, stride=8), :] for f in range(FIELDS)]
            a, terms = stepped_back(c, drag, a)
            grad_cells[pl.ds(r, 1), :] = jnp.sum(weight * terms, axis=0, keepdims=True)
            for f in range(FIELDS):
                a_ext[f, r + 1] = a[f]
            add_edges(edges_a, a, r)
            return carry

        lax.fori_loop(0, ROWS, one_row, 0)
        backward_strip(1, strip, edges_a, edge_words, left_words, sfv, su, sdc, sdu, to_c)

        def put(row, values):
            for f in range(FIELDS):
                part[f, row + 2] = values[f]

        backward_fluxes(1, ext, words, low_words, a_ext, fvx, ux, fvy, vy, sdc, sdu, gl, gh, dvy, put)
        ghost_rows_out(part, to_a, to_b)

    return kernel


def collect(part, from_a, from_b, pick, incoming):
    is_even = row_bases()
    a_row = jnp.where(is_even, ROWS, 2)
    b_row = jnp.where(is_even, 2, ROWS)
    for f in range(FIELDS):
        for j in range(2):
            part[f, a_row + j] = part[f, a_row + j] + from_a[2 * f + j]
            part[f, b_row + j] = part[f, b_row + j] + from_b[2 * f + j]
    pos = strip_pos()
    for g in range(4):
        left, right = pick(g)
        for f in range(4 * g, min(4 * g + 4, FIELDS)):
            q = f % 4
            at_left = (pos == 4) | (pos == 5)
            at_right = (pos == 2) | (pos == 3)
            value = jnp.where(at_left, roll(left, 4 - 4 * q), jnp.where(at_right, roll(right, -4 * q), 0.0))
            incoming[f] = value


def third_kernel(has_odd):
    def kernel(*refs):
        (part_in, grad_cells, terrain, ext, strip, carried_ref, fvx, ux, fvy, vy, sfv, su) = refs[:12]
        drag_ref, low_ref, left_ref, edge_words, words = refs[12:17]
        from_a, from_b, from_c = refs[17:20]
        from_d = refs[20] if has_odd else None
        outs = refs[20 + has_odd :]
        part, to_a, to_b, to_c, grads = outs[:5]
        (incoming, a_ext, edges_a, sdc, sdu, gl, gh, dvy, cells) = outs[5:]
        pick = side_payloads(from_c, from_d)
        low_words, left_words = low_ref[...], left_ref[...]

        def copy_row(r, carry):
            for f in range(FIELDS):
                part[f, r + 2] = part_in[f, r + 2]
            return carry

        lax.fori_loop(0, ROWS, copy_row, 0)
        collect(part, from_a, from_b, pick, incoming)
        zero_edges(edges_a)
        for f in range(FIELDS):
            a_ext[f, 0] = jnp.zeros((8, LANES), jnp.float32)
            a_ext[f, ROWS + 1] = jnp.zeros((8, LANES), jnp.float32)
        edges = edge_lanes()

        def one_row(r, carry):
            c = [carried_ref[f, r] for f in range(FIELDS)]
            weight, drag = drag_row(drag_ref, r)
            a = [
                part[f, r + 2] + jnp.where(edges, roll(incoming[f], 124 - 16 * r), 0.0)
                for f in range(FIELDS)
            ]
            a, terms = stepped_back(c, drag, a)
            cells[pl.ds(r, 1), :] = jnp.sum(weight * terms, axis=0, keepdims=True)
            for f in range(FIELDS):
                a_ext[f, r + 1] = a[f]
            add_edges(edges_a, a, r)
            return carry

        lax.fori_loop(0, ROWS, one_row, 0)
        total = cells[...] + grad_cells[...]
        classes = terrain[...]
        lanes = lane_ids()
        binned = jnp.zeros((8, LANES), jnp.float32)
        for k in range(NCLASS):
            one = jnp.sum(jnp.where(classes == k, total, 0.0), axis=0, keepdims=True)
            one = jnp.sum(one, axis=1, keepdims=True)
            binned = jnp.where(lanes == k, one, binned)
        grads[...] = binned
        backward_strip(0, strip, edges_a, edge_words, left_words, sfv, su, sdc, sdu, to_c)

        def put(row, values):
            for f in range(FIELDS):
                part[f, row + 2] = values[f]

        backward_fluxes(0, ext, words, low_words, a_ext, fvx, ux, fvy, vy, sdc, sdu, gl, gh, dvy, put)
        ghost_rows_out(part, to_a, to_b)

    return kernel


def last_kernel(has_odd):
    def kernel(*refs):
        part_in, from_a, from_b, from_c = refs[:4]
        from_d = refs[4] if has_odd else None
        out, part, incoming = refs[4 + has_odd :]
        pick = side_payloads(from_c, from_d)

        def copy_row(r, carry):
            for f in range(FIELDS):
                part[f, r + 2] = part_in[f, r + 2]
            return carry

        lax.fori_loop(0, ROWS, copy_row, 0)
        collect(part, from_a, from_b, pick, incoming)
        edges = edge_lanes()

        def one_row(r, carry):
            for f in range(FIELDS):
                value = part[f, r + 2] + jnp.where(edges, roll(incoming[f], 124 - 16 * r), 0.0)
                out[f, pl.ds(r, 8, stride=8), :] = value
            return carry

        lax.fori_loop(0, ROWS, one_row, 0)

    return kernel


def shaped(*shape, dtype=jnp.float32):
    return jax.ShapeDtypeStruct(shape, dtype)


def tiles(*shape, dtype=jnp.float32):
    return shaped(*shape, 8, LANES, dtype=dtype)


def scratch(*shape, dtype=jnp.float32):
    return pltpu.VMEM((*shape, 8, LANES), dtype)


def call(kernel, outs, scratches, args, smem=()):
    in_specs = [
        pl.BlockSpec(memory_space=pltpu.SMEM if k in smem else pltpu.VMEM) for k in range(len(args))
    ]
    return pl.pallas_call(
        kernel,
        out_shape=outs,
        in_specs=in_specs,
        out_specs=[pl.BlockSpec(memory_space=pltpu.VMEM)] * len(outs),
        scratch_shapes=scratches,
        compiler_params=pltpu.CompilerParams(vmem_limit_bytes=32 << 20),
    )(*args)


def swap(x, axis, first):
    peers = lax.axis_size(axis)
    pairs = [(i, i + 1) for i in range(first, peers - 1, 2)]
    if not pairs:
        return None
    return lax.ppermute(x, axis, pairs + [(j, i) for i, j in pairs])


def exchange(to_a, to_b, to_c):
    from_a = swap(to_a, "gy", 0)
    from_b = swap(to_b, "gy", 1)
    from_c = swap(to_c, "gx", 0)
    from_d = swap(to_c, "gx", 1)
    if from_b is None:
        from_b = jnp.zeros_like(to_b)
    return (from_a, from_b, from_c) + (() if from_d is None else (from_d,))


def summed_over(x, axis):
    peers = lax.axis_size(axis)
    distance = 1
    while distance < peers:
        x = x + lax.ppermute(x, axis, [(i, i ^ distance) for i in range(peers)])
        distance *= 2
    return x


def body(start_state, final_adjoint, face_words, terrain, drag_coef):
    has_odd = lax.axis_size("gx") > 2
    start = start_state.reshape(FIELDS, LEV * ROWS, LANES)
    adjoint = final_adjoint.reshape(FIELDS, LEV * ROWS, LANES)
    words = face_words.reshape(8 * ROWS, LANES)
    ints = jnp.int32

    rows, edges, edge_words, to_a, to_b, to_c = call(
        pack_kernel,
        [tiles(14, 8), tiles(14), tiles(dtype=ints), tiles(29), tiles(29), tiles(5)],
        [],
        [start, words],
    )
    got = exchange(to_a, to_b, to_c)
    faces = [tiles(14, 8), tiles(4, 8), tiles(14, 9), tiles(4, 9), tiles(14), tiles(4)]
    res = call(
        first_kernel(has_odd),
        [tiles(14, 12), tiles(14), tiles(14, 8), *faces, tiles(), tiles(dtype=ints), tiles(dtype=ints)]
        + [tiles(14, 8), tiles(14), tiles(28), tiles(28), tiles(4)],
        [scratch(14)],
        [rows, edges, edge_words, words, terrain, drag_coef, *got],
        smem=(5,),
    )
    ext, strip, carried_ref = res[:3]
    saved = res[3:9]
    drag_ref, low_ref, left_ref = res[9:12]
    middle, middle_edges = res[12:14]
    got = exchange(*res[14:17])
    back = [scratch(14, 10), scratch(14), scratch(14), scratch(4), scratch(14, 15), scratch(14, 15), scratch(4, 15)]
    part, to_a, to_b, to_c, grad_cells = call(
        second_kernel(has_odd),
        [tiles(14, 12), tiles(28), tiles(28), tiles(4), tiles()],
        [scratch(14, 12), scratch(14), scratch(14, 8), scratch(4, 8), scratch(14, 9), scratch(4, 9)]
        + [scratch(14), scratch(4), scratch(14), *back],
        [middle, middle_edges, edge_words, words, drag_ref, low_ref, left_ref, adjoint, *got],
    )
    got = exchange(to_a, to_b, to_c)
    part, to_a, to_b, to_c, grads = call(
        third_kernel(has_odd),
        [tiles(14, 12), tiles(28), tiles(28), tiles(4), tiles()],
        [scratch(14), *back, scratch()],
        [part, grad_cells, terrain, ext, strip, carried_ref, *saved]
        + [drag_ref, low_ref, left_ref, edge_words, words, *got],
    )
    got = exchange(to_a, to_b, to_c)
    (out,) = call(
        last_kernel(has_odd),
        [shaped(FIELDS, LEV * ROWS, LANES)],
        [scratch(14, 12), scratch(14)],
        [part, *got],
    )
    total_cells = terrain.size * lax.axis_size("gx") * lax.axis_size("gy") * LEV
    grad_scale = math.sqrt(NCLASS / total_cells)
    summed = summed_over(summed_over(grads, "gy"), "gx")[0, :NCLASS]
    return (out.reshape(start_state.shape), summed * grad_scale)


def solution(mesh):
    placed = (
        P(None, None, "gy", "gx"),
        P(None, None, "gy", "gx"),
        P(None, None, None, "gy", "gx"),
        P("gy", "gx"),
        P(),
    )
    return jax.shard_map(
        body,
        mesh=mesh,
        in_specs=placed,
        out_specs=(P(None, None, "gy", "gx"), P()),
        check_vma=False,
    )
```

profile of v0, /device:TPU:9, one launch (start us, length us, event | category | flops | bytes accessed | tf_op | source)
XLA Modules:
  0.0 64.2 jit_solution(7128253699254911219)
XLA Ops:
  0.6 0.7 %copy-done = s32[2,2,2,8,128]{4,3,2,1,0:T(8,128)S(1)} copy-done((s32[2,2,2,8,128]{4,3,2,1,0:T(8,128)S(1)}, s32[2,2,2,8,128]{4,3,2,1,0:T(8,128)}, u32[]{:S(2)}) %copy-start) | copy-done | bytes 32792
  1.4 1.0 %copy-done.2 = f32[14,8,8,128]{3,2,1,0:T(8,128)S(1)} copy-done((f32[14,8,8,128]{3,2,1,0:T(8,128)S(1)}, f32[14,8,8,128]{3,2,1,0:T(8,128)}, u32[]{:S(2)}) %copy-start.2) | copy-done | bytes 458776
  2.4 0.8 %shard_map.68 = (f32[14,8,8,128]{3,2,1,0:T(8,128)S(1)}, f32[14,8,128]{2,1,0:T(8,128)S(1)}, s32[8,128]{1,0:T(8,128)S(1)}, f32[29,8,128]{2,1,0:T(8,128)S(1)}, f32[...) custom-call(f32[14,64,128]{2,1,0:T(8,128)S(1)} %bitcast.10, s32[64,128]{1,0:T(8,128)S(1)} %bitcast.6), custom_call_target="tpu_custom_call" | custom-call | tf_op jit(solution)/shard_map/pallas_call | solution.py:678
  3.2 0.7 %collective-permute-start = (f32[29,8,128]{2,1,0:T(8,128)S(1)}, f32[29,8,128]{2,1,0:T(8,128)S(1)}, u32[]{:S(2)}, u32[]{:S(2)}) collective-permute-start(f32[29,8,128]{2,1,0:T(8,128)S(1)} %get-tuple-element.38), channel_id=1, source_target_pairs={{0,1},{2,3},{4,5},{6,7},{8,9},{10,11},{12,13},{14,15},{1,0},{3,2},... | collective-permute-start | bytes 356360 | tf_op jit(solution)/shard_map/ppermute | solution.py:693
  3.9 3.1 %collective-permute-start.1 = (f32[29,8,128]{2,1,0:T(8,128)S(1)}, f32[29,8,128]{2,1,0:T(8,128)S(1)}, u32[]{:S(2)}, u32[]{:S(2)}) collective-permute-start(f32[29,8,128]{2,1,0:T(8,128)S(1)} %get-tuple-element.39), channel_id=1, source_target_pairs={{1,2},{3,4},{5,6},{7,8},{9,10},{11,12},{13,14},{2,1},{4,3},{6,5},{... | collective-permute-start | bytes 356360 | tf_op jit(solution)/shard_map/ppermute | solution.py:693
  7.1 1.3 %collective-permute-start.2 = (f32[5,8,128]{2,1,0:T(8,128)S(1)}, f32[5,8,128]{2,1,0:T(8,128)S(1)}, u32[]{:S(2)}, u32[]{:S(2)}) collective-permute-start(f32[5,8,128]{2,1,0:T(8,128)S(1)} %get-tuple-element.40), channel_id=1, source_target_pairs={{0,16},{16,0},{1,17},{17,1},{2,18},{18,2},{3,19},{19,3},{4,20},{20... | collective-permute-start | bytes 61448 | tf_op jit(solution)/shard_map/ppermute | solution.py:693
  8.4 1.7 %collective-permute-done.2.refs_8_ = f32[5,8,128]{2,1,0:T(8,128)S(1)} collective-permute-done((f32[5,8,128]{2,1,0:T(8,128)S(1)}, f32[5,8,128]{2,1,0:T(8,128)S(1)}, u32[]{:S(2)}, u32[]{:S(2)}) %collective-permute-start.2) | collective-permute-done | bytes 20512 | tf_op jit(solution)/shard_map/ppermute | solution.py:693
  10.1 1.3 %collective-permute-done.1.refs_7_ = f32[29,8,128]{2,1,0:T(8,128)S(1)} collective-permute-done((f32[29,8,128]{2,1,0:T(8,128)S(1)}, f32[29,8,128]{2,1,0:T(8,128)S(1)}, u32[]{:S(2)}, u32[]{:S(2)}) %collective-permute-start.1) | collective-permute-done | bytes 118816 | tf_op jit(solution)/shard_map/ppermute | solution.py:693
  11.4 3.6 %shard_map.69 = (f32[14,12,8,128]{3,2,1,0:T(8,128)S(1)}, f32[14,8,128]{2,1,0:T(8,128)S(1)}, f32[14,8,8,128]{3,2,1,0:T(8,128)S(1)}, f32[14,8,8,128]{3,2,1,0:T(8,1...) custom-call(f32[14,8,8,128]{3,2,1,0:T(8,128)S(1)} %get-tuple-element, ...), custom_call_target="tpu_custom_call" | custom-call | tf_op jit(solution)/shard_map/pallas_call | solution.py:678
  15.0 3.1 %collective-permute-start.4 = (f32[28,8,128]{2,1,0:T(8,128)S(1)}, f32[28,8,128]{2,1,0:T(8,128)S(1)}, u32[]{:S(2)}, u32[]{:S(2)}) collective-permute-start(f32[28,8,128]{2,1,0:T(8,128)S(1)} %get-tuple-element.47), channel_id=1, source_target_pairs={{1,2},{3,4},{5,6},{7,8},{9,10},{11,12},{13,14},{2,1},{4,3},{6,5},{... | collective-permute-start | bytes 344072 | tf_op jit(solution)/shard_map/ppermute | solution.py:693
  18.2 1.3 %collective-permute-start.5 = (f32[4,8,128]{2,1,0:T(8,128)S(1)}, f32[4,8,128]{2,1,0:T(8,128)S(1)}, u32[]{:S(2)}, u32[]{:S(2)}) collective-permute-start(f32[4,8,128]{2,1,0:T(8,128)S(1)} %get-tuple-element.48), channel_id=1, source_target_pairs={{0,16},{16,0},{1,17},{17,1},{2,18},{18,2},{3,19},{19,3},{4,20},{20... | collective-permute-start | bytes 49160 | tf_op jit(solution)/shard_map/ppermute | solution.py:693
  19.5 1.6 %collective-permute-done.5.refs_10_ = f32[4,8,128]{2,1,0:T(8,128)S(1)} collective-permute-done((f32[4,8,128]{2,1,0:T(8,128)S(1)}, f32[4,8,128]{2,1,0:T(8,128)S(1)}, u32[]{:S(2)}, u32[]{:S(2)}) %collective-permute-start.5) | collective-permute-done | bytes 16416 | tf_op jit(solution)/shard_map/ppermute | solution.py:693
  21.1 1.3 %collective-permute-done.4.refs_9_ = f32[28,8,128]{2,1,0:T(8,128)S(1)} collective-permute-done((f32[28,8,128]{2,1,0:T(8,128)S(1)}, f32[28,8,128]{2,1,0:T(8,128)S(1)}, u32[]{:S(2)}, u32[]{:S(2)}) %collective-permute-start.4) | collective-permute-done | bytes 114720 | tf_op jit(solution)/shard_map/ppermute | solution.py:693
  22.4 5.7 %shard_map.70 = (f32[14,12,8,128]{3,2,1,0:T(8,128)S(1)}, f32[28,8,128]{2,1,0:T(8,128)S(1)}, f32[28,8,128]{2,1,0:T(8,128)S(1)}, f32[4,8,128]{2,1,0:T(8,128)S(1)}, f32[8,128]{1,0:T(8,128)S(1)}) custom-call(f32[14,8,8,128]{3,2,1,0:T(8,128)S(1)} %get-tuple-element.41.refs_0_, f32[14,8,128]{2,1,0:T(8,128)S(1)} %get-tuple-element.42.refs_1_, ...), custom_call_target="tpu_custom_call" | custom-call | tf_op jit(solution)/shard_map/pallas_call | solution.py:678
  28.1 0.3 collective-permute-start.6
  28.4 2.9 %collective-permute-start.7 = (f32[28,8,128]{2,1,0:T(8,128)S(1)}, f32[28,8,128]{2,1,0:T(8,128)S(1)}, u32[]{:S(2)}, u32[]{:S(2)}) collective-permute-start(f32[28,8,128]{2,1,0:T(8,128)S(1)} %get-tuple-element.61), channel_id=1, source_target_pairs={{1,2},{3,4},{5,6},{7,8},{9,10},{11,12},{13,14},{2,1},{4,3},{6,5},{... | collective-permute-start | bytes 344072 | tf_op jit(solution)/shard_map/ppermute | solution.py:693
  31.3 1.3 %collective-permute-start.8 = (f32[4,8,128]{2,1,0:T(8,128)S(1)}, f32[4,8,128]{2,1,0:T(8,128)S(1)}, u32[]{:S(2)}, u32[]{:S(2)}) collective-permute-start(f32[4,8,128]{2,1,0:T(8,128)S(1)} %get-tuple-element.62), channel_id=1, source_target_pairs={{0,16},{16,0},{1,17},{17,1},{2,18},{18,2},{3,19},{19,3},{4,20},{20... | collective-permute-start | bytes 49160 | tf_op jit(solution)/shard_map/ppermute | solution.py:693
  32.6 1.6 %collective-permute-done.8.refs_19_ = f32[4,8,128]{2,1,0:T(8,128)S(1)} collective-permute-done((f32[4,8,128]{2,1,0:T(8,128)S(1)}, f32[4,8,128]{2,1,0:T(8,128)S(1)}, u32[]{:S(2)}, u32[]{:S(2)}) %collective-permute-start.8) | collective-permute-done | bytes 16416 | tf_op jit(solution)/shard_map/ppermute | solution.py:693
  34.3 1.5 %collective-permute-done.7.refs_18_ = f32[28,8,128]{2,1,0:T(8,128)S(1)} collective-permute-done((f32[28,8,128]{2,1,0:T(8,128)S(1)}, f32[28,8,128]{2,1,0:T(8,128)S(1)}, u32[]{:S(2)}, u32[]{:S(2)}) %collective-permute-start.7) | collective-permute-done | bytes 114720 | tf_op jit(solution)/shard_map/ppermute | solution.py:693
  35.8 4.3 %shard_map.71 = (f32[14,12,8,128]{3,2,1,0:T(8,128)S(1)}, f32[28,8,128]{2,1,0:T(8,128)S(1)}, f32[28,8,128]{2,1,0:T(8,128)S(1)}, f32[4,8,128]{2,1,0:T(8,128)S(1)}, f32[8,128]{1,0:T(8,128)S(1)}) custom-call(f32[14,12,8,128]{3,2,1,0:T(8,128)S(1)} %get-tuple-element.49.refs_0_, f32[8,128]{1,0:T(8,128)S(1)} %get-tuple-element.50.refs_1_, s32[8,128]{1,0:T(8,128)S(1)} %copy-done.4, ...), custom_call_target="tpu_custom_call" | custom-call | tf_op jit(solution)/shard_map/pallas_call | solution.py:678
  40.2 1.1 %collective-permute-done.12 = f32[8,128]{1,0:T(8,128)S(1)} collective-permute-done((f32[8,128]{1,0:T(8,128)S(1)}, f32[8,128]{1,0:T(8,128)S(1)}, u32[]{:S(2)}, u32[]{:S(2)}) %collective-permute-start.12) | collective-permute-done | bytes 4128 | tf_op jit(solution)/shard_map/ppermute | solution.py:710
  41.3 0.7 %collective-permute-start.13 = (f32[8,128]{1,0:T(8,128)S(1)}, f32[8,128]{1,0:T(8,128)S(1)}, u32[]{:S(2)}, u32[]{:S(2)}) collective-permute-start(f32[8,128]{1,0:T(8,128)S(1)} %add.15), channel_id=1, source_target_pairs={{0,2},{1,3},{2,0},{3,1},{4,6},{5,7},{6,4},{7,5},{8,10},{9,11},{10,... | collective-permute-start | bytes 12296 | tf_op jit(solution)/shard_map/ppermute | solution.py:710
  42.1 1.7 %collective-permute-done.13 = f32[8,128]{1,0:T(8,128)S(1)} collective-permute-done((f32[8,128]{1,0:T(8,128)S(1)}, f32[8,128]{1,0:T(8,128)S(1)}, u32[]{:S(2)}, u32[]{:S(2)}) %collective-permute-start.13) | collective-permute-done | bytes 4128 | tf_op jit(solution)/shard_map/ppermute | solution.py:710
  43.8 2.5 %collective-permute-done.14 = f32[8,128]{1,0:T(8,128)S(1)} collective-permute-done((f32[8,128]{1,0:T(8,128)S(1)}, f32[8,128]{1,0:T(8,128)S(1)}, u32[]{:S(2)}, u32[]{:S(2)}) %collective-permute-start.14) | collective-permute-done | bytes 4128 | tf_op jit(solution)/shard_map/ppermute | solution.py:710
  46.2 2.3 %collective-permute-start.15 = (f32[8,128]{1,0:T(8,128)S(1)}, f32[8,128]{1,0:T(8,128)S(1)}, u32[]{:S(2)}, u32[]{:S(2)}) collective-permute-start(f32[8,128]{1,0:T(8,128)S(1)} %add.17), channel_id=1, source_target_pairs={{0,8},{1,9},{2,10},{3,11},{4,12},{5,13},{6,14},{7,15},{8,0},{9,1},... | collective-permute-start | bytes 12296 | tf_op jit(solution)/shard_map/ppermute | solution.py:710
  48.6 1.0 %collective-permute-done.15 = f32[8,128]{1,0:T(8,128)S(1)} collective-permute-done((f32[8,128]{1,0:T(8,128)S(1)}, f32[8,128]{1,0:T(8,128)S(1)}, u32[]{:S(2)}, u32[]{:S(2)}) %collective-permute-start.15) | collective-permute-done | bytes 4128 | tf_op jit(solution)/shard_map/ppermute | solution.py:710
  49.6 1.2 %collective-permute-start.16 = (f32[8,128]{1,0:T(8,128)S(1)}, f32[8,128]{1,0:T(8,128)S(1)}, u32[]{:S(2)}, u32[]{:S(2)}) collective-permute-start(f32[8,128]{1,0:T(8,128)S(1)} %add.18), channel_id=1, source_target_pairs={{0,16},{16,0},{1,17},{17,1},{2,18},{18,2},{3,19},{19,3},{4,20},{20... | collective-permute-start | bytes 12296 | tf_op jit(solution)/shard_map/ppermute | solution.py:710
  51.1 4.2 %collective-permute-start.9 = (f32[28,8,128]{2,1,0:T(8,128)S(1)}, f32[28,8,128]{2,1,0:T(8,128)S(1)}, u32[]{:S(2)}, u32[]{:S(2)}) collective-permute-start(f32[28,8,128]{2,1,0:T(8,128)S(1)} %get-tuple-element.64), channel_id=1, source_target_pairs={{0,1},{2,3},{4,5},{6,7},{8,9},{10,11},{12,13},{14,15},{1,0},{3,2},... | collective-permute-start | bytes 344072 | tf_op jit(solution)/shard_map/ppermute | solution.py:693
  55.3 2.5 %collective-permute-start.10 = (f32[28,8,128]{2,1,0:T(8,128)S(1)}, f32[28,8,128]{2,1,0:T(8,128)S(1)}, u32[]{:S(2)}, u32[]{:S(2)}) collective-permute-start(f32[28,8,128]{2,1,0:T(8,128)S(1)} %get-tuple-element.65), channel_id=1, source_target_pairs={{1,2},{3,4},{5,6},{7,8},{9,10},{11,12},{13,14},{2,1},{4,3},{6,5},{... | collective-permute-start | bytes 344072 | tf_op jit(solution)/shard_map/ppermute | solution.py:693
  57.8 0.5 multiply_bitcast_fusion
  58.3 4.3 %collective-permute-done.10.refs_2_ = f32[28,8,128]{2,1,0:T(8,128)S(1)} collective-permute-done((f32[28,8,128]{2,1,0:T(8,128)S(1)}, f32[28,8,128]{2,1,0:T(8,128)S(1)}, u32[]{:S(2)}, u32[]{:S(2)}) %collective-permute-start.10) | collective-permute-done | bytes 114720 | tf_op jit(solution)/shard_map/ppermute | solution.py:693
  62.6 1.6 %shard_map.72 = f32[14,64,128]{2,1,0:T(8,128)} custom-call(f32[14,12,8,128]{3,2,1,0:T(8,128)S(1)} %get-tuple-element.63.refs_0_, f32[28,8,128]{2,1,0:T(8,128)S(1)} %collective-permute-done.9.refs_1_, f32[28,8,128]{2,1,0:T(8,128)S(1)} %collective-permute-done.10.refs_2_, f32[4,8,128]{2,1,0:T(8,128)S(1)} %collective-permute-done.11.refs_3_), custom_call_target="tpu_custom_call" | custom-call | tf_op jit(solution)/shard_map/pallas_call | solution.py:678
  (25 shorter events, 0.4 us)
Async XLA Ops:
  0.6 0.8 %copy-start = (s32[2,2,2,8,128]{4,3,2,1,0:T(8,128)S(1)}, s32[2,2,2,8,128]{4,3,2,1,0:T(8,128)}, u32[]{:S(2)}) copy-start(s32[2,2,2,8,128]{4,3,2,1,0:T(8,128)} %param.7) | copy-start | bytes 98308
  1.4 1.0 %copy-start.2 = (f32[14,8,8,128]{3,2,1,0:T(8,128)S(1)}, f32[14,8,8,128]{3,2,1,0:T(8,128)}, u32[]{:S(2)}) copy-start(f32[14,8,8,128]{3,2,1,0:T(8,128)} %param.5) | copy-start | bytes 1376260
  2.4 9.0 %copy-start.1 = (s32[2,2,2,8,128]{4,3,2,1,0:T(8,128)S(1)}, s32[2,2,2,8,128]{4,3,2,1,0:T(8,128)}, u32[]{:S(2)}) copy-start(s32[2,2,2,8,128]{4,3,2,1,0:T(8,128)} %param.7) | copy-start | bytes 98308
  2.4 9.0 %copy-start.4 = (s32[8,128]{1,0:T(8,128)S(1)}, s32[8,128]{1,0:T(8,128)}, u32[]{:S(2)}) copy-start(s32[8,128]{1,0:T(8,128)} %refs_2_.1) | copy-start | bytes 12292
  2.4 9.0 %copy-start.5 = (f32[24]{0:T(128)S(1)}, f32[24]{0:T(128)}, u32[]{:S(2)}) copy-start(f32[24]{0:T(128)} %refs_5_.1) | copy-start | bytes 292
  3.2 19.2 %copy-start.3 = (f32[14,8,8,128]{3,2,1,0:T(8,128)S(1)}, f32[14,8,8,128]{3,2,1,0:T(8,128)}, u32[]{:S(2)}) copy-start(f32[14,8,8,128]{3,2,1,0:T(8,128)} %param.6) | copy-start | bytes 1376260
  3.2 6.9 %collective-permute-start = (f32[29,8,128]{2,1,0:T(8,128)S(1)}, f32[29,8,128]{2,1,0:T(8,128)S(1)}, u32[]{:S(2)}, u32[]{:S(2)}) collective-permute-start(f32[29,8,128]{2,1,0:T(8,128)S(1)} %get-tuple-element.38), channel_id=1, source_target_pairs={{0,1},{2,3},{4,5},{6,7},{8,9},{10,11},{12,13},{14,15},{1,0},{3,2},... | collective-permute-start | bytes 356360 | tf_op jit(solution)/shard_map/ppermute | solution.py:693
  3.9 7.4 %collective-permute-start.1 = (f32[29,8,128]{2,1,0:T(8,128)S(1)}, f32[29,8,128]{2,1,0:T(8,128)S(1)}, u32[]{:S(2)}, u32[]{:S(2)}) collective-permute-start(f32[29,8,128]{2,1,0:T(8,128)S(1)} %get-tuple-element.39), channel_id=1, source_target_pairs={{1,2},{3,4},{5,6},{7,8},{9,10},{11,12},{13,14},{2,1},{4,3},{6,5},{... | collective-permute-start | bytes 356360 | tf_op jit(solution)/shard_map/ppermute | solution.py:693
  7.1 3.0 %collective-permute-start.2 = (f32[5,8,128]{2,1,0:T(8,128)S(1)}, f32[5,8,128]{2,1,0:T(8,128)S(1)}, u32[]{:S(2)}, u32[]{:S(2)}) collective-permute-start(f32[5,8,128]{2,1,0:T(8,128)S(1)} %get-tuple-element.40), channel_id=1, source_target_pairs={{0,16},{16,0},{1,17},{17,1},{2,18},{18,2},{3,19},{19,3},{4,20},{20... | collective-permute-start | bytes 61448 | tf_op jit(solution)/shard_map/ppermute | solution.py:693
  15.0 6.2 %collective-permute-start.3 = (f32[28,8,128]{2,1,0:T(8,128)S(1)}, f32[28,8,128]{2,1,0:T(8,128)S(1)}, u32[]{:S(2)}, u32[]{:S(2)}) collective-permute-start(f32[28,8,128]{2,1,0:T(8,128)S(1)} %get-tuple-element.46), channel_id=1, source_target_pairs={{0,1},{2,3},{4,5},{6,7},{8,9},{10,11},{12,13},{14,15},{1,0},{3,2},... | collective-permute-start | bytes 344072 | tf_op jit(solution)/shard_map/ppermute | solution.py:693
  15.0 7.3 %collective-permute-start.4 = (f32[28,8,128]{2,1,0:T(8,128)S(1)}, f32[28,8,128]{2,1,0:T(8,128)S(1)}, u32[]{:S(2)}, u32[]{:S(2)}) collective-permute-start(f32[28,8,128]{2,1,0:T(8,128)S(1)} %get-tuple-element.47), channel_id=1, source_target_pairs={{1,2},{3,4},{5,6},{7,8},{9,10},{11,12},{13,14},{2,1},{4,3},{6,5},{... | collective-permute-start | bytes 344072 | tf_op jit(solution)/shard_map/ppermute | solution.py:693
  18.2 2.9 %collective-permute-start.5 = (f32[4,8,128]{2,1,0:T(8,128)S(1)}, f32[4,8,128]{2,1,0:T(8,128)S(1)}, u32[]{:S(2)}, u32[]{:S(2)}) collective-permute-start(f32[4,8,128]{2,1,0:T(8,128)S(1)} %get-tuple-element.48), channel_id=1, source_target_pairs={{0,16},{16,0},{1,17},{17,1},{2,18},{18,2},{3,19},{19,3},{4,20},{20... | collective-permute-start | bytes 49160 | tf_op jit(solution)/shard_map/ppermute | solution.py:693
  28.1 6.2 %collective-permute-start.6 = (f32[28,8,128]{2,1,0:T(8,128)S(1)}, f32[28,8,128]{2,1,0:T(8,128)S(1)}, u32[]{:S(2)}, u32[]{:S(2)}) collective-permute-start(f32[28,8,128]{2,1,0:T(8,128)S(1)} %get-tuple-element.60), channel_id=1, source_target_pairs={{0,1},{2,3},{4,5},{6,7},{8,9},{10,11},{12,13},{14,15},{1,0},{3,2},... | collective-permute-start | bytes 344072 | tf_op jit(solution)/shard_map/ppermute | solution.py:693
  28.4 7.3 %collective-permute-start.7 = (f32[28,8,128]{2,1,0:T(8,128)S(1)}, f32[28,8,128]{2,1,0:T(8,128)S(1)}, u32[]{:S(2)}, u32[]{:S(2)}) collective-permute-start(f32[28,8,128]{2,1,0:T(8,128)S(1)} %get-tuple-element.61), channel_id=1, source_target_pairs={{1,2},{3,4},{5,6},{7,8},{9,10},{11,12},{13,14},{2,1},{4,3},{6,5},{... | collective-permute-start | bytes 344072 | tf_op jit(solution)/shard_map/ppermute | solution.py:693
  31.3 2.9 %collective-permute-start.8 = (f32[4,8,128]{2,1,0:T(8,128)S(1)}, f32[4,8,128]{2,1,0:T(8,128)S(1)}, u32[]{:S(2)}, u32[]{:S(2)}) collective-permute-start(f32[4,8,128]{2,1,0:T(8,128)S(1)} %get-tuple-element.62), channel_id=1, source_target_pairs={{0,16},{16,0},{1,17},{17,1},{2,18},{18,2},{3,19},{19,3},{4,20},{20... | collective-permute-start | bytes 49160 | tf_op jit(solution)/shard_map/ppermute | solution.py:693
  40.1 1.2 %collective-permute-start.12 = (f32[8,128]{1,0:T(8,128)S(1)}, f32[8,128]{1,0:T(8,128)S(1)}, u32[]{:S(2)}, u32[]{:S(2)}) collective-permute-start(f32[8,128]{1,0:T(8,128)S(1)} %get-tuple-element.67), channel_id=1, source_target_pairs={{0,1},{1,0},{2,3},{3,2},{4,5},{5,4},{6,7},{7,6},{8,9},{9,8},{10,11... | collective-permute-start | bytes 12296 | tf_op jit(solution)/shard_map/ppermute | solution.py:710
  41.3 2.5 %collective-permute-start.13 = (f32[8,128]{1,0:T(8,128)S(1)}, f32[8,128]{1,0:T(8,128)S(1)}, u32[]{:S(2)}, u32[]{:S(2)}) collective-permute-start(f32[8,128]{1,0:T(8,128)S(1)} %add.15), channel_id=1, source_target_pairs={{0,2},{1,3},{2,0},{3,1},{4,6},{5,7},{6,4},{7,5},{8,10},{9,11},{10,... | collective-permute-start | bytes 12296 | tf_op jit(solution)/shard_map/ppermute | solution.py:710
  43.8 2.5 %collective-permute-start.14 = (f32[8,128]{1,0:T(8,128)S(1)}, f32[8,128]{1,0:T(8,128)S(1)}, u32[]{:S(2)}, u32[]{:S(2)}) collective-permute-start(f32[8,128]{1,0:T(8,128)S(1)} %add.16), channel_id=1, source_target_pairs={{0,4},{1,5},{2,6},{3,7},{4,0},{5,1},{6,2},{7,3},{8,12},{9,13},{10,... | collective-permute-start | bytes 12296 | tf_op jit(solution)/shard_map/ppermute | solution.py:710
  46.2 3.4 %collective-permute-start.15 = (f32[8,128]{1,0:T(8,128)S(1)}, f32[8,128]{1,0:T(8,128)S(1)}, u32[]{:S(2)}, u32[]{:S(2)}) collective-permute-start(f32[8,128]{1,0:T(8,128)S(1)} %add.17), channel_id=1, source_target_pairs={{0,8},{1,9},{2,10},{3,11},{4,12},{5,13},{6,14},{7,15},{8,0},{9,1},... | collective-permute-start | bytes 12296 | tf_op jit(solution)/shard_map/ppermute | solution.py:710
  49.6 8.2 %collective-permute-start.16 = (f32[8,128]{1,0:T(8,128)S(1)}, f32[8,128]{1,0:T(8,128)S(1)}, u32[]{:S(2)}, u32[]{:S(2)}) collective-permute-start(f32[8,128]{1,0:T(8,128)S(1)} %add.18), channel_id=1, source_target_pairs={{0,16},{16,0},{1,17},{17,1},{2,18},{18,2},{3,19},{19,3},{4,20},{20... | collective-permute-start | bytes 12296 | tf_op jit(solution)/shard_map/ppermute | solution.py:710
  50.9 7.5 %collective-permute-start.11 = (f32[4,8,128]{2,1,0:T(8,128)S(1)}, f32[4,8,128]{2,1,0:T(8,128)S(1)}, u32[]{:S(2)}, u32[]{:S(2)}) collective-permute-start(f32[4,8,128]{2,1,0:T(8,128)S(1)} %get-tuple-element.66), channel_id=1, source_target_pairs={{0,16},{16,0},{1,17},{17,1},{2,18},{18,2},{3,19},{19,3},{4,20},{20... | collective-permute-start | bytes 49160 | tf_op jit(solution)/shard_map/ppermute | solution.py:693
  51.1 7.2 %collective-permute-start.9 = (f32[28,8,128]{2,1,0:T(8,128)S(1)}, f32[28,8,128]{2,1,0:T(8,128)S(1)}, u32[]{:S(2)}, u32[]{:S(2)}) collective-permute-start(f32[28,8,128]{2,1,0:T(8,128)S(1)} %get-tuple-element.64), channel_id=1, source_target_pairs={{0,1},{2,3},{4,5},{6,7},{8,9},{10,11},{12,13},{14,15},{1,0},{3,2},... | collective-permute-start | bytes 344072 | tf_op jit(solution)/shard_map/ppermute | solution.py:693
  55.3 7.3 %collective-permute-start.10 = (f32[28,8,128]{2,1,0:T(8,128)S(1)}, f32[28,8,128]{2,1,0:T(8,128)S(1)}, u32[]{:S(2)}, u32[]{:S(2)}) collective-permute-start(f32[28,8,128]{2,1,0:T(8,128)S(1)} %get-tuple-element.65), channel_id=1, source_target_pairs={{1,2},{3,4},{5,6},{7,8},{9,10},{11,12},{13,14},{2,1},{4,3},{6,5},{... | collective-permute-start | bytes 344072 | tf_op jit(solution)/shard_map/ppermute | solution.py:693
where the time goes:
time: 64.5 us; the launch traced here: 64.2 us
  starting transfers between devices  25.5 us (40%)
  waiting for transfers between devices  19.6 us (30%)
  Pallas kernels  16 us (25%)
  local copies, waits for them, and re-layouts  1.79 us (3%)
  between operations  0.74 us (1%)
    ppermute x12, starting transfers between devices, swap(): return lax.ppermute(x, axis, pairs + [(j, i) for i, j in pairs])  21.1 us
    pallas_call x5, Pallas kernels, call(): pl.pallas_call(kernel, out_shape=outs, in_specs=in_specs, out_specs=[pl.B...  16 us
    ppermute x12, waiting for transfers between devices, swap(): return lax.ppermute(x, axis, pairs + [(j, i) for i, j in pairs])  13.3 us
    ppermute x5, waiting for transfers between devices, summed_over(): x = x + lax.ppermute(x, axis, [(i, i ^ distance) for i in range(peers)])  6.37 us
    ppermute x5, starting transfers between devices, summed_over(): x = x + lax.ppermute(x, axis, [(i, i ^ distance) for i in range(peers)])  4.37 us
    unnamed x12, local copies, waits for them, and re-layouts  1.79 us
  transfers between devices with their start and end apart: 17, of which 11 were waited for; matrix products, arithmetic and copies ran while one was open for 1% of the time, Pallas kernels for 0%

commit v1 on v0

--- a/solution.py
+++ b/solution.py
@@ -16,6 +16,7 @@
 FACE = 0.3 * 0.5 * 0.5
 COUPLING = 0.5
 DRAG_STEP = 0.5
+TERRAIN_SLOT = 2
 
 
 def roll(v, shift):
@@ -112,6 +113,14 @@
     left = jnp.broadcast_to(left_words[which : which + 1], (8, LANES))
     value = jnp.where(pos < 4, own, roll(own, 4))
     return jnp.where(pos == 7, roll(left, 4), value)
+
+
+def strip_classes(edge_words_ref, pick):
+    pos = strip_pos()
+    own = spread(edge_words_ref, TERRAIN_SLOT)
+    left, right = [jnp.broadcast_to(v[TERRAIN_SLOT : TERRAIN_SLOT + 1], (8, LANES)).astype(jnp.int32) for v in pick(4)]
+    value = jnp.where(pos < 4, own, jnp.where(pos < 6, right, jnp.where(pos < 8, roll(left, 4), roll(own, 4))))
+    return value
 
 
 def face_walls():
@@ -215,8 +224,8 @@
     return out, s, u, v
 
 
-def stepped(c, drag):
-    q, _, _, _ = coupled(c)
+def dragged(q, drag):
+    q = list(q)
     for lead, _ in PHASES:
         s = inverse_root(q[lead])
         u, v = q[lead + 1] * s, q[lead + 2] * s
@@ -225,10 +234,21 @@
     return q
 
 
-def stepped_back(c, drag, a):
+def drag_terms(q, a):
+    total = None
+    for lead, _ in PHASES:
+        s = inverse_root(q(lead))
+        x, y = q(lead + 1), q(lead + 2)
+        u, v = x * s, y * s
+        term = jnp.sqrt(u * u + v * v + 1.0) * (a[lead + 1] * x + a[lead + 2] * y)
+        total = term if total is None else total + term
+    return -total
+
+
+def stepped_back(c, drag, a, want_terms):
     q, s0, gas_u, gas_v = coupled(c)
     a = list(a)
-    drag_terms = jnp.zeros((8, LANES), jnp.float32)
+    terms = jnp.zeros((8, LANES), jnp.float32)
     for lead, _ in PHASES:
         m, x, y = q[lead], q[lead + 1], q[lead + 2]
         s = s0 if lead == 0 else inverse_root(m)
@@ -237,15 +257,16 @@
         root = lax.rsqrt(energy + 1.0)
         w = (energy + 1.0) * root
         dot = a[lead + 1] * x + a[lead + 2] * y
-        drag_terms = drag_terms - w * dot
+        if want_terms:
+            terms = terms - w * dot
         k = drag * dot * root
         factor = 1.0 - drag * w
         ks = k * s
         a[lead + 1] = a[lead + 1] * factor - ks * u
         a[lead + 2] = a[lead + 2] * factor - ks * v
         a[lead] = a[lead] + k * energy * m * (s * s)
-    du = jnp.zeros_like(drag_terms)
-    dv = jnp.zeros_like(drag_terms)
+    du = jnp.zeros((8, LANES), jnp.float32)
+    dv = jnp.zeros((8, LANES), jnp.float32)
     for lead, _ in PHASES[1:]:
         rx, ry = COUPLING * (a[lead + 1] - a[1]), COUPLING * (a[lead + 2] - a[2])
         a[lead] = a[lead] + rx * gas_u + ry * gas_v
@@ -253,7 +274,7 @@
         a[lead + 1], a[lead + 2] = a[lead + 1] - rx, a[lead + 2] - ry
     a[1], a[2] = a[1] + du * s0, a[2] + dv * s0
     a[0] = a[0] - (gas_u * du + gas_v * dv) * c[0] * (s0 * s0)
-    return a, drag_terms
+    return a, terms
 
 
 def add_speed_terms(total, state, lead, du, dv):
@@ -305,6 +326,7 @@
     for g in range(4):
         fields = range(4 * g, min(4 * g + 4, FIELDS))
         out_c[g] = into_slots([roll(ghosts[f], 4 * (f % 4) - 4) for f in fields])
+    return ghosts
 
 
 def backward_fluxes(step, ext, words, low_words, a_ext, fvx, ux, fvy, vy, sdc, sdu, gl, gh, dvy, put):
@@ -378,20 +400,23 @@
     lax.fori_loop(0, 4, ghost, 0)
 
 
-def drag_row(drag_ref, r):
+def level_weight():
     levels = lax.broadcasted_iota(jnp.int32, (8, LANES), 0)
     weight = jnp.full((8, LANES), DRAG_STEP, jnp.float32)
     for k in range(3):
         weight = jnp.where((levels // 2**k) % 2 == 1, weight * 0.5 ** (2**k), weight)
-    return weight, weight * spread(drag_ref, r)
-
-
-def drag_table(terrain, coef, drag_ref):
-    classes = terrain[...]
-    drag = jnp.zeros((8, LANES), jnp.float32)
+    return weight
+
+
+def drag_table(classes, coef):
+    drag = jnp.zeros(classes.shape, jnp.float32)
     for k in range(NCLASS):
         drag = jnp.where(classes == k, coef[k], drag)
-    drag_ref[...] = drag
+    return drag
+
+
+def level_sum(v):
+    return jnp.sum(v, axis=0, keepdims=True)
 
 
 def row_bases():
@@ -420,9 +445,10 @@
             to_b[2 * f + j] = source[f, b_row + j]
 
 
-def pack_kernel(start, words, rows, edges, edge_words, to_a, to_b, to_c):
+def pack_kernel(start, words, terrain, rows, edges, edge_words, to_a, to_b, to_c):
     zero_edges(edges)
     edge_words[...] = jnp.zeros((8, LANES), jnp.int32)
+    slots = lax.broadcasted_iota(jnp.int32, (8, LANES), 0)
 
     def one_row(r, carry):
         values = [start[f, pl.ds(r, 8, stride=8), :] for f in range(FIELDS)]
@@ -430,14 +456,18 @@
             rows[f, r] = values[f]
         add_edges(edges, values, r)
         mine = strip_row() == r
-        edge_words[...] = jnp.where(mine, roll(words[pl.ds(r, 8, stride=8), :], 16 * r + 4), edge_words[...])
+        row_words = jnp.where(slots == TERRAIN_SLOT, spread(terrain, r), words[pl.ds(r, 8, stride=8), :])
+        edge_words[...] = jnp.where(mine, roll(row_words, 16 * r + 4), edge_words[...])
         return carry
 
     lax.fori_loop(0, ROWS, one_row, 0)
     put_edge_rows(rows, 0, to_a, to_b)
-    top = words[pl.ds(ROWS - 1, 8, stride=8), :].astype(jnp.float32)
-    to_a[2 * FIELDS] = top
-    to_b[2 * FIELDS] = top
+    top = words[pl.ds(ROWS - 1, 8, stride=8), :]
+    is_even = row_bases()
+    a_row = jnp.where(is_even, ROWS - 2, 0)
+    for target, row in ((to_a, a_row), (to_b, ROWS - 2 - a_row)):
+        mixed = jnp.where(slots == 0, spread(terrain, row), jnp.where(slots == 1, spread(terrain, row + 1), top))
+        target[2 * FIELDS] = mixed.astype(jnp.float32)
     edge_payload(edges, to_c)
     to_c[4] = edge_words[...].astype(jnp.float32)
 
@@ -453,9 +483,9 @@
         rows, edges, edge_words, words, terrain, coef, from_a, from_b, from_c = refs[:9]
         from_d = refs[9] if has_odd else None
         outs = refs[9 + has_odd :]
-        (ext, strip, carried_ref, fvx, ux, fvy, vy, sfv, su, drag_ref, low_ref, left_ref) = outs[:12]
-        middle, middle_edges, to_a, to_b, to_c = outs[12:17]
-        (sdx,) = outs[17:]
+        (ext, strip, carried_ref, fvx, ux, fvy, vy, sfv, su, drag_ref, class_ref, low_ref, left_ref) = outs[:13]
+        middle, before, before_edges, to_a, to_b, to_c = outs[13:19]
+        (sdx,) = outs[19:]
         pick = side_payloads(from_c, from_d)
 
         def copy_row(r, carry):
@@ -469,25 +499,35 @@
         low_words, left_words = neighbour_words(from_a, from_b, pick)
         low_ref[...] = low_words
         left_ref[...] = left_words
-        drag_table(terrain, coef, drag_ref)
+        is_even = row_bases()
+        a_row = jnp.where(is_even, ROWS + 2, 0)
+        class_ref[pl.ds(2, ROWS), :] = terrain[...]
+        for source, row in ((from_a, a_row), (from_b, ROWS + 2 - a_row)):
+            for j in range(2):
+                class_ref[pl.ds(row + j, 1), :] = source[2 * FIELDS, pl.ds(j, 1), :].astype(jnp.int32)
+        class_ref[pl.ds(12, 4), :] = strip_classes(edge_words, pick)[:4]
+        drag_ref[...] = drag_table(class_ref[...], coef)
         forward_strip(0, strip, edge_words, left_words, sfv, su, sdx)
         forward_rows(0, ext, words, low_words, fvy, vy)
-        zero_edges(middle_edges)
+        zero_edges(before_edges)
+        weight = level_weight()
 
         def one_row(r, carry):
             c = carried_row(0, r, ext, words, sdx, fvx, ux, fvy, vy)
             for f in range(FIELDS):
                 carried_ref[f, r] = c[f]
-            _, drag = drag_row(drag_ref, r)
-            q = stepped(c, drag)
+            q = coupled(c)[0]
+            for f in range(FIELDS):
+                before[f, r] = q[f]
+            add_edges(before_edges, q, r)
+            q = dragged(q, weight * spread(drag_ref, r + 2))
             for f in range(FIELDS):
                 middle[f, r] = q[f]
-            add_edges(middle_edges, q, r)
             return carry
 
         lax.fori_loop(0, ROWS, one_row, 0)
-        put_edge_rows(middle, 0, to_a, to_b)
-        edge_payload(middle_edges, to_c)
+        put_edge_rows(before, 0, to_a, to_b)
+        edge_payload(before_edges, to_c)
 
     return kernel
 
@@ -504,52 +544,87 @@
 
 def second_kernel(has_odd):
     def kernel(*refs):
-        middle, middle_edges, edge_words, words, drag_ref, low_ref, left_ref, adjoint = refs[:8]
-        from_a, from_b, from_c = refs[8:11]
-        from_d = refs[11] if has_odd else None
-        outs = refs[11 + has_odd :]
-        part, to_a, to_b, to_c, grad_cells = outs[:5]
-        (ext, strip, fvx, ux, fvy, vy, sfv, su, sdx, a_ext, edges_a, sdc, sdu, gl, gh, dvy) = outs[5:]
+        middle, before, before_edges, edge_words, words, drag_ref, class_ref, low_ref, left_ref, adjoint = refs[:10]
+        from_a, from_b, from_c = refs[10:13]
+        from_d = refs[13] if has_odd else None
+        outs = refs[13 + has_odd :]
+        part, to_a, to_b, to_c = outs[:4]
+        (ext, strip, fvx, ux, fvy, vy, sfv, su, sdx, a_ext, edges_a, sdc, sdu, gl, gh, dvy) = outs[4:20]
+        before_ext, before_strip, cells = outs[20:]
         pick = side_payloads(from_c, from_d)
         low_words, left_words = low_ref[...], left_ref[...]
+        weight = level_weight()
 
         def copy_row(r, carry):
             for f in range(FIELDS):
                 ext[f, r + 2] = middle[f, r]
+                before_ext[f, r + 2] = before[f, r]
             return carry
 
         lax.fori_loop(0, ROWS, copy_row, 0)
-        fill_ghost_rows(ext, from_a, from_b)
-        build_strip(middle_edges, pick, strip)
+        fill_ghost_rows(before_ext, from_a, from_b)
+
+        def ghost_row(t, carry):
+            row = jnp.where(t < 2, t, t + 8)
+            q = dragged([before_ext[f, row] for f in range(FIELDS)], weight * spread(drag_ref, row))
+            for f in range(FIELDS):
+                ext[f, row] = q[f]
+            return carry
+
+        lax.fori_loop(0, 4, ghost_row, 0)
+        build_strip(before_edges, pick, before_strip)
+        q = dragged([before_strip[f] for f in range(FIELDS)], weight * spread(drag_ref, 12))
+        for f in range(FIELDS):
+            strip[f] = q[f]
         forward_strip(1, strip, edge_words, left_words, sfv, su, sdx)
         forward_rows(1, ext, words, low_words, fvy, vy)
         zero_edges(edges_a)
         for f in range(FIELDS):
             a_ext[f, 0] = jnp.zeros((8, LANES), jnp.float32)
             a_ext[f, ROWS + 1] = jnp.zeros((8, LANES), jnp.float32)
+        cells[...] = jnp.zeros((16, LANES), jnp.float32)
 
         def one_row(r, carry):
             c = carried_row(1, r, ext, words, sdx, fvx, ux, fvy, vy)
-            weight, drag = drag_row(drag_ref, r)
             a = [adjoint[f, pl.ds(r, 8, stride=8), :] for f in range(FIELDS)]
-            a, terms = stepped_back(c, drag, a)
-            grad_cells[pl.ds(r, 1), :] = jnp.sum(weight * terms, axis=0, keepdims=True)
+            a, terms = stepped_back(c, weight * spread(drag_ref, r + 2), a, True)
+            cells[pl.ds(r + 2, 1), :] = level_sum(weight * terms)
             for f in range(FIELDS):
                 a_ext[f, r + 1] = a[f]
             add_edges(edges_a, a, r)
             return carry
 
         lax.fori_loop(0, ROWS, one_row, 0)
-        backward_strip(1, strip, edges_a, edge_words, left_words, sfv, su, sdc, sdu, to_c)
+        ghosts = backward_strip(1, strip, edges_a, edge_words, left_words, sfv, su, sdc, sdu, to_c)
+        pos = strip_pos()
+        terms = jnp.where((pos >= 4) & (pos < 8), drag_terms(lambda f: before_strip[f], ghosts), 0.0)
+        cells[pl.ds(12, 1), :] = level_sum(weight * terms)
 
         def put(row, values):
             for f in range(FIELDS):
                 part[f, row + 2] = values[f]
+            terms = drag_terms(lambda f: before_ext[f, row + 2], values)
+            at = pl.ds(row + 2, 1)
+            cells[at, :] = cells[at, :] + level_sum(weight * terms)
 
         backward_fluxes(1, ext, words, low_words, a_ext, fvx, ux, fvy, vy, sdc, sdu, gl, gh, dvy, put)
         ghost_rows_out(part, to_a, to_b)
+        to_c[4] = binned(class_ref[...], cells[...])
 
     return kernel
+
+
+def binned(classes, cells):
+    lanes = lane_ids()
+    slots = lax.broadcasted_iota(jnp.int32, (8, LANES), 0)
+    total = jnp.zeros((8, LANES), jnp.float32)
+    for first in range(0, NCLASS, 8):
+        block = jnp.zeros((8, LANES), jnp.float32)
+        for k in range(first, min(first + 8, NCLASS)):
+            block = jnp.where(slots == k - first, level_sum(jnp.where(classes == k, cells, 0.0)), block)
+        block = jnp.sum(block, axis=1, keepdims=True)
+        total = jnp.where(lanes == first + slots, block, total)
+    return jnp.broadcast_to(level_sum(total), (8, LANES))
 
 
 def collect(part, from_a, from_b, pick, incoming):
@@ -573,13 +648,13 @@
 
 def third_kernel(has_odd):
     def kernel(*refs):
-        (part_in, grad_cells, terrain, ext, strip, carried_ref, fvx, ux, fvy, vy, sfv, su) = refs[:12]
-        drag_ref, low_ref, left_ref, edge_words, words = refs[12:17]
-        from_a, from_b, from_c = refs[17:20]
-        from_d = refs[20] if has_odd else None
-        outs = refs[20 + has_odd :]
-        part, to_a, to_b, to_c, grads = outs[:5]
-        (incoming, a_ext, edges_a, sdc, sdu, gl, gh, dvy, cells) = outs[5:]
+        (part_in, grads, ext, strip, carried_ref, fvx, ux, fvy, vy, sfv, su) = refs[:11]
+        drag_ref, low_ref, left_ref, edge_words, words = refs[11:16]
+        from_a, from_b, from_c = refs[16:19]
+        from_d = refs[19] if has_odd else None
+        outs = refs[19 + has_odd :]
+        part, to_a, to_b, to_c = outs[:4]
+        (incoming, a_ext, edges_a, sdc, sdu, gl, gh, dvy) = outs[4:]
         pick = side_payloads(from_c, from_d)
         low_words, left_words = low_ref[...], left_ref[...]
 
@@ -595,31 +670,22 @@
             a_ext[f, 0] = jnp.zeros((8, LANES), jnp.float32)
             a_ext[f, ROWS + 1] = jnp.zeros((8, LANES), jnp.float32)
         edges = edge_lanes()
+        weight = level_weight()
 
         def one_row(r, carry):
             c = [carried_ref[f, r] for f in range(FIELDS)]
-            weight, drag = drag_row(drag_ref, r)
             a = [
                 part[f, r + 2] + jnp.where(edges, roll(incoming[f], 124 - 16 * r), 0.0)
                 for f in range(FIELDS)
             ]
-            a, terms = stepped_back(c, drag, a)
-            cells[pl.ds(r, 1), :] = jnp.sum(weight * terms, axis=0, keepdims=True)
+            a, _ = stepped_back(c, weight * spread(drag_ref, r + 2), a, False)
             for f in range(FIELDS):
                 a_ext[f, r + 1] = a[f]
             add_edges(edges_a, a, r)
             return carry
 
         lax.fori_loop(0, ROWS, one_row, 0)
-        total = cells[...] + grad_cells[...]
-        classes = terrain[...]
-        lanes = lane_ids()
-        binned = jnp.zeros((8, LANES), jnp.float32)
-        for k in range(NCLASS):
-            one = jnp.sum(jnp.where(classes == k, total, 0.0), axis=0, keepdims=True)
-            one = jnp.sum(one, axis=1, keepdims=True)
-            binned = jnp.where(lanes == k, one, binned)
-        grads[...] = binned
+        to_a[2 * FIELDS] = grads[...]
         backward_strip(0, strip, edges_a, edge_words, left_words, sfv, su, sdc, sdu, to_c)
 
         def put(row, values):
@@ -703,17 +769,13 @@
     return (from_a, from_b, from_c) + (() if from_d is None else (from_d,))
 
 
-def summed_over(x, axis):
-    peers = lax.axis_size(axis)
-    distance = 1
-    while distance < peers:
-        x = x + lax.ppermute(x, axis, [(i, i ^ distance) for i in range(peers)])
-        distance *= 2
-    return x
+def add_partner(x, axis, distance):
+    return x + lax.ppermute(x, axis, [(i, i ^ distance) for i in range(lax.axis_size(axis))])
 
 
 def body(start_state, final_adjoint, face_words, terrain, drag_coef):
-    has_odd = lax.axis_size("gx") > 2
+    nx, ny = lax.axis_size("gx"), lax.axis_size("gy")
+    has_odd = nx > 2
     start = start_state.reshape(FIELDS, LEV * ROWS, LANES)
     adjoint = final_adjoint.reshape(FIELDS, LEV * ROWS, LANES)
     words = face_words.reshape(8 * ROWS, LANES)
@@ -723,50 +785,61 @@
         pack_kernel,
         [tiles(14, 8), tiles(14), tiles(dtype=ints), tiles(29), tiles(29), tiles(5)],
         [],
-        [start, words],
+        [start, words, terrain],
     )
     got = exchange(to_a, to_b, to_c)
     faces = [tiles(14, 8), tiles(4, 8), tiles(14, 9), tiles(4, 9), tiles(14), tiles(4)]
     res = call(
         first_kernel(has_odd),
-        [tiles(14, 12), tiles(14), tiles(14, 8), *faces, tiles(), tiles(dtype=ints), tiles(dtype=ints)]
-        + [tiles(14, 8), tiles(14), tiles(28), tiles(28), tiles(4)],
+        [tiles(14, 12), tiles(14), tiles(14, 8), *faces, shaped(16, LANES), shaped(16, LANES, dtype=ints)]
+        + [tiles(dtype=ints), tiles(dtype=ints), tiles(14, 8), tiles(14, 8), tiles(14), tiles(28), tiles(28), tiles(4)],
         [scratch(14)],
         [rows, edges, edge_words, words, terrain, drag_coef, *got],
         smem=(5,),
     )
     ext, strip, carried_ref = res[:3]
     saved = res[3:9]
-    drag_ref, low_ref, left_ref = res[9:12]
-    middle, middle_edges = res[12:14]
-    got = exchange(*res[14:17])
+    drag_ref, class_ref, low_ref, left_ref = res[9:13]
+    middle, before, before_edges = res[13:16]
+    got = exchange(*res[16:19])
     back = [scratch(14, 10), scratch(14), scratch(14), scratch(4), scratch(14, 15), scratch(14, 15), scratch(4, 15)]
-    part, to_a, to_b, to_c, grad_cells = call(
+    part, to_a, to_b, to_c = call(
         second_kernel(has_odd),
-        [tiles(14, 12), tiles(28), tiles(28), tiles(4), tiles()],
+        [tiles(14, 12), tiles(28), tiles(28), tiles(5)],
         [scratch(14, 12), scratch(14), scratch(14, 8), scratch(4, 8), scratch(14, 9), scratch(4, 9)]
-        + [scratch(14), scratch(4), scratch(14), *back],
-        [middle, middle_edges, edge_words, words, drag_ref, low_ref, left_ref, adjoint, *got],
+        + [scratch(14), scratch(4), scratch(14), *back]
+        + [scratch(14, 12), scratch(14), pltpu.VMEM((16, LANES), jnp.float32)],
+        [middle, before, before_edges, edge_words, words, drag_ref, class_ref, low_ref, left_ref, adjoint, *got],
     )
     got = exchange(to_a, to_b, to_c)
-    part, to_a, to_b, to_c, grads = call(
+    grads = to_c[4] + got[2][4]
+    distance = 2
+    while distance < nx:
+        grads = add_partner(grads, "gx", distance)
+        distance *= 2
+    if ny > 2:
+        grads = add_partner(grads, "gy", 2)
+    part, to_a, to_b, to_c = call(
         third_kernel(has_odd),
-        [tiles(14, 12), tiles(28), tiles(28), tiles(4), tiles()],
-        [scratch(14), *back, scratch()],
-        [part, grad_cells, terrain, ext, strip, carried_ref, *saved]
+        [tiles(14, 12), tiles(29), tiles(28), tiles(4)],
+        [scratch(14), *back],
+        [part, grads, ext, strip, carried_ref, *saved]
         + [drag_ref, low_ref, left_ref, edge_words, words, *got],
     )
     got = exchange(to_a, to_b, to_c)
+    grads = grads + got[0][2 * FIELDS]
+    distance = 4
+    while distance < ny:
+        grads = add_partner(grads, "gy", distance)
+        distance *= 2
     (out,) = call(
         last_kernel(has_odd),
         [shaped(FIELDS, LEV * ROWS, LANES)],
         [scratch(14, 12), scratch(14)],
         [part, *got],
     )
-    total_cells = terrain.size * lax.axis_size("gx") * lax.axis_size("gy") * LEV
-    grad_scale = math.sqrt(NCLASS / total_cells)
-    summed = summed_over(summed_over(grads, "gy"), "gx")[0, :NCLASS]
-    return (out.reshape(start_state.shape), summed * grad_scale)
+    grad_scale = math.sqrt(NCLASS / (terrain.size * nx * ny * LEV))
+    return (out.reshape(start_state.shape), grads[0, :NCLASS] * grad_scale)
 
 
 def solution(mesh):

time: 64.5 us -> 56.6 us (0.88)
  the two profiles are of different devices: /device:TPU:9 before, /device:TPU:0 now
where the time goes in v1:
time: 56.6 us; the launch traced here: 56.3 us
  starting transfers between devices  26.9 us (48%)
  Pallas kernels  16.4 us (29%)
  waiting for transfers between devices  9.22 us (16%)
  local copies, waits for them, and re-layouts  2.47 us (4%)
  between operations  0.76 us (1%)
    pallas_call x5, Pallas kernels, call(): pl.pallas_call(kernel, out_shape=outs, in_specs=in_specs, out_specs=[pl.B...  16.4 us
    ppermute x12, starting transfers between devices, swap(): return lax.ppermute(x, axis, pairs + [(j, i) for i, j in pairs])  14.9 us
    ppermute x3, starting transfers between devices, add_partner(): lax.ppermute(x, axis, [(i, i ^ distance) for i in range(lax.axis_size(axi...  12 us
    ppermute x3, waiting for transfers between devices, add_partner(): lax.ppermute(x, axis, [(i, i ^ distance) for i in range(lax.axis_size(axi...  5.46 us
    ppermute x12, waiting for transfers between devices, swap(): return lax.ppermute(x, axis, pairs + [(j, i) for i, j in pairs])  3.76 us
    unnamed x12, local copies, waits for them, and re-layouts  2.47 us
  transfers between devices with their start and end apart: 15, of which 5 were waited for; matrix products, arithmetic and copies ran while one was open for 0% of the time, Pallas kernels for 3%

profile of v1, /device:TPU:0, one launch (start us, length us, event | category | flops | bytes accessed | tf_op | source)
XLA Modules:
  0.0 56.3 jit_solution(540808726613158201)
XLA Ops:
  0.6 0.7 %copy-done = s32[2,2,2,8,128]{4,3,2,1,0:T(8,128)S(1)} copy-done((s32[2,2,2,8,128]{4,3,2,1,0:T(8,128)S(1)}, s32[2,2,2,8,128]{4,3,2,1,0:T(8,128)}, u32[]{:S(2)}) %copy-start) | copy-done | bytes 32792
  1.4 1.0 %copy-done.2 = f32[14,8,8,128]{3,2,1,0:T(8,128)S(1)} copy-done((f32[14,8,8,128]{3,2,1,0:T(8,128)S(1)}, f32[14,8,8,128]{3,2,1,0:T(8,128)}, u32[]{:S(2)}) %copy-start.2) | copy-done | bytes 458776
  2.4 0.7 %copy-done.4 = s32[8,128]{1,0:T(8,128)S(1)} copy-done((s32[8,128]{1,0:T(8,128)S(1)}, s32[8,128]{1,0:T(8,128)}, u32[]{:S(2)}) %copy-start.4) | copy-done | bytes 4120
  3.1 0.8 %shard_map.68 = (f32[14,8,8,128]{3,2,1,0:T(8,128)S(1)}, f32[14,8,128]{2,1,0:T(8,128)S(1)}, s32[8,128]{1,0:T(8,128)S(1)}, f32[29,8,128]{2,1,0:T(8,128)S(1)}, f32[...) custom-call(f32[14,64,128]{2,1,0:T(8,128)S(1)} %bitcast.16, s32[64,128]{1,0:T(8,128)S(1)} %bitcast.12, s32[8,128]{1,0:T(8,128)S(1)} %copy-done.4), custom_call_target="tpu_custom_call" | custom-call | tf_op jit(solution)/shard_map/pallas_call | solution.py:744
  3.9 0.0 copy-start.3
  3.9 0.5 collective-permute-start
  4.4 0.7 %collective-permute-start.1 = (f32[29,8,128]{2,1,0:T(8,128)S(1)}, f32[29,8,128]{2,1,0:T(8,128)S(1)}, u32[]{:S(2)}, u32[]{:S(2)}) collective-permute-start(f32[29,8,128]{2,1,0:T(8,128)S(1)} %get-tuple-element.39), channel_id=1, source_target_pairs={{1,2},{3,4},{5,6},{7,8},{9,10},{11,12},{13,14},{2,1},{4,3},{6,5},{... | collective-permute-start | bytes 356360 | tf_op jit(solution)/shard_map/ppermute | solution.py:759
  5.1 2.7 %collective-permute-start.2 = (f32[5,8,128]{2,1,0:T(8,128)S(1)}, f32[5,8,128]{2,1,0:T(8,128)S(1)}, u32[]{:S(2)}, u32[]{:S(2)}) collective-permute-start(f32[5,8,128]{2,1,0:T(8,128)S(1)} %get-tuple-element.40), channel_id=1, source_target_pairs={{0,16},{16,0},{1,17},{17,1},{2,18},{18,2},{3,19},{19,3},{4,20},{20... | collective-permute-start | bytes 61448 | tf_op jit(solution)/shard_map/ppermute | solution.py:759
  7.8 1.8 %collective-permute-done.2.refs_8_ = f32[5,8,128]{2,1,0:T(8,128)S(1)} collective-permute-done((f32[5,8,128]{2,1,0:T(8,128)S(1)}, f32[5,8,128]{2,1,0:T(8,128)S(1)}, u32[]{:S(2)}, u32[]{:S(2)}) %collective-permute-start.2) | collective-permute-done | bytes 20512 | tf_op jit(solution)/shard_map/ppermute | solution.py:759
  9.6 3.6 %shard_map.69 = (f32[14,12,8,128]{3,2,1,0:T(8,128)S(1)}, f32[14,8,128]{2,1,0:T(8,128)S(1)}, f32[14,8,8,128]{3,2,1,0:T(8,128)S(1)}, f32[14,8,8,128]{3,2,1,0:T(8,1...) custom-call(f32[14,8,8,128]{3,2,1,0:T(8,128)S(1)} %get-tuple-element, ...), custom_call_target="tpu_custom_call" | custom-call | tf_op jit(solution)/shard_map/pallas_call | solution.py:744
  13.2 2.3 %collective-permute-start.3 = (f32[28,8,128]{2,1,0:T(8,128)S(1)}, f32[28,8,128]{2,1,0:T(8,128)S(1)}, u32[]{:S(2)}, u32[]{:S(2)}) collective-permute-start(f32[28,8,128]{2,1,0:T(8,128)S(1)} %get-tuple-element.48), channel_id=1, source_target_pairs={{0,1},{2,3},{4,5},{6,7},{8,9},{10,11},{12,13},{14,15},{1,0},{3,2},... | collective-permute-start | bytes 344072 | tf_op jit(solution)/shard_map/ppermute | solution.py:759
  15.4 0.7 %collective-permute-start.4 = (f32[28,8,128]{2,1,0:T(8,128)S(1)}, f32[28,8,128]{2,1,0:T(8,128)S(1)}, u32[]{:S(2)}, u32[]{:S(2)}) collective-permute-start(f32[28,8,128]{2,1,0:T(8,128)S(1)} %get-tuple-element.49), channel_id=1, source_target_pairs={{1,2},{3,4},{5,6},{7,8},{9,10},{11,12},{13,14},{2,1},{4,3},{6,5},{... | collective-permute-start | bytes 344072 | tf_op jit(solution)/shard_map/ppermute | solution.py:759
  16.1 1.8 %collective-permute-start.5 = (f32[4,8,128]{2,1,0:T(8,128)S(1)}, f32[4,8,128]{2,1,0:T(8,128)S(1)}, u32[]{:S(2)}, u32[]{:S(2)}) collective-permute-start(f32[4,8,128]{2,1,0:T(8,128)S(1)} %get-tuple-element.50), channel_id=1, source_target_pairs={{0,16},{16,0},{1,17},{17,1},{2,18},{18,2},{3,19},{19,3},{4,20},{20... | collective-permute-start | bytes 49160 | tf_op jit(solution)/shard_map/ppermute | solution.py:759
  17.9 2.0 %collective-permute-done.5.refs_12_ = f32[4,8,128]{2,1,0:T(8,128)S(1)} collective-permute-done((f32[4,8,128]{2,1,0:T(8,128)S(1)}, f32[4,8,128]{2,1,0:T(8,128)S(1)}, u32[]{:S(2)}, u32[]{:S(2)}) %collective-permute-start.5) | collective-permute-done | bytes 16416 | tf_op jit(solution)/shard_map/ppermute | solution.py:759
  19.9 0.0 collective-permute-done.3.refs_10_
  19.9 0.0 collective-permute-done.4.refs_11_
  19.9 6.1 %shard_map.70 = (f32[14,12,8,128]{3,2,1,0:T(8,128)S(1)}, f32[28,8,128]{2,1,0:T(8,128)S(1)}, f32[28,8,128]{2,1,0:T(8,128)S(1)}, f32[5,8,128]{2,1,0:T(8,128)S(1)}) custom-call(f32[14,8,8,128]{3,2,1,0:T(8,128)S(1)} %get-tuple-element.41.refs_0_, f32[14,8,8,128]{3,2,1,0:T(8,128)S(1)} %get-tuple-element.42.refs_1_, f32[14,8,128]{2,1,0:T(8,128)S(1)} %get-tuple-element.43.refs_2_, ...), custom_call_target="tpu_custom_call" | custom-call | tf_op jit(solution)/shard_map/pallas_call | solution.py:744
  26.0 1.8 %collective-permute-start.6 = (f32[5,8,128]{2,1,0:T(8,128)S(1)}, f32[5,8,128]{2,1,0:T(8,128)S(1)}, u32[]{:S(2)}, u32[]{:S(2)}) collective-permute-start(f32[5,8,128]{2,1,0:T(8,128)S(1)} %get-tuple-element.52), channel_id=1, source_target_pairs={{0,16},{16,0},{1,17},{17,1},{2,18},{18,2},{3,19},{19,3},{4,20},{20... | collective-permute-start | bytes 61448 | tf_op jit(solution)/shard_map/ppermute | solution.py:759
  27.8 2.3 %collective-permute-start.8 = (f32[28,8,128]{2,1,0:T(8,128)S(1)}, f32[28,8,128]{2,1,0:T(8,128)S(1)}, u32[]{:S(2)}, u32[]{:S(2)}) collective-permute-start(f32[28,8,128]{2,1,0:T(8,128)S(1)} %get-tuple-element.62), channel_id=1, source_target_pairs={{0,1},{2,3},{4,5},{6,7},{8,9},{10,11},{12,13},{14,15},{1,0},{3,2},... | collective-permute-start | bytes 344072 | tf_op jit(solution)/shard_map/ppermute | solution.py:759
  30.1 0.7 %collective-permute-start.9 = (f32[28,8,128]{2,1,0:T(8,128)S(1)}, f32[28,8,128]{2,1,0:T(8,128)S(1)}, u32[]{:S(2)}, u32[]{:S(2)}) collective-permute-start(f32[28,8,128]{2,1,0:T(8,128)S(1)} %get-tuple-element.63), channel_id=1, source_target_pairs={{1,2},{3,4},{5,6},{7,8},{9,10},{11,12},{13,14},{2,1},{4,3},{6,5},{... | collective-permute-start | bytes 344072 | tf_op jit(solution)/shard_map/ppermute | solution.py:759
  30.8 4.5 %collective-permute-start.7 = (f32[8,128]{1,0:T(8,128)S(1)}, f32[8,128]{1,0:T(8,128)S(1)}, u32[]{:S(2)}, u32[]{:S(2)}) collective-permute-start(f32[8,128]{1,0:T(8,128)S(1)} %fusion.1), channel_id=1, source_target_pairs={{0,2},{1,3},{2,0},{3,1},{4,6},{5,7},{6,4},{7,5},{8,10},{9,11},{10,... | collective-permute-start | bytes 12296 | tf_op jit(solution)/shard_map/ppermute | solution.py:773
  35.3 2.4 %collective-permute-done.7 = f32[8,128]{1,0:T(8,128)S(1)} collective-permute-done((f32[8,128]{1,0:T(8,128)S(1)}, f32[8,128]{1,0:T(8,128)S(1)}, u32[]{:S(2)}, u32[]{:S(2)}) %collective-permute-start.7) | collective-permute-done | bytes 4128 | tf_op jit(solution)/shard_map/ppermute | solution.py:773
  37.8 4.3 %shard_map.71 = (f32[14,12,8,128]{3,2,1,0:T(8,128)S(1)}, f32[29,8,128]{2,1,0:T(8,128)S(1)}, f32[28,8,128]{2,1,0:T(8,128)S(1)}, f32[4,8,128]{2,1,0:T(8,128)S(1)}) custom-call(f32[14,12,8,128]{3,2,1,0:T(8,128)S(1)} %get-tuple-element.51.refs_0_, f32[8,128]{1,0:T(8,128)S(1)} %add.20.refs_1_, f32[14,12,8,128]{3,2,1,0:T(8,128)S(1)} %get-tuple-element.53.refs_2_, ...), custom_call_target="tpu_custom_call" | custom-call | tf_op jit(solution)/shard_map/pallas_call | solution.py:744
  42.1 0.2 collective-permute-start.10
  42.2 0.6 %collective-permute-start.12 = (f32[4,8,128]{2,1,0:T(8,128)S(1)}, f32[4,8,128]{2,1,0:T(8,128)S(1)}, u32[]{:S(2)}, u32[]{:S(2)}) collective-permute-start(f32[4,8,128]{2,1,0:T(8,128)S(1)} %get-tuple-element.67), channel_id=1, source_target_pairs={{0,16},{16,0},{1,17},{17,1},{2,18},{18,2},{3,19},{19,3},{4,20},{20... | collective-permute-start | bytes 49160 | tf_op jit(solution)/shard_map/ppermute | solution.py:759
  42.9 0.7 %collective-permute-start.11 = (f32[28,8,128]{2,1,0:T(8,128)S(1)}, f32[28,8,128]{2,1,0:T(8,128)S(1)}, u32[]{:S(2)}, u32[]{:S(2)}) collective-permute-start(f32[28,8,128]{2,1,0:T(8,128)S(1)} %get-tuple-element.66), channel_id=1, source_target_pairs={{1,2},{3,4},{5,6},{7,8},{9,10},{11,12},{13,14},{2,1},{4,3},{6,5},{... | collective-permute-start | bytes 344072 | tf_op jit(solution)/shard_map/ppermute | solution.py:759
  43.6 5.0 %collective-permute-start.13 = (f32[8,128]{1,0:T(8,128)S(1)}, f32[8,128]{1,0:T(8,128)S(1)}, u32[]{:S(2)}, u32[]{:S(2)}) collective-permute-start(f32[8,128]{1,0:T(8,128)S(1)} %fusion), channel_id=1, source_target_pairs={{0,4},{1,5},{2,6},{3,7},{4,0},{5,1},{6,2},{7,3},{8,12},{9,13},{10,... | collective-permute-start | bytes 12296 | tf_op jit(solution)/shard_map/ppermute | solution.py:773
  48.5 2.7 %collective-permute-done.13 = f32[8,128]{1,0:T(8,128)S(1)} collective-permute-done((f32[8,128]{1,0:T(8,128)S(1)}, f32[8,128]{1,0:T(8,128)S(1)}, u32[]{:S(2)}, u32[]{:S(2)}) %collective-permute-start.13) | collective-permute-done | bytes 4128 | tf_op jit(solution)/shard_map/ppermute | solution.py:773
  51.3 2.6 %collective-permute-start.14 = (f32[8,128]{1,0:T(8,128)S(1)}, f32[8,128]{1,0:T(8,128)S(1)}, u32[]{:S(2)}, u32[]{:S(2)}) collective-permute-start(f32[8,128]{1,0:T(8,128)S(1)} %add.22), channel_id=1, source_target_pairs={{0,8},{1,9},{2,10},{3,11},{4,12},{5,13},{6,14},{7,15},{8,0},{9,1},... | collective-permute-start | bytes 12296 | tf_op jit(solution)/shard_map/ppermute | solution.py:773
  53.9 1.6 %shard_map.72 = f32[14,64,128]{2,1,0:T(8,128)} custom-call(f32[14,12,8,128]{3,2,1,0:T(8,128)S(1)} %get-tuple-element.64.refs_0_, f32[29,8,128]{2,1,0:T(8,128)S(1)} %collective-permute-done.10.refs_1_, f32[28,8,128]{2,1,0:T(8,128)S(1)} %collective-permute-done.11.refs_2_, f32[4,8,128]{2,1,0:T(8,128)S(1)} %collective-permute-done.12.refs_3_), custom_call_target="tpu_custom_call" | custom-call | tf_op jit(solution)/shard_map/pallas_call | solution.py:744
  55.5 0.3 collective-permute-done.14
  55.8 0.5 multiply_bitcast_fusion
  (21 shorter events, 0.1 us)
Async XLA Ops:
  0.6 0.8 %copy-start = (s32[2,2,2,8,128]{4,3,2,1,0:T(8,128)S(1)}, s32[2,2,2,8,128]{4,3,2,1,0:T(8,128)}, u32[]{:S(2)}) copy-start(s32[2,2,2,8,128]{4,3,2,1,0:T(8,128)} %param.7) | copy-start | bytes 98308
  1.4 1.0 %copy-start.2 = (f32[14,8,8,128]{3,2,1,0:T(8,128)S(1)}, f32[14,8,8,128]{3,2,1,0:T(8,128)}, u32[]{:S(2)}) copy-start(f32[14,8,8,128]{3,2,1,0:T(8,128)} %param.5) | copy-start | bytes 1376260
  2.4 0.7 %copy-start.4 = (s32[8,128]{1,0:T(8,128)S(1)}, s32[8,128]{1,0:T(8,128)}, u32[]{:S(2)}) copy-start(s32[8,128]{1,0:T(8,128)} %refs_4_.1) | copy-start | bytes 12292
  3.1 6.5 %copy-start.1 = (s32[2,2,2,8,128]{4,3,2,1,0:T(8,128)S(1)}, s32[2,2,2,8,128]{4,3,2,1,0:T(8,128)}, u32[]{:S(2)}) copy-start(s32[2,2,2,8,128]{4,3,2,1,0:T(8,128)} %param.7) | copy-start | bytes 98308
  3.1 6.5 %copy-start.5 = (f32[24]{0:T(128)S(1)}, f32[24]{0:T(128)}, u32[]{:S(2)}) copy-start(f32[24]{0:T(128)} %refs_5_.1) | copy-start | bytes 292
  3.9 16.0 %copy-start.3 = (f32[14,8,8,128]{3,2,1,0:T(8,128)S(1)}, f32[14,8,8,128]{3,2,1,0:T(8,128)}, u32[]{:S(2)}) copy-start(f32[14,8,8,128]{3,2,1,0:T(8,128)} %param.6) | copy-start | bytes 1376260
  3.9 5.7 %collective-permute-start = (f32[29,8,128]{2,1,0:T(8,128)S(1)}, f32[29,8,128]{2,1,0:T(8,128)S(1)}, u32[]{:S(2)}, u32[]{:S(2)}) collective-permute-start(f32[29,8,128]{2,1,0:T(8,128)S(1)} %get-tuple-element.38), channel_id=1, source_target_pairs={{0,1},{2,3},{4,5},{6,7},{8,9},{10,11},{12,13},{14,15},{1,0},{3,2},... | collective-permute-start | bytes 356360 | tf_op jit(solution)/shard_map/ppermute | solution.py:759
  4.4 5.2 %collective-permute-start.1 = (f32[29,8,128]{2,1,0:T(8,128)S(1)}, f32[29,8,128]{2,1,0:T(8,128)S(1)}, u32[]{:S(2)}, u32[]{:S(2)}) collective-permute-start(f32[29,8,128]{2,1,0:T(8,128)S(1)} %get-tuple-element.39), channel_id=1, source_target_pairs={{1,2},{3,4},{5,6},{7,8},{9,10},{11,12},{13,14},{2,1},{4,3},{6,5},{... | collective-permute-start | bytes 356360 | tf_op jit(solution)/shard_map/ppermute | solution.py:759
  5.1 4.5 %collective-permute-start.2 = (f32[5,8,128]{2,1,0:T(8,128)S(1)}, f32[5,8,128]{2,1,0:T(8,128)S(1)}, u32[]{:S(2)}, u32[]{:S(2)}) collective-permute-start(f32[5,8,128]{2,1,0:T(8,128)S(1)} %get-tuple-element.40), channel_id=1, source_target_pairs={{0,16},{16,0},{1,17},{17,1},{2,18},{18,2},{3,19},{19,3},{4,20},{20... | collective-permute-start | bytes 61448 | tf_op jit(solution)/shard_map/ppermute | solution.py:759
  13.2 6.7 %collective-permute-start.3 = (f32[28,8,128]{2,1,0:T(8,128)S(1)}, f32[28,8,128]{2,1,0:T(8,128)S(1)}, u32[]{:S(2)}, u32[]{:S(2)}) collective-permute-start(f32[28,8,128]{2,1,0:T(8,128)S(1)} %get-tuple-element.48), channel_id=1, source_target_pairs={{0,1},{2,3},{4,5},{6,7},{8,9},{10,11},{12,13},{14,15},{1,0},{3,2},... | collective-permute-start | bytes 344072 | tf_op jit(solution)/shard_map/ppermute | solution.py:759
  15.4 4.5 %collective-permute-start.4 = (f32[28,8,128]{2,1,0:T(8,128)S(1)}, f32[28,8,128]{2,1,0:T(8,128)S(1)}, u32[]{:S(2)}, u32[]{:S(2)}) collective-permute-start(f32[28,8,128]{2,1,0:T(8,128)S(1)} %get-tuple-element.49), channel_id=1, source_target_pairs={{1,2},{3,4},{5,6},{7,8},{9,10},{11,12},{13,14},{2,1},{4,3},{6,5},{... | collective-permute-start | bytes 344072 | tf_op jit(solution)/shard_map/ppermute | solution.py:759
  16.1 3.8 %collective-permute-start.5 = (f32[4,8,128]{2,1,0:T(8,128)S(1)}, f32[4,8,128]{2,1,0:T(8,128)S(1)}, u32[]{:S(2)}, u32[]{:S(2)}) collective-permute-start(f32[4,8,128]{2,1,0:T(8,128)S(1)} %get-tuple-element.50), channel_id=1, source_target_pairs={{0,16},{16,0},{1,17},{17,1},{2,18},{18,2},{3,19},{19,3},{4,20},{20... | collective-permute-start | bytes 49160 | tf_op jit(solution)/shard_map/ppermute | solution.py:759
  26.0 4.8 %collective-permute-start.6 = (f32[5,8,128]{2,1,0:T(8,128)S(1)}, f32[5,8,128]{2,1,0:T(8,128)S(1)}, u32[]{:S(2)}, u32[]{:S(2)}) collective-permute-start(f32[5,8,128]{2,1,0:T(8,128)S(1)} %get-tuple-element.52), channel_id=1, source_target_pairs={{0,16},{16,0},{1,17},{17,1},{2,18},{18,2},{3,19},{19,3},{4,20},{20... | collective-permute-start | bytes 61448 | tf_op jit(solution)/shard_map/ppermute | solution.py:759
  27.8 9.9 %collective-permute-start.8 = (f32[28,8,128]{2,1,0:T(8,128)S(1)}, f32[28,8,128]{2,1,0:T(8,128)S(1)}, u32[]{:S(2)}, u32[]{:S(2)}) collective-permute-start(f32[28,8,128]{2,1,0:T(8,128)S(1)} %get-tuple-element.62), channel_id=1, source_target_pairs={{0,1},{2,3},{4,5},{6,7},{8,9},{10,11},{12,13},{14,15},{1,0},{3,2},... | collective-permute-start | bytes 344072 | tf_op jit(solution)/shard_map/ppermute | solution.py:759
  30.1 7.6 %collective-permute-start.9 = (f32[28,8,128]{2,1,0:T(8,128)S(1)}, f32[28,8,128]{2,1,0:T(8,128)S(1)}, u32[]{:S(2)}, u32[]{:S(2)}) collective-permute-start(f32[28,8,128]{2,1,0:T(8,128)S(1)} %get-tuple-element.63), channel_id=1, source_target_pairs={{1,2},{3,4},{5,6},{7,8},{9,10},{11,12},{13,14},{2,1},{4,3},{6,5},{... | collective-permute-start | bytes 344072 | tf_op jit(solution)/shard_map/ppermute | solution.py:759
  30.8 6.9 %collective-permute-start.7 = (f32[8,128]{1,0:T(8,128)S(1)}, f32[8,128]{1,0:T(8,128)S(1)}, u32[]{:S(2)}, u32[]{:S(2)}) collective-permute-start(f32[8,128]{1,0:T(8,128)S(1)} %fusion.1), channel_id=1, source_target_pairs={{0,2},{1,3},{2,0},{3,1},{4,6},{5,7},{6,4},{7,5},{8,10},{9,11},{10,... | collective-permute-start | bytes 12296 | tf_op jit(solution)/shard_map/ppermute | solution.py:773
  42.1 1.5 %collective-permute-start.10 = (f32[29,8,128]{2,1,0:T(8,128)S(1)}, f32[29,8,128]{2,1,0:T(8,128)S(1)}, u32[]{:S(2)}, u32[]{:S(2)}) collective-permute-start(f32[29,8,128]{2,1,0:T(8,128)S(1)} %get-tuple-element.65), channel_id=1, source_target_pairs={{0,1},{2,3},{4,5},{6,7},{8,9},{10,11},{12,13},{14,15},{1,0},{3,2},... | collective-permute-start | bytes 356360 | tf_op jit(solution)/shard_map/ppermute | solution.py:759
  42.2 11.6 %collective-permute-start.12 = (f32[4,8,128]{2,1,0:T(8,128)S(1)}, f32[4,8,128]{2,1,0:T(8,128)S(1)}, u32[]{:S(2)}, u32[]{:S(2)}) collective-permute-start(f32[4,8,128]{2,1,0:T(8,128)S(1)} %get-tuple-element.67), channel_id=1, source_target_pairs={{0,16},{16,0},{1,17},{17,1},{2,18},{18,2},{3,19},{19,3},{4,20},{20... | collective-permute-start | bytes 49160 | tf_op jit(solution)/shard_map/ppermute | solution.py:759
  42.9 11.0 %collective-permute-start.11 = (f32[28,8,128]{2,1,0:T(8,128)S(1)}, f32[28,8,128]{2,1,0:T(8,128)S(1)}, u32[]{:S(2)}, u32[]{:S(2)}) collective-permute-start(f32[28,8,128]{2,1,0:T(8,128)S(1)} %get-tuple-element.66), channel_id=1, source_target_pairs={{1,2},{3,4},{5,6},{7,8},{9,10},{11,12},{13,14},{2,1},{4,3},{6,5},{... | collective-permute-start | bytes 344072 | tf_op jit(solution)/shard_map/ppermute | solution.py:759
  43.6 7.7 %collective-permute-start.13 = (f32[8,128]{1,0:T(8,128)S(1)}, f32[8,128]{1,0:T(8,128)S(1)}, u32[]{:S(2)}, u32[]{:S(2)}) collective-permute-start(f32[8,128]{1,0:T(8,128)S(1)} %fusion), channel_id=1, source_target_pairs={{0,4},{1,5},{2,6},{3,7},{4,0},{5,1},{6,2},{7,3},{8,12},{9,13},{10,... | collective-permute-start | bytes 12296 | tf_op jit(solution)/shard_map/ppermute | solution.py:773
  51.3 4.5 %collective-permute-start.14 = (f32[8,128]{1,0:T(8,128)S(1)}, f32[8,128]{1,0:T(8,128)S(1)}, u32[]{:S(2)}, u32[]{:S(2)}) collective-permute-start(f32[8,128]{1,0:T(8,128)S(1)} %add.22), channel_id=1, source_target_pairs={{0,8},{1,9},{2,10},{3,11},{4,12},{5,13},{6,14},{7,15},{8,0},{9,1},... | collective-permute-start | bytes 12296 | tf_op jit(solution)/shard_map/ppermute | solution.py:773

commit v2 on v1

--- a/solution.py
+++ b/solution.py
@@ -167,46 +167,68 @@
             sdx[f] = gather_edges(flux - roll(flux, 1))
 
 
-def forward_rows(step, ext, words, low_words, fvy, vy):
+def forward_face(j, step, ext, words, low_words, fvy, vy):
     bits = level_bits()
-
-    def face(j, carry):
-        wall = row_wall(j)
-        for p, (lead, members) in enumerate(PHASES):
-            here = spread(words, plane(step, 1, p // 2) * ROWS + jnp.maximum(j - 1, 0))
-            low = jnp.broadcast_to(low_words[plane(step, 1, p // 2)][None], (8, LANES))
-            word = jnp.where(j == 0, low, here)
-            flag = (word & bits[p % 2]) != 0
-            v_low = ext[lead + 2, j + 1] * inverse_root(ext[lead, j + 1])
-            v_high = ext[lead + 2, j + 2] * inverse_root(ext[lead, j + 2])
-            vy[p, j] = wall * (v_low + v_high)
-            for f in range(lead, lead + members):
-                fvy[f, j] = face_values(ext[f, j], ext[f, j + 1], ext[f, j + 2], ext[f, j + 3], flag)
-        return carry
-
-    lax.fori_loop(0, ROWS + 1, face, 0)
-
-
-def carried_row(step, r, ext, words, sdx, fvx, ux, fvy, vy):
-    bits = level_bits()
-    edges = edge_lanes()
+    wall = FACE if low_words is None else row_wall(j)
+    for p, (lead, members) in enumerate(PHASES):
+        which = plane(step, 1, p // 2)
+        word = face_word(j, words, low_words, which)
+        flag = (word & bits[p % 2]) != 0
+        v_low = ext[lead + 2, j + 1] * inverse_root(ext[lead, j + 1])
+        v_high = ext[lead + 2, j + 2] * inverse_root(ext[lead, j + 2])
+        vy[p, j] = wall * (v_low + v_high)
+        for f in range(lead, lead + members):
+            fvy[f, j] = face_values(ext[f, j], ext[f, j + 1], ext[f, j + 2], ext[f, j + 3], flag)
+
+
+def face_word(j, words, low_words, which):
+    if low_words is None:
+        return spread(words, which * ROWS + j - 1)
+    here = spread(words, which * ROWS + jnp.maximum(j - 1, 0))
+    low = jnp.broadcast_to(low_words[which : which + 1], (8, LANES))
+    return jnp.where(j == 0, low, here)
+
+
+def carried_row(r, edges, ext, sdx, along, fvy, vy):
     carried = []
     for p, (lead, members) in enumerate(PHASES):
-        word = spread(words, plane(step, 0, p // 2) * ROWS + r)
-        flag = (word & bits[p % 2]) != 0
-        u = ext[lead + 1, r + 2] * inverse_root(ext[lead, r + 2])
-        speed = FACE * (u + roll(u, -1))
-        ux[p, r] = speed
         below, above = vy[p, r], vy[p, r + 1]
         for f in range(lead, lead + members):
-            c = ext[f, r + 2]
-            value = face_values(roll(c, 1), c, roll(c, -1), roll(c, -2), flag)
-            fvx[f, r] = value
-            flux = speed * value
-            along_x = jnp.where(edges, roll(sdx[f], 124 - 16 * r), flux - roll(flux, 1))
+            seam = ext[f, r + 2] - roll(sdx[f], 124 - 16 * r)
             along_y = above * fvy[f, r + 1] - below * fvy[f, r]
-            carried.append(c - along_x - along_y)
+            carried.append(jnp.where(edges, seam, along[f, r]) - along_y)
     return carried
+
+
+def early_kernel(step):
+    def kernel(ext, words, fvx, ux, along, fvy, vy):
+        bits = level_bits()
+
+        def one_row(r, carry):
+            for p, (lead, members) in enumerate(PHASES):
+                word = spread(words, plane(step, 0, p // 2) * ROWS + r)
+                flag = (word & bits[p % 2]) != 0
+                u = ext[lead + 1, r + 2] * inverse_root(ext[lead, r + 2])
+                speed = FACE * (u + roll(u, -1))
+                ux[p, r] = speed
+                for f in range(lead, lead + members):
+                    c = ext[f, r + 2]
+                    value = face_values(roll(c, 1), c, roll(c, -1), roll(c, -2), flag)
+                    fvx[f, r] = value
+                    flux = speed * value
+                    along[f, r] = c - (flux - roll(flux, 1))
+            return carry
+
+        lax.fori_loop(0, ROWS, one_row, 0, unroll=2)
+        for j in range(2, ROWS - 1):
+            forward_face(j, step, ext, words, None, fvy, vy)
+
+    return kernel
+
+
+def outer_faces(step, ext, words, low_words, fvy, vy):
+    for j in (0, 1, ROWS - 1, ROWS):
+        forward_face(j, step, ext, words, low_words, fvy, vy)
 
 
 def coupled(c):
@@ -329,9 +351,8 @@
     return ghosts
 
 
-def backward_fluxes(step, ext, words, low_words, a_ext, fvx, ux, fvy, vy, sdc, sdu, gl, gh, dvy, put):
+def backward_faces(step, ext, words, low_words, a_ext, fvy, vy, gl, gh, dvy, put):
     bits = level_bits()
-    edges = edge_lanes()
     zero = jnp.zeros((8, LANES), jnp.float32)
     for k in (0, 1, 2, 12, 13, 14):
         for f in range(FIELDS):
@@ -343,9 +364,7 @@
     def face(j, carry):
         wall = row_wall(j)
         for p, (lead, members) in enumerate(PHASES):
-            here = spread(words, plane(step, 1, p // 2) * ROWS + jnp.maximum(j - 1, 0))
-            low_word = jnp.broadcast_to(low_words[plane(step, 1, p // 2)][None], (8, LANES))
-            word = jnp.where(j == 0, low_word, here)
+            word = face_word(j, words, low_words, plane(step, 1, p // 2))
             flag = (word & bits[p % 2]) != 0
             speed = vy[p, j]
             dv = jnp.zeros((8, LANES), jnp.float32)
@@ -359,10 +378,23 @@
             dvy[p, j + 3] = wall * dv
         return carry
 
-    lax.fori_loop(0, ROWS + 1, face, 0)
-
-    def along_y(f, i):
-        return 3.0 * (gl[f, i + 4] + gh[f, i + 3]) - gl[f, i + 5] - gh[f, i + 2]
+    lax.fori_loop(0, ROWS + 1, face, 0, unroll=9)
+    for i in (-2, -1, ROWS, ROWS + 1):
+        total = [transposed_y(gl, gh, f, i) for f in range(FIELDS)]
+        for p, (lead, members) in enumerate(PHASES):
+            dv = dvy[p, i + 4] + dvy[p, i + 3]
+            state = (ext[lead, i + 2], ext[lead + 1, i + 2], ext[lead + 2, i + 2])
+            add_speed_terms(total, state, lead, None, dv)
+        put(i, total)
+
+
+def transposed_y(gl, gh, f, i):
+    return 3.0 * (gl[f, i + 4] + gh[f, i + 3]) - gl[f, i + 5] - gh[f, i + 2]
+
+
+def backward_own(step, ext, words, a_ext, fvx, ux, sdc, sdu, gl, gh, dvy, put):
+    bits = level_bits()
+    edges = edge_lanes()
 
     def own(r, carry):
         total = [None] * FIELDS
@@ -375,7 +407,7 @@
                 a = a_ext[f, r + 1]
                 part, term = scatter_x(a, fvx[f, r], speed, flag)
                 part = jnp.where(edges, roll(sdc[f], 124 - 16 * r), part)
-                total[f] = a + part + along_y(f, r)
+                total[f] = a + part + transposed_y(gl, gh, f, r)
                 du = du + term
             du = FACE * (du + roll(du, 1))
             du = jnp.where(edges, roll(sdu[p], 124 - 16 * r), du)
@@ -385,19 +417,7 @@
         put(r, total)
         return carry
 
-    lax.fori_loop(0, ROWS, own, 0)
-
-    def ghost(t, carry):
-        i = jnp.where(t < 2, t - 2, t + 6)
-        total = [along_y(f, i) for f in range(FIELDS)]
-        for p, (lead, members) in enumerate(PHASES):
-            dv = dvy[p, i + 4] + dvy[p, i + 3]
-            state = (ext[lead, i + 2], ext[lead + 1, i + 2], ext[lead + 2, i + 2])
-            add_speed_terms(total, state, lead, None, dv)
-        put(i, total)
-        return carry
-
-    lax.fori_loop(0, 4, ghost, 0)
+    lax.fori_loop(0, ROWS, own, 0, unroll=2)
 
 
 def level_weight():
@@ -445,23 +465,31 @@
             to_b[2 * f + j] = source[f, b_row + j]
 
 
-def pack_kernel(start, words, terrain, rows, edges, edge_words, to_a, to_b, to_c):
+def pack_kernel(start_in, words_in, terrain_in, ext, edges, edge_words, to_a, to_b, to_c, start, words, terrain, sems):
+    copies = [
+        pltpu.make_async_copy(source, target, sems.at[k])
+        for k, (source, target) in enumerate(((start_in, start), (words_in, words), (terrain_in, terrain)))
+    ]
+    for copy in copies:
+        copy.start()
     zero_edges(edges)
     edge_words[...] = jnp.zeros((8, LANES), jnp.int32)
     slots = lax.broadcasted_iota(jnp.int32, (8, LANES), 0)
+    for copy in copies:
+        copy.wait()
 
     def one_row(r, carry):
         values = [start[f, pl.ds(r, 8, stride=8), :] for f in range(FIELDS)]
         for f in range(FIELDS):
-            rows[f, r] = values[f]
+            ext[f, r + 2] = values[f]
         add_edges(edges, values, r)
         mine = strip_row() == r
         row_words = jnp.where(slots == TERRAIN_SLOT, spread(terrain, r), words[pl.ds(r, 8, stride=8), :])
-        edge_words[...] = jnp.where(mine, roll(row_words, 16 * r + 4), edge_words[...])
+        edge_words[...] = jnp.where(mine, roll(row_words, (16 * r + 4) % LANES), edge_words[...])
         return carry
 
-    lax.fori_loop(0, ROWS, one_row, 0)
-    put_edge_rows(rows, 0, to_a, to_b)
+    lax.fori_loop(0, ROWS, one_row, 0, unroll=8)
+    put_edge_rows(ext, 2, to_a, to_b)
     top = words[pl.ds(ROWS - 1, 8, stride=8), :]
     is_even = row_bases()
     a_row = jnp.where(is_even, ROWS - 2, 0)
@@ -480,20 +508,13 @@
 
 def first_kernel(has_odd):
     def kernel(*refs):
-        rows, edges, edge_words, words, terrain, coef, from_a, from_b, from_c = refs[:9]
-        from_d = refs[9] if has_odd else None
-        outs = refs[9 + has_odd :]
-        (ext, strip, carried_ref, fvx, ux, fvy, vy, sfv, su, drag_ref, class_ref, low_ref, left_ref) = outs[:13]
-        middle, before, before_edges, to_a, to_b, to_c = outs[13:19]
-        (sdx,) = outs[19:]
+        (_, _, _, edges, edge_words, along, words, terrain, coef, from_a, from_b, from_c) = refs[:12]
+        from_d = refs[12] if has_odd else None
+        outs = refs[12 + has_odd :]
+        (ext, fvy, vy, strip, carried_ref, sfv, su, drag_ref, class_ref, low_ref, left_ref) = outs[:11]
+        middle, before, before_edges, to_a, to_b, to_c = outs[11:17]
+        (sdx,) = outs[17:]
         pick = side_payloads(from_c, from_d)
-
-        def copy_row(r, carry):
-            for f in range(FIELDS):
-                ext[f, r + 2] = rows[f, r]
-            return carry
-
-        lax.fori_loop(0, ROWS, copy_row, 0)
         fill_ghost_rows(ext, from_a, from_b)
         build_strip(edges, pick, strip)
         low_words, left_words = neighbour_words(from_a, from_b, pick)
@@ -508,84 +529,78 @@
         class_ref[pl.ds(12, 4), :] = strip_classes(edge_words, pick)[:4]
         drag_ref[...] = drag_table(class_ref[...], coef)
         forward_strip(0, strip, edge_words, left_words, sfv, su, sdx)
-        forward_rows(0, ext, words, low_words, fvy, vy)
+        outer_faces(0, ext, words, low_words, fvy, vy)
         zero_edges(before_edges)
         weight = level_weight()
+        seams = edge_lanes()
 
         def one_row(r, carry):
-            c = carried_row(0, r, ext, words, sdx, fvx, ux, fvy, vy)
+            c = carried_row(r, seams, ext, sdx, along, fvy, vy)
             for f in range(FIELDS):
                 carried_ref[f, r] = c[f]
             q = coupled(c)[0]
             for f in range(FIELDS):
-                before[f, r] = q[f]
+                before[f, r + 2] = q[f]
             add_edges(before_edges, q, r)
             q = dragged(q, weight * spread(drag_ref, r + 2))
             for f in range(FIELDS):
-                middle[f, r] = q[f]
+                middle[f, r + 2] = q[f]
             return carry
 
-        lax.fori_loop(0, ROWS, one_row, 0)
-        put_edge_rows(before, 0, to_a, to_b)
+        lax.fori_loop(0, ROWS, one_row, 0, unroll=2)
+        put_edge_rows(before, 2, to_a, to_b)
         edge_payload(before_edges, to_c)
 
     return kernel
 
 
-def ghost_rows_out(part, to_a, to_b):
+def put_ghost_rows(values, row, to_a, to_b):
     is_even = row_bases()
-    a_row = jnp.where(is_even, ROWS + 2, 0)
-    b_row = jnp.where(is_even, 0, ROWS + 2)
-    for f in range(FIELDS):
-        for j in range(2):
-            to_a[2 * f + j] = part[f, a_row + j]
-            to_b[2 * f + j] = part[f, b_row + j]
+    j = row % 2
+    above = row >= ROWS
+
+    @pl.when(is_even if above else jnp.logical_not(is_even))
+    def _():
+        for f in range(FIELDS):
+            to_a[2 * f + j] = values[f]
+
+    @pl.when(jnp.logical_not(is_even) if above else is_even)
+    def _():
+        for f in range(FIELDS):
+            to_b[2 * f + j] = values[f]
 
 
 def second_kernel(has_odd):
     def kernel(*refs):
-        middle, before, before_edges, edge_words, words, drag_ref, class_ref, low_ref, left_ref, adjoint = refs[:10]
-        from_a, from_b, from_c = refs[10:13]
-        from_d = refs[13] if has_odd else None
-        outs = refs[13 + has_odd :]
-        part, to_a, to_b, to_c = outs[:4]
-        (ext, strip, fvx, ux, fvy, vy, sfv, su, sdx, a_ext, edges_a, sdc, sdu, gl, gh, dvy) = outs[4:20]
-        before_ext, before_strip, cells = outs[20:]
+        (_, _, _, _, before_edges, edge_words, along, fvx, ux, words) = refs[:10]
+        (drag_ref, class_ref, low_ref, left_ref, adjoint, from_a, from_b, from_c) = refs[10:18]
+        from_d = refs[18] if has_odd else None
+        outs = refs[18 + has_odd :]
+        ext, before, fvy, vy, part, to_a, to_b, to_c = outs[:8]
+        (strip, sfv, su, sdx, a_ext, edges_a, sdc, sdu, gl, gh, dvy, before_strip, cells) = outs[8:]
         pick = side_payloads(from_c, from_d)
         low_words, left_words = low_ref[...], left_ref[...]
         weight = level_weight()
-
-        def copy_row(r, carry):
-            for f in range(FIELDS):
-                ext[f, r + 2] = middle[f, r]
-                before_ext[f, r + 2] = before[f, r]
-            return carry
-
-        lax.fori_loop(0, ROWS, copy_row, 0)
-        fill_ghost_rows(before_ext, from_a, from_b)
-
-        def ghost_row(t, carry):
-            row = jnp.where(t < 2, t, t + 8)
-            q = dragged([before_ext[f, row] for f in range(FIELDS)], weight * spread(drag_ref, row))
+        fill_ghost_rows(before, from_a, from_b)
+        for row in (0, 1, ROWS + 2, ROWS + 3):
+            q = dragged([before[f, row] for f in range(FIELDS)], weight * spread(drag_ref, row))
             for f in range(FIELDS):
                 ext[f, row] = q[f]
-            return carry
-
-        lax.fori_loop(0, 4, ghost_row, 0)
         build_strip(before_edges, pick, before_strip)
         q = dragged([before_strip[f] for f in range(FIELDS)], weight * spread(drag_ref, 12))
         for f in range(FIELDS):
             strip[f] = q[f]
         forward_strip(1, strip, edge_words, left_words, sfv, su, sdx)
-        forward_rows(1, ext, words, low_words, fvy, vy)
+        outer_faces(1, ext, words, low_words, fvy, vy)
         zero_edges(edges_a)
         for f in range(FIELDS):
             a_ext[f, 0] = jnp.zeros((8, LANES), jnp.float32)
             a_ext[f, ROWS + 1] = jnp.zeros((8, LANES), jnp.float32)
         cells[...] = jnp.zeros((16, LANES), jnp.float32)
+        seams = edge_lanes()
 
         def one_row(r, carry):
-            c = carried_row(1, r, ext, words, sdx, fvx, ux, fvy, vy)
+            c = carried_row(r, seams, ext, sdx, along, fvy, vy)
             a = [adjoint[f, pl.ds(r, 8, stride=8), :] for f in range(FIELDS)]
             a, terms = stepped_back(c, weight * spread(drag_ref, r + 2), a, True)
             cells[pl.ds(r + 2, 1), :] = level_sum(weight * terms)
@@ -594,21 +609,28 @@
             add_edges(edges_a, a, r)
             return carry
 
-        lax.fori_loop(0, ROWS, one_row, 0)
+        lax.fori_loop(0, ROWS, one_row, 0, unroll=2)
         ghosts = backward_strip(1, strip, edges_a, edge_words, left_words, sfv, su, sdc, sdu, to_c)
         pos = strip_pos()
         terms = jnp.where((pos >= 4) & (pos < 8), drag_terms(lambda f: before_strip[f], ghosts), 0.0)
         cells[pl.ds(12, 1), :] = level_sum(weight * terms)
 
-        def put(row, values):
-            for f in range(FIELDS):
-                part[f, row + 2] = values[f]
-            terms = drag_terms(lambda f: before_ext[f, row + 2], values)
+        def put_terms(row, values):
+            terms = drag_terms(lambda f: before[f, row + 2], values)
             at = pl.ds(row + 2, 1)
             cells[at, :] = cells[at, :] + level_sum(weight * terms)
 
-        backward_fluxes(1, ext, words, low_words, a_ext, fvx, ux, fvy, vy, sdc, sdu, gl, gh, dvy, put)
-        ghost_rows_out(part, to_a, to_b)
+        def put_ghost(row, values):
+            put_ghost_rows(values, row, to_a, to_b)
+            put_terms(row, values)
+
+        def put_own(row, values):
+            for f in range(FIELDS):
+                part[f, row] = values[f]
+            put_terms(row, values)
+
+        backward_faces(1, ext, words, low_words, a_ext, fvy, vy, gl, gh, dvy, put_ghost)
+        backward_own(1, ext, words, a_ext, fvx, ux, sdc, sdu, gl, gh, dvy, put_own)
         to_c[4] = binned(class_ref[...], cells[...])
 
     return kernel
@@ -629,41 +651,33 @@
 
 def collect(part, from_a, from_b, pick, incoming):
     is_even = row_bases()
-    a_row = jnp.where(is_even, ROWS, 2)
-    b_row = jnp.where(is_even, 2, ROWS)
+    a_row = jnp.where(is_even, ROWS - 2, 0)
+    b_row = ROWS - 2 - a_row
     for f in range(FIELDS):
         for j in range(2):
             part[f, a_row + j] = part[f, a_row + j] + from_a[2 * f + j]
             part[f, b_row + j] = part[f, b_row + j] + from_b[2 * f + j]
     pos = strip_pos()
+    at_left = (pos == 4) | (pos == 5)
+    at_right = (pos == 2) | (pos == 3)
     for g in range(4):
         left, right = pick(g)
         for f in range(4 * g, min(4 * g + 4, FIELDS)):
             q = f % 4
-            at_left = (pos == 4) | (pos == 5)
-            at_right = (pos == 2) | (pos == 3)
-            value = jnp.where(at_left, roll(left, 4 - 4 * q), jnp.where(at_right, roll(right, -4 * q), 0.0))
-            incoming[f] = value
+            incoming[f] = jnp.where(at_left, roll(left, 4 - 4 * q), jnp.where(at_right, roll(right, -4 * q), 0.0))
 
 
 def third_kernel(has_odd):
     def kernel(*refs):
-        (part_in, grads, ext, strip, carried_ref, fvx, ux, fvy, vy, sfv, su) = refs[:11]
-        drag_ref, low_ref, left_ref, edge_words, words = refs[11:16]
-        from_a, from_b, from_c = refs[16:19]
-        from_d = refs[19] if has_odd else None
-        outs = refs[19 + has_odd :]
-        part, to_a, to_b, to_c = outs[:4]
-        (incoming, a_ext, edges_a, sdc, sdu, gl, gh, dvy) = outs[4:]
+        (_, ext, strip, carried_ref, fvy, vy, sfv, su) = refs[:8]
+        drag_ref, low_ref, left_ref, edge_words, words = refs[8:13]
+        from_a, from_b, from_c = refs[13:16]
+        from_d = refs[16] if has_odd else None
+        outs = refs[16 + has_odd :]
+        part, to_a, to_b, to_c, a_ext, sdc, sdu, gl, gh, dvy = outs[:10]
+        incoming, edges_a = outs[10:]
         pick = side_payloads(from_c, from_d)
         low_words, left_words = low_ref[...], left_ref[...]
-
-        def copy_row(r, carry):
-            for f in range(FIELDS):
-                part[f, r + 2] = part_in[f, r + 2]
-            return carry
-
-        lax.fori_loop(0, ROWS, copy_row, 0)
         collect(part, from_a, from_b, pick, incoming)
         zero_edges(edges_a)
         for f in range(FIELDS):
@@ -674,53 +688,48 @@
 
         def one_row(r, carry):
             c = [carried_ref[f, r] for f in range(FIELDS)]
-            a = [
-                part[f, r + 2] + jnp.where(edges, roll(incoming[f], 124 - 16 * r), 0.0)
-                for f in range(FIELDS)
-            ]
+            a = [part[f, r] + jnp.where(edges, roll(incoming[f], 124 - 16 * r), 0.0) for f in range(FIELDS)]
             a, _ = stepped_back(c, weight * spread(drag_ref, r + 2), a, False)
             for f in range(FIELDS):
                 a_ext[f, r + 1] = a[f]
             add_edges(edges_a, a, r)
             return carry
 
-        lax.fori_loop(0, ROWS, one_row, 0)
-        to_a[2 * FIELDS] = grads[...]
+        lax.fori_loop(0, ROWS, one_row, 0, unroll=4)
         backward_strip(0, strip, edges_a, edge_words, left_words, sfv, su, sdc, sdu, to_c)
 
-        def put(row, values):
-            for f in range(FIELDS):
-                part[f, row + 2] = values[f]
-
-        backward_fluxes(0, ext, words, low_words, a_ext, fvx, ux, fvy, vy, sdc, sdu, gl, gh, dvy, put)
-        ghost_rows_out(part, to_a, to_b)
+        def put_ghost(row, values):
+            put_ghost_rows(values, row, to_a, to_b)
+
+        backward_faces(0, ext, words, low_words, a_ext, fvy, vy, gl, gh, dvy, put_ghost)
 
     return kernel
+
+
+def own_kernel(ext, words, a_ext, fvx, ux, sdc, sdu, gl, gh, dvy, part):
+    def put(row, values):
+        for f in range(FIELDS):
+            part[f, row] = values[f]
+
+    backward_own(0, ext, words, a_ext, fvx, ux, sdc, sdu, gl, gh, dvy, put)
 
 
 def last_kernel(has_odd):
     def kernel(*refs):
-        part_in, from_a, from_b, from_c = refs[:4]
+        _, from_a, from_b, from_c = refs[:4]
         from_d = refs[4] if has_odd else None
         out, part, incoming = refs[4 + has_odd :]
         pick = side_payloads(from_c, from_d)
-
-        def copy_row(r, carry):
-            for f in range(FIELDS):
-                part[f, r + 2] = part_in[f, r + 2]
-            return carry
-
-        lax.fori_loop(0, ROWS, copy_row, 0)
         collect(part, from_a, from_b, pick, incoming)
         edges = edge_lanes()
 
         def one_row(r, carry):
             for f in range(FIELDS):
-                value = part[f, r + 2] + jnp.where(edges, roll(incoming[f], 124 - 16 * r), 0.0)
+                value = part[f, r] + jnp.where(edges, roll(incoming[f], (124 - 16 * r) % LANES), 0.0)
                 out[f, pl.ds(r, 8, stride=8), :] = value
             return carry
 
-        lax.fori_loop(0, ROWS, one_row, 0)
+        lax.fori_loop(0, ROWS, one_row, 0, unroll=8)
 
     return kernel
 
@@ -737,16 +746,17 @@
     return pltpu.VMEM((*shape, 8, LANES), dtype)
 
 
-def call(kernel, outs, scratches, args, smem=()):
-    in_specs = [
-        pl.BlockSpec(memory_space=pltpu.SMEM if k in smem else pltpu.VMEM) for k in range(len(args))
-    ]
+def call(kernel, outs, scratches, args, smem=(), hbm=(), aliases=None):
+    def space(k):
+        return pltpu.SMEM if k in smem else pltpu.HBM if k in hbm else pltpu.VMEM
+
     return pl.pallas_call(
         kernel,
         out_shape=outs,
-        in_specs=in_specs,
+        in_specs=[pl.BlockSpec(memory_space=space(k)) for k in range(len(args))],
         out_specs=[pl.BlockSpec(memory_space=pltpu.VMEM)] * len(outs),
         scratch_shapes=scratches,
+        input_output_aliases=aliases or {},
         compiler_params=pltpu.CompilerParams(vmem_limit_bytes=32 << 20),
     )(*args)
 
@@ -781,62 +791,73 @@
     words = face_words.reshape(8 * ROWS, LANES)
     ints = jnp.int32
 
-    rows, edges, edge_words, to_a, to_b, to_c = call(
+    ext, edges, edge_words, *payload = call(
         pack_kernel,
-        [tiles(14, 8), tiles(14), tiles(dtype=ints), tiles(29), tiles(29), tiles(5)],
-        [],
-        [start, words, terrain],
+        [tiles(14, 12), tiles(14), tiles(dtype=ints), tiles(29), tiles(29), tiles(5)],
+        [
+            pltpu.VMEM(start.shape, jnp.float32),
+            pltpu.VMEM(words.shape, ints),
+            pltpu.VMEM(terrain.shape, ints),
+            pltpu.SemaphoreType.DMA((3,)),
+        ],
+        [pltpu.with_memory_space_constraint(x, pltpu.HBM) for x in (start, words, terrain)],
+        hbm=(0, 1, 2),
     )
-    got = exchange(to_a, to_b, to_c)
-    faces = [tiles(14, 8), tiles(4, 8), tiles(14, 9), tiles(4, 9), tiles(14), tiles(4)]
+    got = exchange(*payload)
+    early = [tiles(14, 8), tiles(4, 8), tiles(14, 8), tiles(14, 9), tiles(4, 9)]
+    fvx, ux, along, fvy, vy = call(early_kernel(0), early, [], [ext, words])
     res = call(
         first_kernel(has_odd),
-        [tiles(14, 12), tiles(14), tiles(14, 8), *faces, shaped(16, LANES), shaped(16, LANES, dtype=ints)]
-        + [tiles(dtype=ints), tiles(dtype=ints), tiles(14, 8), tiles(14, 8), tiles(14), tiles(28), tiles(28), tiles(4)],
+        [tiles(14, 12), tiles(14, 9), tiles(4, 9), tiles(14), tiles(14, 8), tiles(14), tiles(4)]
+        + [shaped(16, LANES), shaped(16, LANES, dtype=ints), tiles(dtype=ints), tiles(dtype=ints)]
+        + [tiles(14, 12), tiles(14, 12), tiles(14), tiles(28), tiles(28), tiles(4)],
         [scratch(14)],
-        [rows, edges, edge_words, words, terrain, drag_coef, *got],
-        smem=(5,),
+        [ext, fvy, vy, edges, edge_words, along, words, terrain, drag_coef, *got],
+        smem=(8,),
+        aliases={0: 0, 1: 1, 2: 2},
     )
-    ext, strip, carried_ref = res[:3]
-    saved = res[3:9]
-    drag_ref, class_ref, low_ref, left_ref = res[9:13]
-    middle, before, before_edges = res[13:16]
-    got = exchange(*res[16:19])
-    back = [scratch(14, 10), scratch(14), scratch(14), scratch(4), scratch(14, 15), scratch(14, 15), scratch(4, 15)]
-    part, to_a, to_b, to_c = call(
+    ext, fvy, vy, strip, carried_ref, sfv, su, drag_ref, class_ref, low_ref, left_ref = res[:11]
+    middle, before, before_edges, *payload = res[11:]
+    got = exchange(*payload)
+    fvx2, ux2, along2, fvy2, vy2 = call(early_kernel(1), early, [], [middle, words])
+    back = [tiles(14, 10), tiles(14), tiles(4), tiles(14, 15), tiles(14, 15), tiles(4, 15)]
+    kept = [scratch(14, 10), scratch(14), scratch(14), scratch(4), scratch(14, 15), scratch(14, 15), scratch(4, 15)]
+    part, *payload = call(
         second_kernel(has_odd),
-        [tiles(14, 12), tiles(28), tiles(28), tiles(5)],
-        [scratch(14, 12), scratch(14), scratch(14, 8), scratch(4, 8), scratch(14, 9), scratch(4, 9)]
-        + [scratch(14), scratch(4), scratch(14), *back]
-        + [scratch(14, 12), scratch(14), pltpu.VMEM((16, LANES), jnp.float32)],
-        [middle, before, before_edges, edge_words, words, drag_ref, class_ref, low_ref, left_ref, adjoint, *got],
+        [tiles(14, 12), tiles(14, 12), tiles(14, 9), tiles(4, 9), tiles(14, 8), tiles(28), tiles(28), tiles(5)],
+        [scratch(14), scratch(14), scratch(4), scratch(14), *kept, scratch(14), pltpu.VMEM((16, LANES), jnp.float32)],
+        [middle, before, fvy2, vy2, before_edges, edge_words, along2, fvx2, ux2, words]
+        + [drag_ref, class_ref, low_ref, left_ref, adjoint, *got],
+        aliases={0: 0, 1: 1, 2: 2, 3: 3},
+    )[4:]
+    got = exchange(*payload)
+    grads = payload[2][4] + got[2][4]
+    steps = [("gx", 2**k) for k in range(1, 32) if 2**k < nx] + [("gy", 2**k) for k in range(1, 32) if 2**k < ny]
+    grads = add_partner(add_partner(grads, "gy", 1), *steps[0])
+    part, to_a, to_b, to_c, *adjoints = call(
+        third_kernel(has_odd),
+        [tiles(14, 8), tiles(28), tiles(28), tiles(4), *back],
+        [scratch(14), scratch(14)],
+        [part, ext, strip, carried_ref, fvy, vy, sfv, su, drag_ref, low_ref, left_ref, edge_words, words, *got],
+        aliases={0: 0},
     )
+    a_ext, sdc, sdu, gl, gh, dvy = adjoints
+    grads, to_c = lax.optimization_barrier((grads, to_c))
     got = exchange(to_a, to_b, to_c)
-    grads = to_c[4] + got[2][4]
-    distance = 2
-    while distance < nx:
-        grads = add_partner(grads, "gx", distance)
-        distance *= 2
-    if ny > 2:
-        grads = add_partner(grads, "gy", 2)
-    part, to_a, to_b, to_c = call(
-        third_kernel(has_odd),
-        [tiles(14, 12), tiles(29), tiles(28), tiles(4)],
-        [scratch(14), *back],
-        [part, grads, ext, strip, carried_ref, *saved]
-        + [drag_ref, low_ref, left_ref, edge_words, words, *got],
-    )
-    got = exchange(to_a, to_b, to_c)
-    grads = grads + got[0][2 * FIELDS]
-    distance = 4
-    while distance < ny:
-        grads = add_partner(grads, "gy", distance)
-        distance *= 2
-    (out,) = call(
+    half = len(steps) // 2 + 1
+    a_ext, from_a = lax.optimization_barrier((a_ext, got[0]))
+    got = (from_a, *got[1:])
+    for axis, distance in steps[1:half]:
+        grads = add_partner(grads, axis, distance)
+    (part,) = call(own_kernel, [tiles(14, 8)], [], [ext, words, a_ext, fvx, ux, sdc, sdu, gl, gh, dvy])
+    for axis, distance in steps[half:]:
+        grads = add_partner(grads, axis, distance)
+    out, _ = call(
         last_kernel(has_odd),
-        [shaped(FIELDS, LEV * ROWS, LANES)],
-        [scratch(14, 12), scratch(14)],
+        [shaped(FIELDS, LEV * ROWS, LANES), tiles(14, 8)],
+        [scratch(14)],
         [part, *got],
+        aliases={0: 1},
     )
     grad_scale = math.sqrt(NCLASS / (terrain.size * nx * ny * LEV))
     return (out.reshape(start_state.shape), grads[0, :NCLASS] * grad_scale)

time: 56.6 us -> 49.9 us (0.88)
  the two profiles are of different devices: /device:TPU:0 before, /device:TPU:9 now
where the time goes in v2:
time: 49.9 us; the launch traced here: 49.7 us
  starting transfers between devices  23 us (46%)
  waiting for transfers between devices  12.4 us (25%)
  Pallas kernels  12.2 us (24%)
  between operations  0.8 us (2%)
  local copies, waits for them, and re-layouts  0.7 us (1%)
  other arithmetic  0.53 us (1%)
    ppermute x12, starting transfers between devices, swap(): return lax.ppermute(x, axis, pairs + [(j, i) for i, j in pairs])  18.6 us
    pallas_call x8, Pallas kernels, call(): pl.pallas_call(kernel, out_shape=outs, in_specs=[pl.BlockSpec(memory_spac...  12.2 us
    ppermute x12, waiting for transfers between devices, swap(): return lax.ppermute(x, axis, pairs + [(j, i) for i, j in pairs])  7.7 us
    ppermute x4, waiting for transfers between devices, add_partner(): lax.ppermute(x, axis, [(i, i ^ distance) for i in range(lax.axis_size(axi...  4.72 us
    ppermute x4, starting transfers between devices, add_partner(): lax.ppermute(x, axis, [(i, i ^ distance) for i in range(lax.axis_size(axi...  4.42 us
  transfers between devices with their start and end apart: 16, of which 9 were waited for; matrix products, arithmetic and copies ran while one was open for 1% of the time, Pallas kernels for 7%

profile of v2, /device:TPU:9, one launch (start us, length us, event | category | flops | bytes accessed | tf_op | source)
XLA Modules:
  0.0 49.7 jit_solution(5259362300033446678)
XLA Ops:
  0.6 1.3 %shard_map.68 = (f32[14,12,8,128]{3,2,1,0:T(8,128)S(1)}, f32[14,8,128]{2,1,0:T(8,128)S(1)}, s32[8,128]{1,0:T(8,128)S(1)}, f32[29,8,128]{2,1,0:T(8,128)S(1)}, f32...) custom-call(f32[14,64,128]{2,1,0:T(8,128)} %bitcast.16, s32[64,128]{1,0:T(8,128)} %bitcast.8, s32[8,128]{1,0:T(8,128)} %refs_7_.1), custom_call_target="tpu_custom_call" | custom-call | tf_op jit(solution)/shard_map/pallas_call | solution.py:753
  2.0 0.7 %collective-permute-start = (f32[29,8,128]{2,1,0:T(8,128)S(1)}, f32[29,8,128]{2,1,0:T(8,128)S(1)}, u32[]{:S(2)}, u32[]{:S(2)}) collective-permute-start(f32[29,8,128]{2,1,0:T(8,128)S(1)} %get-tuple-element.59), channel_id=1, source_target_pairs={{0,1},{2,3},{4,5},{6,7},{8,9},{10,11},{12,13},{14,15},{1,0},{3,2},... | collective-permute-start | bytes 356360 | tf_op jit(solution)/shard_map/ppermute | solution.py:769
  2.7 3.0 %collective-permute-start.1 = (f32[29,8,128]{2,1,0:T(8,128)S(1)}, f32[29,8,128]{2,1,0:T(8,128)S(1)}, u32[]{:S(2)}, u32[]{:S(2)}) collective-permute-start(f32[29,8,128]{2,1,0:T(8,128)S(1)} %get-tuple-element.60), channel_id=1, source_target_pairs={{1,2},{3,4},{5,6},{7,8},{9,10},{11,12},{13,14},{2,1},{4,3},{6,5},{... | collective-permute-start | bytes 356360 | tf_op jit(solution)/shard_map/ppermute | solution.py:769
  5.8 1.3 %collective-permute-start.2 = (f32[5,8,128]{2,1,0:T(8,128)S(1)}, f32[5,8,128]{2,1,0:T(8,128)S(1)}, u32[]{:S(2)}, u32[]{:S(2)}) collective-permute-start(f32[5,8,128]{2,1,0:T(8,128)S(1)} %get-tuple-element.61), channel_id=1, source_target_pairs={{0,16},{16,0},{1,17},{17,1},{2,18},{18,2},{3,19},{19,3},{4,20},{20... | collective-permute-start | bytes 61448 | tf_op jit(solution)/shard_map/ppermute | solution.py:769
  7.1 1.2 %shard_map.69 = (f32[14,8,8,128]{3,2,1,0:T(8,128)S(1)}, f32[4,8,8,128]{3,2,1,0:T(8,128)S(1)}, f32[14,8,8,128]{3,2,1,0:T(8,128)S(1)}, f32[14,9,8,128]{3,2,1,0:T(8,128)S(1)}, f32[4,9,8,128]{3,2,1,0:T(8,128)S(1)}) custom-call(f32[14,12,8,128]{3,2,1,0:T(8,128)S(1)} %get-tuple-element.53.ext.refs_0_, s32[64,128]{1,0:T(8,128)S(1)} %bitcast.9), custom_call_target="tpu_custom_call" | custom-call | tf_op jit(solution)/shard_map/pallas_call | solution.py:753
  8.2 0.5 %collective-permute-done.2.refs_11_ = f32[5,8,128]{2,1,0:T(8,128)S(1)} collective-permute-done((f32[5,8,128]{2,1,0:T(8,128)S(1)}, f32[5,8,128]{2,1,0:T(8,128)S(1)}, u32[]{:S(2)}, u32[]{:S(2)}) %collective-permute-start.2) | collective-permute-done | bytes 20512 | tf_op jit(solution)/shard_map/ppermute | solution.py:769
  8.8 1.4 %collective-permute-done.1.refs_10_ = f32[29,8,128]{2,1,0:T(8,128)S(1)} collective-permute-done((f32[29,8,128]{2,1,0:T(8,128)S(1)}, f32[29,8,128]{2,1,0:T(8,128)S(1)}, u32[]{:S(2)}, u32[]{:S(2)}) %collective-permute-start.1) | collective-permute-done | bytes 118816 | tf_op jit(solution)/shard_map/ppermute | solution.py:769
  10.2 0.7 %copy-done.2 = s32[8,128]{1,0:T(8,128)S(1)} copy-done((s32[8,128]{1,0:T(8,128)S(1)}, s32[8,128]{1,0:T(8,128)}, u32[]{:S(2)}) %copy-start.2) | copy-done | bytes 4120
  10.8 1.8 %shard_map.70 = (f32[14,12,8,128]{3,2,1,0:T(8,128)S(1)}, f32[14,9,8,128]{3,2,1,0:T(8,128)S(1)}, f32[4,9,8,128]{3,2,1,0:T(8,128)S(1)}, f32[14,8,128]{2,1,0:T(8,12...) custom-call(f32[14,12,8,128]{3,2,1,0:T(8,128)S(1)} %get-tuple-elemen, ...), custom_call_target="tpu_custom_call", output_to_operand_aliasing={{0}: (0, {}), {1}: (1, {}), {2}: (2, {})} | custom-call | tf_op jit(solution)/shard_map/pallas_call | solution.py:753
  12.7 3.1 %collective-permute-start.4 = (f32[28,8,128]{2,1,0:T(8,128)S(1)}, f32[28,8,128]{2,1,0:T(8,128)S(1)}, u32[]{:S(2)}, u32[]{:S(2)}) collective-permute-start(f32[28,8,128]{2,1,0:T(8,128)S(1)} %get-tuple-element.76), channel_id=1, source_target_pairs={{1,2},{3,4},{5,6},{7,8},{9,10},{11,12},{13,14},{2,1},{4,3},{6,5},{... | collective-permute-start | bytes 344072 | tf_op jit(solution)/shard_map/ppermute | solution.py:769
  15.9 1.3 %collective-permute-start.5 = (f32[4,8,128]{2,1,0:T(8,128)S(1)}, f32[4,8,128]{2,1,0:T(8,128)S(1)}, u32[]{:S(2)}, u32[]{:S(2)}) collective-permute-start(f32[4,8,128]{2,1,0:T(8,128)S(1)} %get-tuple-element.77), channel_id=1, source_target_pairs={{0,16},{16,0},{1,17},{17,1},{2,18},{18,2},{3,19},{19,3},{4,20},{20... | collective-permute-start | bytes 49160 | tf_op jit(solution)/shard_map/ppermute | solution.py:769
  17.2 1.2 %shard_map.71 = (f32[14,8,8,128]{3,2,1,0:T(8,128)S(1)}, f32[4,8,8,128]{3,2,1,0:T(8,128)S(1)}, f32[14,8,8,128]{3,2,1,0:T(8,128)S(1)}, f32[14,9,8,128]{3,2,1,0:T(8,128)S(1)}, f32[4,9,8,128]{3,2,1,0:T(8,128)S(1)}) custom-call(f32[14,12,8,128]{3,2,1,0:T(8,128)S(1)} %get-tuple-element.63.ext.refs_0_, s32[64,128]{1,0:T(8,128)S(1)} %bitcast.11), custom_call_target="tpu_custom_call" | custom-call | tf_op jit(solution)/shard_map/pallas_call | solution.py:753
  18.4 0.5 collective-permute-done.5.refs_17_
  18.8 1.4 %collective-permute-done.4.refs_16_ = f32[28,8,128]{2,1,0:T(8,128)S(1)} collective-permute-done((f32[28,8,128]{2,1,0:T(8,128)S(1)}, f32[28,8,128]{2,1,0:T(8,128)S(1)}, u32[]{:S(2)}, u32[]{:S(2)}) %collective-permute-start.4) | collective-permute-done | bytes 114720 | tf_op jit(solution)/shard_map/ppermute | solution.py:769
  20.2 3.3 %shard_map.72 = (f32[14,12,8,128]{3,2,1,0:T(8,128)S(1)}, f32[14,12,8,128]{3,2,1,0:T(8,128)S(1)}, f32[14,9,8,128]{3,2,1,0:T(8,128)S(1)}, f32[4,9,8,128]{3,2,1,0:T...) custom-call(f32[14,12,8,128]{3,2,1,0:T(8,128)S(1)} %get-tuple-elemen, ...), custom_call_target="tpu_custom_call", output_to_operand_aliasing={{0}: (0, {}), {1}: (1, {}), {2}: (2, {}), {3}: (3, {})} | custom-call | tf_op jit(solution)/shard_map/pallas_call | solution.py:753
  23.6 1.2 %collective-permute-start.8 = (f32[5,8,128]{2,1,0:T(8,128)S(1)}, f32[5,8,128]{2,1,0:T(8,128)S(1)}, u32[]{:S(2)}, u32[]{:S(2)}) collective-permute-start(f32[5,8,128]{2,1,0:T(8,128)S(1)} %get-tuple-element.87), channel_id=1, source_target_pairs={{0,16},{16,0},{1,17},{17,1},{2,18},{18,2},{3,19},{19,3},{4,20},{20... | collective-permute-start | bytes 61448 | tf_op jit(solution)/shard_map/ppermute | solution.py:769
  24.8 0.4 collective-permute-start.6
  25.2 2.4 %collective-permute-start.7 = (f32[28,8,128]{2,1,0:T(8,128)S(1)}, f32[28,8,128]{2,1,0:T(8,128)S(1)}, u32[]{:S(2)}, u32[]{:S(2)}) collective-permute-start(f32[28,8,128]{2,1,0:T(8,128)S(1)} %get-tuple-element.86), channel_id=1, source_target_pairs={{1,2},{3,4},{5,6},{7,8},{9,10},{11,12},{13,14},{2,1},{4,3},{6,5},{... | collective-permute-start | bytes 344072 | tf_op jit(solution)/shard_map/ppermute | solution.py:769
  27.7 1.2 %collective-permute-done.11 = f32[8,128]{1,0:T(8,128)S(1)} collective-permute-done((f32[8,128]{1,0:T(8,128)S(1)}, f32[8,128]{1,0:T(8,128)S(1)}, u32[]{:S(2)}, u32[]{:S(2)}) %collective-permute-start.11) | collective-permute-done | bytes 4128 | tf_op jit(solution)/shard_map/ppermute | solution.py:783
  28.9 2.0 %collective-permute-start.12 = (f32[8,128]{1,0:T(8,128)S(1)}, f32[8,128]{1,0:T(8,128)S(1)}, u32[]{:S(2)}, u32[]{:S(2)}) collective-permute-start(f32[8,128]{1,0:T(8,128)S(1)} %add.20), channel_id=1, source_target_pairs={{0,2},{1,3},{2,0},{3,1},{4,6},{5,7},{6,4},{7,5},{8,10},{9,11},{10,... | collective-permute-start | bytes 12296 | tf_op jit(solution)/shard_map/ppermute | solution.py:783
  30.8 1.1 %collective-permute-done.12 = f32[8,128]{1,0:T(8,128)S(1)} collective-permute-done((f32[8,128]{1,0:T(8,128)S(1)}, f32[8,128]{1,0:T(8,128)S(1)}, u32[]{:S(2)}, u32[]{:S(2)}) %collective-permute-start.12) | collective-permute-done | bytes 4128 | tf_op jit(solution)/shard_map/ppermute | solution.py:783
  32.0 0.6 %collective-permute-done.7.refs_14_ = f32[28,8,128]{2,1,0:T(8,128)S(1)} collective-permute-done((f32[28,8,128]{2,1,0:T(8,128)S(1)}, f32[28,8,128]{2,1,0:T(8,128)S(1)}, u32[]{:S(2)}, u32[]{:S(2)}) %collective-permute-start.7) | collective-permute-done | bytes 114720 | tf_op jit(solution)/shard_map/ppermute | solution.py:769
  32.6 1.2 %shard_map.73 = (f32[14,8,8,128]{3,2,1,0:T(8,128)S(1)}, f32[28,8,128]{2,1,0:T(8,128)S(1)}, f32[28,8,128]{2,1,0:T(8,128)S(1)}, f32[4,8,128]{2,1,0:T(8,128)S(1)}, ...) custom-call(f32[14,8,8,128]{3,2,1,0:T(8,128)S(1)} %get-tuple-element, ...), custom_call_target="tpu_custom_call", output_to_operand_aliasing={{0}: (0, {})} | custom-call | tf_op jit(solution)/shard_map/pallas_call | solution.py:753
  33.9 2.4 %collective-permute-done.14 = f32[8,128]{1,0:T(8,128)S(1)} collective-permute-done((f32[8,128]{1,0:T(8,128)S(1)}, f32[8,128]{1,0:T(8,128)S(1)}, u32[]{:S(2)}, u32[]{:S(2)}) %collective-permute-start.14) | collective-permute-done | bytes 4128 | tf_op jit(solution)/shard_map/ppermute | solution.py:783
  36.3 2.3 %collective-permute-start.15 = (f32[8,128]{1,0:T(8,128)S(1)}, f32[8,128]{1,0:T(8,128)S(1)}, u32[]{:S(2)}, u32[]{:S(2)}) collective-permute-start(f32[8,128]{1,0:T(8,128)S(1)} %add.22), channel_id=1, source_target_pairs={{0,8},{1,9},{2,10},{3,11},{4,12},{5,13},{6,14},{7,15},{8,0},{9,1},... | collective-permute-start | bytes 12296 | tf_op jit(solution)/shard_map/ppermute | solution.py:783
  38.6 0.2 collective-permute-start.13
  38.9 2.5 %collective-permute-start.9 = (f32[28,8,128]{2,1,0:T(8,128)S(1)}, f32[28,8,128]{2,1,0:T(8,128)S(1)}, u32[]{:S(2)}, u32[]{:S(2)}) collective-permute-start(f32[28,8,128]{2,1,0:T(8,128)S(1)} %get-tuple-element.89), channel_id=1, source_target_pairs={{0,1},{2,3},{4,5},{6,7},{8,9},{10,11},{12,13},{14,15},{1,0},{3,2},... | collective-permute-start | bytes 344072 | tf_op jit(solution)/shard_map/ppermute | solution.py:769
  41.3 2.3 %collective-permute-start.10 = (f32[28,8,128]{2,1,0:T(8,128)S(1)}, f32[28,8,128]{2,1,0:T(8,128)S(1)}, u32[]{:S(2)}, u32[]{:S(2)}) collective-permute-start(f32[28,8,128]{2,1,0:T(8,128)S(1)} %get-tuple-element.99), channel_id=1, source_target_pairs={{1,2},{3,4},{5,6},{7,8},{9,10},{11,12},{13,14},{2,1},{4,3},{6,5},{... | collective-permute-start | bytes 344072 | tf_op jit(solution)/shard_map/ppermute | solution.py:769
  43.7 0.5 %multiply_bitcast_fusion = f32[24]{0:T(128)} fusion(f32[8,128]{1,0:T(8,128)S(1)} %add.23), kind=kLoop, calls=%fused_computation.2 | loop fusion | flops 24 | bytes 192 | tf_op jit(solution)/shard_map/mul | solution.py:863
  44.2 1.2 %shard_map.74.refs_0_ = f32[14,8,8,128]{3,2,1,0:T(8,128)S(1)} custom-call(f32[14,12,8,128]{3,2,1,0:T(8,128)S(1)} %get-tuple-element.62.refs_1_.ext, s32[64,128]{1,0:T(8,128)S(1)} %bitcast.14, f32[14,10,8,128]{3,2,1,0:T(8,128)S(1)} %get-tuple-element.90.a_ext, f32[14,8,8,128]{3,2,1,0:T(8,128)S(1)} %get-tuple-element.91.fvx, ...), custom_call_target="tpu_custom_call" | custom-call | tf_op jit(solution)/shard_map/pallas_call | solution.py:753
  45.4 3.3 %collective-permute-done.10.refs_2_ = f32[28,8,128]{2,1,0:T(8,128)S(1)} collective-permute-done((f32[28,8,128]{2,1,0:T(8,128)S(1)}, f32[28,8,128]{2,1,0:T(8,128)S(1)}, u32[]{:S(2)}, u32[]{:S(2)}) %collective-permute-start.10) | collective-permute-done | bytes 114720 | tf_op jit(solution)/shard_map/ppermute | solution.py:769
  48.7 1.1 %shard_map.75 = (f32[14,64,128]{2,1,0:T(8,128)}, f32[14,8,8,128]{3,2,1,0:T(8,128)S(1)}) custom-call(f32[14,8,8,128]{3,2,1,0:T(8,128)S(1)} %shard_map.74.refs_0_, f32[28,8,128]{2,1,0:T(8,128)S(1)} %collective-permute-done.9.refs_1_, f32[28,8,128]{2,1,0:T(8,128)S(1)} %collective-permute-done.10.refs_2_, ...), custom_call_target="tpu_custom_call", output_to_operand_aliasing={{1}: (0, {})} | custom-call | tf_op jit(solution)/shard_map/pallas_call | solution.py:753
  (22 shorter events, 0.3 us)
Async XLA Ops:
  0.6 6.4 %copy-start = (s32[2,2,2,8,128]{4,3,2,1,0:T(8,128)S(1)}, s32[2,2,2,8,128]{4,3,2,1,0:T(8,128)}, u32[]{:S(2)}) copy-start(s32[2,2,2,8,128]{4,3,2,1,0:T(8,128)} %param.7) | copy-start | bytes 98308
  2.0 6.8 %collective-permute-start = (f32[29,8,128]{2,1,0:T(8,128)S(1)}, f32[29,8,128]{2,1,0:T(8,128)S(1)}, u32[]{:S(2)}, u32[]{:S(2)}) collective-permute-start(f32[29,8,128]{2,1,0:T(8,128)S(1)} %get-tuple-element.59), channel_id=1, source_target_pairs={{0,1},{2,3},{4,5},{6,7},{8,9},{10,11},{12,13},{14,15},{1,0},{3,2},... | collective-permute-start | bytes 356360 | tf_op jit(solution)/shard_map/ppermute | solution.py:769
  2.7 7.4 %collective-permute-start.1 = (f32[29,8,128]{2,1,0:T(8,128)S(1)}, f32[29,8,128]{2,1,0:T(8,128)S(1)}, u32[]{:S(2)}, u32[]{:S(2)}) collective-permute-start(f32[29,8,128]{2,1,0:T(8,128)S(1)} %get-tuple-element.60), channel_id=1, source_target_pairs={{1,2},{3,4},{5,6},{7,8},{9,10},{11,12},{13,14},{2,1},{4,3},{6,5},{... | collective-permute-start | bytes 356360 | tf_op jit(solution)/shard_map/ppermute | solution.py:769
  5.8 3.0 %collective-permute-start.2 = (f32[5,8,128]{2,1,0:T(8,128)S(1)}, f32[5,8,128]{2,1,0:T(8,128)S(1)}, u32[]{:S(2)}, u32[]{:S(2)}) collective-permute-start(f32[5,8,128]{2,1,0:T(8,128)S(1)} %get-tuple-element.61), channel_id=1, source_target_pairs={{0,16},{16,0},{1,17},{17,1},{2,18},{18,2},{3,19},{19,3},{4,20},{20... | collective-permute-start | bytes 61448 | tf_op jit(solution)/shard_map/ppermute | solution.py:769
  10.1 0.7 %copy-start.2 = (s32[8,128]{1,0:T(8,128)S(1)}, s32[8,128]{1,0:T(8,128)}, u32[]{:S(2)}) copy-start(s32[8,128]{1,0:T(8,128)} %refs_7_.1) | copy-start | bytes 12292
  10.2 0.7 %copy-start.3 = (f32[24]{0:T(128)S(1)}, f32[24]{0:T(128)}, u32[]{:S(2)}) copy-start(f32[24]{0:T(128)} %refs_8_.1) | copy-start | bytes 292
  12.7 7.6 %copy-start.1 = (f32[14,8,8,128]{3,2,1,0:T(8,128)S(1)}, f32[14,8,8,128]{3,2,1,0:T(8,128)}, u32[]{:S(2)}) copy-start(f32[14,8,8,128]{3,2,1,0:T(8,128)} %param.6) | copy-start | bytes 1376260
  12.7 6.2 %collective-permute-start.3 = (f32[28,8,128]{2,1,0:T(8,128)S(1)}, f32[28,8,128]{2,1,0:T(8,128)S(1)}, u32[]{:S(2)}, u32[]{:S(2)}) collective-permute-start(f32[28,8,128]{2,1,0:T(8,128)S(1)} %get-tuple-element.75), channel_id=1, source_target_pairs={{0,1},{2,3},{4,5},{6,7},{8,9},{10,11},{12,13},{14,15},{1,0},{3,2},... | collective-permute-start | bytes 344072 | tf_op jit(solution)/shard_map/ppermute | solution.py:769
  12.7 7.5 %collective-permute-start.4 = (f32[28,8,128]{2,1,0:T(8,128)S(1)}, f32[28,8,128]{2,1,0:T(8,128)S(1)}, u32[]{:S(2)}, u32[]{:S(2)}) collective-permute-start(f32[28,8,128]{2,1,0:T(8,128)S(1)} %get-tuple-element.76), channel_id=1, source_target_pairs={{1,2},{3,4},{5,6},{7,8},{9,10},{11,12},{13,14},{2,1},{4,3},{6,5},{... | collective-permute-start | bytes 344072 | tf_op jit(solution)/shard_map/ppermute | solution.py:769
  15.9 2.9 %collective-permute-start.5 = (f32[4,8,128]{2,1,0:T(8,128)S(1)}, f32[4,8,128]{2,1,0:T(8,128)S(1)}, u32[]{:S(2)}, u32[]{:S(2)}) collective-permute-start(f32[4,8,128]{2,1,0:T(8,128)S(1)} %get-tuple-element.77), channel_id=1, source_target_pairs={{0,16},{16,0},{1,17},{17,1},{2,18},{18,2},{3,19},{19,3},{4,20},{20... | collective-permute-start | bytes 49160 | tf_op jit(solution)/shard_map/ppermute | solution.py:769
  23.6 4.1 %collective-permute-start.8 = (f32[5,8,128]{2,1,0:T(8,128)S(1)}, f32[5,8,128]{2,1,0:T(8,128)S(1)}, u32[]{:S(2)}, u32[]{:S(2)}) collective-permute-start(f32[5,8,128]{2,1,0:T(8,128)S(1)} %get-tuple-element.87), channel_id=1, source_target_pairs={{0,16},{16,0},{1,17},{17,1},{2,18},{18,2},{3,19},{19,3},{4,20},{20... | collective-permute-start | bytes 61448 | tf_op jit(solution)/shard_map/ppermute | solution.py:769
  24.8 7.2 %collective-permute-start.6 = (f32[28,8,128]{2,1,0:T(8,128)S(1)}, f32[28,8,128]{2,1,0:T(8,128)S(1)}, u32[]{:S(2)}, u32[]{:S(2)}) collective-permute-start(f32[28,8,128]{2,1,0:T(8,128)S(1)} %get-tuple-element.85), channel_id=1, source_target_pairs={{0,1},{2,3},{4,5},{6,7},{8,9},{10,11},{12,13},{14,15},{1,0},{3,2},... | collective-permute-start | bytes 344072 | tf_op jit(solution)/shard_map/ppermute | solution.py:769
  25.2 7.4 %collective-permute-start.7 = (f32[28,8,128]{2,1,0:T(8,128)S(1)}, f32[28,8,128]{2,1,0:T(8,128)S(1)}, u32[]{:S(2)}, u32[]{:S(2)}) collective-permute-start(f32[28,8,128]{2,1,0:T(8,128)S(1)} %get-tuple-element.86), channel_id=1, source_target_pairs={{1,2},{3,4},{5,6},{7,8},{9,10},{11,12},{13,14},{2,1},{4,3},{6,5},{... | collective-permute-start | bytes 344072 | tf_op jit(solution)/shard_map/ppermute | solution.py:769
  27.6 1.2 %collective-permute-start.11 = (f32[8,128]{1,0:T(8,128)S(1)}, f32[8,128]{1,0:T(8,128)S(1)}, u32[]{:S(2)}, u32[]{:S(2)}) collective-permute-start(f32[8,128]{1,0:T(8,128)S(1)} %fusion), channel_id=1, source_target_pairs={{0,1},{1,0},{2,3},{3,2},{4,5},{5,4},{6,7},{7,6},{8,9},{9,8},{10,11... | collective-permute-start | bytes 12296 | tf_op jit(solution)/shard_map/ppermute | solution.py:783
  28.9 3.1 %collective-permute-start.12 = (f32[8,128]{1,0:T(8,128)S(1)}, f32[8,128]{1,0:T(8,128)S(1)}, u32[]{:S(2)}, u32[]{:S(2)}) collective-permute-start(f32[8,128]{1,0:T(8,128)S(1)} %add.20), channel_id=1, source_target_pairs={{0,2},{1,3},{2,0},{3,1},{4,6},{5,7},{6,4},{7,5},{8,10},{9,11},{10,... | collective-permute-start | bytes 12296 | tf_op jit(solution)/shard_map/ppermute | solution.py:783
  33.8 2.5 %collective-permute-start.14 = (f32[8,128]{1,0:T(8,128)S(1)}, f32[8,128]{1,0:T(8,128)S(1)}, u32[]{:S(2)}, u32[]{:S(2)}) collective-permute-start(f32[8,128]{1,0:T(8,128)S(1)} %add.21), channel_id=1, source_target_pairs={{0,4},{1,5},{2,6},{3,7},{4,0},{5,1},{6,2},{7,3},{8,12},{9,13},{10,... | collective-permute-start | bytes 12296 | tf_op jit(solution)/shard_map/ppermute | solution.py:783
  36.3 7.3 %collective-permute-start.15 = (f32[8,128]{1,0:T(8,128)S(1)}, f32[8,128]{1,0:T(8,128)S(1)}, u32[]{:S(2)}, u32[]{:S(2)}) collective-permute-start(f32[8,128]{1,0:T(8,128)S(1)} %add.22), channel_id=1, source_target_pairs={{0,8},{1,9},{2,10},{3,11},{4,12},{5,13},{6,14},{7,15},{8,0},{9,1},... | collective-permute-start | bytes 12296 | tf_op jit(solution)/shard_map/ppermute | solution.py:783
  38.6 6.7 %collective-permute-start.13 = (f32[4,8,128]{2,1,0:T(8,128)S(1)}, f32[4,8,128]{2,1,0:T(8,128)S(1)}, u32[]{:S(2)}, u32[]{:S(2)}) collective-permute-start(f32[4,8,128]{2,1,0:T(8,128)S(1)} %get-tuple-element.101), channel_id=1, source_target_pairs={{0,16},{16,0},{1,17},{17,1},{2,18},{18,2},{3,19},{19,3},{4,20},{20... | collective-permute-start | bytes 49160 | tf_op jit(solution)/shard_map/ppermute | solution.py:769
  38.9 5.3 %collective-permute-start.9 = (f32[28,8,128]{2,1,0:T(8,128)S(1)}, f32[28,8,128]{2,1,0:T(8,128)S(1)}, u32[]{:S(2)}, u32[]{:S(2)}) collective-permute-start(f32[28,8,128]{2,1,0:T(8,128)S(1)} %get-tuple-element.89), channel_id=1, source_target_pairs={{0,1},{2,3},{4,5},{6,7},{8,9},{10,11},{12,13},{14,15},{1,0},{3,2},... | collective-permute-start | bytes 344072 | tf_op jit(solution)/shard_map/ppermute | solution.py:769
  41.3 7.3 %collective-permute-start.10 = (f32[28,8,128]{2,1,0:T(8,128)S(1)}, f32[28,8,128]{2,1,0:T(8,128)S(1)}, u32[]{:S(2)}, u32[]{:S(2)}) collective-permute-start(f32[28,8,128]{2,1,0:T(8,128)S(1)} %get-tuple-element.99), channel_id=1, source_target_pairs={{1,2},{3,4},{5,6},{7,8},{9,10},{11,12},{13,14},{2,1},{4,3},{6,5},{... | collective-permute-start | bytes 344072 | tf_op jit(solution)/shard_map/ppermute | solution.py:769

commit v3 on v2

--- a/solution.py
+++ b/solution.py
@@ -201,8 +201,13 @@
 
 
 def early_kernel(step):
-    def kernel(ext, words, fvx, ux, along, fvy, vy):
+    def kernel(ext, words, *refs):
+        fvx, ux, along, fvy, vy = refs[-6:-1] if step == 0 else refs
         bits = level_bits()
+        if step == 0:
+            coef, coef_rows = refs[0], refs[-1]
+            for k in range(NCLASS):
+                coef_rows[pl.ds(k, 1), :] = jnp.full((1, LANES), coef[k], jnp.float32)
 
         def one_row(r, carry):
             for p, (lead, members) in enumerate(PHASES):
@@ -428,10 +433,10 @@
     return weight
 
 
-def drag_table(classes, coef):
+def drag_table(classes, coef_rows):
     drag = jnp.zeros(classes.shape, jnp.float32)
     for k in range(NCLASS):
-        drag = jnp.where(classes == k, coef[k], drag)
+        drag = jnp.where(classes == k, jnp.broadcast_to(coef_rows[pl.ds(k, 1), :], classes.shape), drag)
     return drag
 
 
@@ -465,7 +470,7 @@
             to_b[2 * f + j] = source[f, b_row + j]
 
 
-def pack_kernel(start_in, words_in, terrain_in, ext, edges, edge_words, to_a, to_b, to_c, start, words, terrain, sems):
+def pack_kernel(start_in, words_in, terrain_in, words, terrain, ext, edges, edge_words, to_a, to_b, to_c, start, sems):
     copies = [
         pltpu.make_async_copy(source, target, sems.at[k])
         for k, (source, target) in enumerate(((start_in, start), (words_in, words), (terrain_in, terrain)))
@@ -669,15 +674,10 @@
 
 def third_kernel(has_odd):
     def kernel(*refs):
-        (_, ext, strip, carried_ref, fvy, vy, sfv, su) = refs[:8]
-        drag_ref, low_ref, left_ref, edge_words, words = refs[8:13]
-        from_a, from_b, from_c = refs[13:16]
-        from_d = refs[16] if has_odd else None
-        outs = refs[16 + has_odd :]
-        part, to_a, to_b, to_c, a_ext, sdc, sdu, gl, gh, dvy = outs[:10]
-        incoming, edges_a = outs[10:]
+        _, carried_ref, drag_ref, from_a, from_b, from_c = refs[:6]
+        from_d = refs[6] if has_odd else None
+        part, a_ext, edges_a, incoming = refs[6 + has_odd :]
         pick = side_payloads(from_c, from_d)
-        low_words, left_words = low_ref[...], left_ref[...]
         collect(part, from_a, from_b, pick, incoming)
         zero_edges(edges_a)
         for f in range(FIELDS):
@@ -696,14 +696,20 @@
             return carry
 
         lax.fori_loop(0, ROWS, one_row, 0, unroll=4)
-        backward_strip(0, strip, edges_a, edge_words, left_words, sfv, su, sdc, sdu, to_c)
-
-        def put_ghost(row, values):
-            put_ghost_rows(values, row, to_a, to_b)
-
-        backward_faces(0, ext, words, low_words, a_ext, fvy, vy, gl, gh, dvy, put_ghost)
 
     return kernel
+
+
+def seam_kernel(a_ext, edges_a, ext, strip, fvy, vy, sfv, su, low_ref, left_ref, edge_words, words, grads, *outs):
+    to_a, to_b, to_c, sdc, sdu, gl, gh, dvy = outs
+    low_words, left_words = low_ref[...], left_ref[...]
+    backward_strip(0, strip, edges_a, edge_words, left_words, sfv, su, sdc, sdu, to_c)
+
+    def put_ghost(row, values):
+        put_ghost_rows(values, row, to_a, to_b)
+
+    backward_faces(0, ext, words, low_words, a_ext, fvy, vy, gl, gh, dvy, put_ghost)
+    to_a[2 * FIELDS] = grads[...]
 
 
 def own_kernel(ext, words, a_ext, fvx, ux, sdc, sdu, gl, gh, dvy, part):
@@ -791,13 +797,12 @@
     words = face_words.reshape(8 * ROWS, LANES)
     ints = jnp.int32
 
-    ext, edges, edge_words, *payload = call(
+    words, terrain, ext, edges, edge_words, *payload = call(
         pack_kernel,
-        [tiles(14, 12), tiles(14), tiles(dtype=ints), tiles(29), tiles(29), tiles(5)],
+        [shaped(*words.shape, dtype=ints), shaped(*terrain.shape, dtype=ints)]
+        + [tiles(14, 12), tiles(14), tiles(dtype=ints), tiles(29), tiles(29), tiles(5)],
         [
             pltpu.VMEM(start.shape, jnp.float32),
-            pltpu.VMEM(words.shape, ints),
-            pltpu.VMEM(terrain.shape, ints),
             pltpu.SemaphoreType.DMA((3,)),
         ],
         [pltpu.with_memory_space_constraint(x, pltpu.HBM) for x in (start, words, terrain)],
@@ -805,22 +810,22 @@
     )
     got = exchange(*payload)
     early = [tiles(14, 8), tiles(4, 8), tiles(14, 8), tiles(14, 9), tiles(4, 9)]
-    fvx, ux, along, fvy, vy = call(early_kernel(0), early, [], [ext, words])
+    fvx, ux, along, fvy, vy, coef_rows = call(
+        early_kernel(0), [*early, shaped(NCLASS, LANES)], [], [ext, words, drag_coef], smem=(2,)
+    )
     res = call(
         first_kernel(has_odd),
         [tiles(14, 12), tiles(14, 9), tiles(4, 9), tiles(14), tiles(14, 8), tiles(14), tiles(4)]
         + [shaped(16, LANES), shaped(16, LANES, dtype=ints), tiles(dtype=ints), tiles(dtype=ints)]
         + [tiles(14, 12), tiles(14, 12), tiles(14), tiles(28), tiles(28), tiles(4)],
         [scratch(14)],
-        [ext, fvy, vy, edges, edge_words, along, words, terrain, drag_coef, *got],
-        smem=(8,),
+        [ext, fvy, vy, edges, edge_words, along, words, terrain, coef_rows, *got],
         aliases={0: 0, 1: 1, 2: 2},
     )
     ext, fvy, vy, strip, carried_ref, sfv, su, drag_ref, class_ref, low_ref, left_ref = res[:11]
     middle, before, before_edges, *payload = res[11:]
     got = exchange(*payload)
     fvx2, ux2, along2, fvy2, vy2 = call(early_kernel(1), early, [], [middle, words])
-    back = [tiles(14, 10), tiles(14), tiles(4), tiles(14, 15), tiles(14, 15), tiles(4, 15)]
     kept = [scratch(14, 10), scratch(14), scratch(14), scratch(4), scratch(14, 15), scratch(14, 15), scratch(4, 15)]
     part, *payload = call(
         second_kernel(has_odd),
@@ -833,25 +838,28 @@
     got = exchange(*payload)
     grads = payload[2][4] + got[2][4]
     steps = [("gx", 2**k) for k in range(1, 32) if 2**k < nx] + [("gy", 2**k) for k in range(1, 32) if 2**k < ny]
-    grads = add_partner(add_partner(grads, "gy", 1), *steps[0])
-    part, to_a, to_b, to_c, *adjoints = call(
+    early_steps = len(steps) - 1
+    for axis, distance in steps[:early_steps]:
+        grads = add_partner(grads, axis, distance)
+    _, a_ext, edges_a = call(
         third_kernel(has_odd),
-        [tiles(14, 8), tiles(28), tiles(28), tiles(4), *back],
-        [scratch(14), scratch(14)],
-        [part, ext, strip, carried_ref, fvy, vy, sfv, su, drag_ref, low_ref, left_ref, edge_words, words, *got],
+        [tiles(14, 8), tiles(14, 10), tiles(14)],
+        [scratch(14)],
+        [part, carried_ref, drag_ref, *got],
         aliases={0: 0},
     )
-    a_ext, sdc, sdu, gl, gh, dvy = adjoints
-    grads, to_c = lax.optimization_barrier((grads, to_c))
+    to_a, to_b, to_c, *adjoints = call(
+        seam_kernel,
+        [tiles(29), tiles(28), tiles(4), tiles(14), tiles(4), tiles(14, 15), tiles(14, 15), tiles(4, 15)],
+        [],
+        [a_ext, edges_a, ext, strip, fvy, vy, sfv, su, low_ref, left_ref, edge_words, words, grads],
+    )
+    sdc, sdu, gl, gh, dvy = adjoints
     got = exchange(to_a, to_b, to_c)
-    half = len(steps) // 2 + 1
-    a_ext, from_a = lax.optimization_barrier((a_ext, got[0]))
-    got = (from_a, *got[1:])
-    for axis, distance in steps[1:half]:
+    grads = grads + got[0][2 * FIELDS]
+    for axis, distance in steps[early_steps:]:
         grads = add_partner(grads, axis, distance)
     (part,) = call(own_kernel, [tiles(14, 8)], [], [ext, words, a_ext, fvx, ux, sdc, sdu, gl, gh, dvy])
-    for axis, distance in steps[half:]:
-        grads = add_partner(grads, axis, distance)
     out, _ = call(
         last_kernel(has_odd),
         [shaped(FIELDS, LEV * ROWS, LANES), tiles(14, 8)],

time: 49.9 us -> 46.4 us (0.930)
  the two profiles are of different devices: /device:TPU:9 before, /device:TPU:0 now
where the time goes in v3:
time: 46.4 us; the launch traced here: 46.2 us
  starting transfers between devices  25.4 us (55%)
  Pallas kernels  12.3 us (27%)
  waiting for transfers between devices  6.51 us (14%)
  between operations  0.8 us (2%)
  local copies, waits for them, and re-layouts  0.66 us (1%)
  other arithmetic  0.53 us (1%)
    ppermute x12, starting transfers between devices, swap(): return lax.ppermute(x, axis, pairs + [(j, i) for i, j in pairs])  13.2 us
    pallas_call x9, Pallas kernels, call(): pl.pallas_call(kernel, out_shape=outs, in_specs=[pl.BlockSpec(memory_spac...  12.3 us
    ppermute x3, starting transfers between devices, add_partner(): lax.ppermute(x, axis, [(i, i ^ distance) for i in range(lax.axis_size(axi...  12.2 us
    ppermute x3, waiting for transfers between devices, add_partner(): lax.ppermute(x, axis, [(i, i ^ distance) for i in range(lax.axis_size(axi...  4.74 us
    ppermute x12, waiting for transfers between devices, swap(): return lax.ppermute(x, axis, pairs + [(j, i) for i, j in pairs])  1.77 us
  transfers between devices with their start and end apart: 15, of which 5 were waited for; matrix products, arithmetic and copies ran while one was open for 0% of the time, Pallas kernels for 11%

profile of v3, /device:TPU:0, one launch (start us, length us, event | category | flops | bytes accessed | tf_op | source)
XLA Modules:
  0.0 46.2 jit_solution(5949046481792483137)
XLA Ops:
  0.6 1.3 %shard_map.68 = (s32[64,128]{1,0:T(8,128)S(1)}, s32[8,128]{1,0:T(8,128)S(1)}, f32[14,12,8,128]{3,2,1,0:T(8,128)S(1)}, f32[14,8,128]{2,1,0:T(8,128)S(1)}, s32[8,1...) custom-call(f32[14,64,128]{2,1,0:T(8,128)} %bitcast.13, ...), custom_call_target="tpu_custom_call" | custom-call | tf_op jit(solution)/shard_map/pallas_call | solution.py:759
  2.0 0.5 %collective-permute-start = (f32[29,8,128]{2,1,0:T(8,128)S(1)}, f32[29,8,128]{2,1,0:T(8,128)S(1)}, u32[]{:S(2)}, u32[]{:S(2)}) collective-permute-start(f32[29,8,128]{2,1,0:T(8,128)S(1)} %get-tuple-element.62), channel_id=1, source_target_pairs={{0,1},{2,3},{4,5},{6,7},{8,9},{10,11},{12,13},{14,15},{1,0},{3,2},... | collective-permute-start | bytes 356360 | tf_op jit(solution)/shard_map/ppermute | solution.py:775
  2.5 0.7 %collective-permute-start.1 = (f32[29,8,128]{2,1,0:T(8,128)S(1)}, f32[29,8,128]{2,1,0:T(8,128)S(1)}, u32[]{:S(2)}, u32[]{:S(2)}) collective-permute-start(f32[29,8,128]{2,1,0:T(8,128)S(1)} %get-tuple-element.63), channel_id=1, source_target_pairs={{1,2},{3,4},{5,6},{7,8},{9,10},{11,12},{13,14},{2,1},{4,3},{6,5},{... | collective-permute-start | bytes 356360 | tf_op jit(solution)/shard_map/ppermute | solution.py:775
  3.2 2.6 %collective-permute-start.2 = (f32[5,8,128]{2,1,0:T(8,128)S(1)}, f32[5,8,128]{2,1,0:T(8,128)S(1)}, u32[]{:S(2)}, u32[]{:S(2)}) collective-permute-start(f32[5,8,128]{2,1,0:T(8,128)S(1)} %get-tuple-element.64), channel_id=1, source_target_pairs={{0,16},{16,0},{1,17},{17,1},{2,18},{18,2},{3,19},{19,3},{4,20},{20... | collective-permute-start | bytes 61448 | tf_op jit(solution)/shard_map/ppermute | solution.py:775
  5.8 0.7 %copy-done.1 = f32[24]{0:T(128)S(1)} copy-done((f32[24]{0:T(128)S(1)}, f32[24]{0:T(128)}, u32[]{:S(2)}) %copy-start.1) | copy-done | bytes 120
  6.4 1.7 %shard_map.69 = (f32[14,8,8,128]{3,2,1,0:T(8,128)S(1)}, f32[4,8,8,128]{3,2,1,0:T(8,128)S(1)}, f32[14,8,8,128]{3,2,1,0:T(8,128)S(1)}, f32[14,9,8,128]{3,2,1,0:T(8...) custom-call(f32[14,12,8,128]{3,2,1,0:T(8,128)S(1)} %get-tuple-element.53.ext.refs_0_, ...), custom_call_target="tpu_custom_call" | custom-call | tf_op jit(solution)/shard_map/pallas_call | solution.py:759
  8.2 1.3 %shard_map.70 = (f32[14,12,8,128]{3,2,1,0:T(8,128)S(1)}, f32[14,9,8,128]{3,2,1,0:T(8,128)S(1)}, f32[4,9,8,128]{3,2,1,0:T(8,128)S(1)}, f32[14,8,128]{2,1,0:T(8,12...) custom-call(f32[14,12,8,128]{3,2,1,0:T(8,128)S(1)} %get-tuple-elemen, ...), custom_call_target="tpu_custom_call", output_to_operand_aliasing={{0}: (0, {}), {1}: (1, {}), {2}: (2, {})} | custom-call | tf_op jit(solution)/shard_map/pallas_call | solution.py:759
  9.5 0.0 copy-start
  9.5 2.6 %collective-permute-start.3 = (f32[28,8,128]{2,1,0:T(8,128)S(1)}, f32[28,8,128]{2,1,0:T(8,128)S(1)}, u32[]{:S(2)}, u32[]{:S(2)}) collective-permute-start(f32[28,8,128]{2,1,0:T(8,128)S(1)} %get-tuple-element.78), channel_id=1, source_target_pairs={{0,1},{2,3},{4,5},{6,7},{8,9},{10,11},{12,13},{14,15},{1,0},{3,2},... | collective-permute-start | bytes 344072 | tf_op jit(solution)/shard_map/ppermute | solution.py:775
  12.1 0.7 %collective-permute-start.4 = (f32[28,8,128]{2,1,0:T(8,128)S(1)}, f32[28,8,128]{2,1,0:T(8,128)S(1)}, u32[]{:S(2)}, u32[]{:S(2)}) collective-permute-start(f32[28,8,128]{2,1,0:T(8,128)S(1)} %get-tuple-element.79), channel_id=1, source_target_pairs={{1,2},{3,4},{5,6},{7,8},{9,10},{11,12},{13,14},{2,1},{4,3},{6,5},{... | collective-permute-start | bytes 344072 | tf_op jit(solution)/shard_map/ppermute | solution.py:775
  12.8 1.0 %collective-permute-start.5 = (f32[4,8,128]{2,1,0:T(8,128)S(1)}, f32[4,8,128]{2,1,0:T(8,128)S(1)}, u32[]{:S(2)}, u32[]{:S(2)}) collective-permute-start(f32[4,8,128]{2,1,0:T(8,128)S(1)} %get-tuple-element.80), channel_id=1, source_target_pairs={{0,16},{16,0},{1,17},{17,1},{2,18},{18,2},{3,19},{19,3},{4,20},{20... | collective-permute-start | bytes 49160 | tf_op jit(solution)/shard_map/ppermute | solution.py:775
  13.7 1.2 %shard_map.71 = (f32[14,8,8,128]{3,2,1,0:T(8,128)S(1)}, f32[4,8,8,128]{3,2,1,0:T(8,128)S(1)}, f32[14,8,8,128]{3,2,1,0:T(8,128)S(1)}, f32[14,9,8,128]{3,2,1,0:T(8,128)S(1)}, f32[4,9,8,128]{3,2,1,0:T(8,128)S(1)}) custom-call(f32[14,12,8,128]{3,2,1,0:T(8,128)S(1)} %get-tuple-element.66.ext.refs_0_, s32[64,128]{1,0:T(8,128)S(1)} %get-tuple-element.54.words.refs_6_.refs_9_), custom_call_target="tpu_custom_call" | custom-call | tf_op jit(solution)/shard_map/pallas_call | solution.py:759
  14.9 1.7 %collective-permute-done.5.refs_17_ = f32[4,8,128]{2,1,0:T(8,128)S(1)} collective-permute-done((f32[4,8,128]{2,1,0:T(8,128)S(1)}, f32[4,8,128]{2,1,0:T(8,128)S(1)}, u32[]{:S(2)}, u32[]{:S(2)}) %collective-permute-start.5) | collective-permute-done | bytes 16416 | tf_op jit(solution)/shard_map/ppermute | solution.py:775
  16.6 3.4 %shard_map.72 = (f32[14,12,8,128]{3,2,1,0:T(8,128)S(1)}, f32[14,12,8,128]{3,2,1,0:T(8,128)S(1)}, f32[14,9,8,128]{3,2,1,0:T(8,128)S(1)}, f32[4,9,8,128]{3,2,1,0:T...) custom-call(f32[14,12,8,128]{3,2,1,0:T(8,128)S(1)} %get-tuple-elemen, ...), custom_call_target="tpu_custom_call", output_to_operand_aliasing={{0}: (0, {}), {1}: (1, {}), {2}: (2, {}), {3}: (3, {})} | custom-call | tf_op jit(solution)/shard_map/pallas_call | solution.py:759
  19.9 0.9 %collective-permute-start.8 = (f32[5,8,128]{2,1,0:T(8,128)S(1)}, f32[5,8,128]{2,1,0:T(8,128)S(1)}, u32[]{:S(2)}, u32[]{:S(2)}) collective-permute-start(f32[5,8,128]{2,1,0:T(8,128)S(1)} %get-tuple-element.85), channel_id=1, source_target_pairs={{0,16},{16,0},{1,17},{17,1},{2,18},{18,2},{3,19},{19,3},{4,20},{20... | collective-permute-start | bytes 61448 | tf_op jit(solution)/shard_map/ppermute | solution.py:775
  20.8 2.3 %collective-permute-start.6 = (f32[28,8,128]{2,1,0:T(8,128)S(1)}, f32[28,8,128]{2,1,0:T(8,128)S(1)}, u32[]{:S(2)}, u32[]{:S(2)}) collective-permute-start(f32[28,8,128]{2,1,0:T(8,128)S(1)} %get-tuple-element.83), channel_id=1, source_target_pairs={{0,1},{2,3},{4,5},{6,7},{8,9},{10,11},{12,13},{14,15},{1,0},{3,2},... | collective-permute-start | bytes 344072 | tf_op jit(solution)/shard_map/ppermute | solution.py:775
  23.1 0.7 %collective-permute-start.7 = (f32[28,8,128]{2,1,0:T(8,128)S(1)}, f32[28,8,128]{2,1,0:T(8,128)S(1)}, u32[]{:S(2)}, u32[]{:S(2)}) collective-permute-start(f32[28,8,128]{2,1,0:T(8,128)S(1)} %get-tuple-element.84), channel_id=1, source_target_pairs={{1,2},{3,4},{5,6},{7,8},{9,10},{11,12},{13,14},{2,1},{4,3},{6,5},{... | collective-permute-start | bytes 344072 | tf_op jit(solution)/shard_map/ppermute | solution.py:775
  23.8 3.8 %collective-permute-start.9 = (f32[8,128]{1,0:T(8,128)S(1)}, f32[8,128]{1,0:T(8,128)S(1)}, u32[]{:S(2)}, u32[]{:S(2)}) collective-permute-start(f32[8,128]{1,0:T(8,128)S(1)} %fusion.1), channel_id=1, source_target_pairs={{0,2},{1,3},{2,0},{3,1},{4,6},{5,7},{6,4},{7,5},{8,10},{9,11},{10,... | collective-permute-start | bytes 12296 | tf_op jit(solution)/shard_map/ppermute | solution.py:789
  27.6 2.7 %collective-permute-done.9 = f32[8,128]{1,0:T(8,128)S(1)} collective-permute-done((f32[8,128]{1,0:T(8,128)S(1)}, f32[8,128]{1,0:T(8,128)S(1)}, u32[]{:S(2)}, u32[]{:S(2)}) %collective-permute-start.9) | collective-permute-done | bytes 4128 | tf_op jit(solution)/shard_map/ppermute | solution.py:789
  30.3 4.1 %collective-permute-start.10 = (f32[8,128]{1,0:T(8,128)S(1)}, f32[8,128]{1,0:T(8,128)S(1)}, u32[]{:S(2)}, u32[]{:S(2)}) collective-permute-start(f32[8,128]{1,0:T(8,128)S(1)} %add.20), channel_id=1, source_target_pairs={{0,4},{1,5},{2,6},{3,7},{4,0},{5,1},{6,2},{7,3},{8,12},{9,13},{10,... | collective-permute-start | bytes 12296 | tf_op jit(solution)/shard_map/ppermute | solution.py:789
  34.4 1.6 %collective-permute-done.10 = f32[8,128]{1,0:T(8,128)S(1)} collective-permute-done((f32[8,128]{1,0:T(8,128)S(1)}, f32[8,128]{1,0:T(8,128)S(1)}, u32[]{:S(2)}, u32[]{:S(2)}) %collective-permute-start.10) | collective-permute-done | bytes 4128 | tf_op jit(solution)/shard_map/ppermute | solution.py:789
  36.0 0.7 %shard_map.73 = (f32[14,8,8,128]{3,2,1,0:T(8,128)S(1)}, f32[14,10,8,128]{3,2,1,0:T(8,128)S(1)}, f32[14,8,128]{2,1,0:T(8,128)S(1)}) custom-call(f32[14,8,8,128]{3,2,1,0:T(8,128)S(1)} %get-tuple-element.81.refs_0_, f32[14,8,8,128]{3,2,1,0:T(8,128)S(1)} %get-tuple-element.82.refs_1_, ...), custom_call_target="tpu_custom_call", output_to_operand_aliasing={{0}: (0, {})} | custom-call | tf_op jit(solution)/shard_map/pallas_call | solution.py:759
  36.7 0.5 %shard_map.74 = (f32[29,8,128]{2,1,0:T(8,128)S(1)}, f32[28,8,128]{2,1,0:T(8,128)S(1)}, f32[4,8,128]{2,1,0:T(8,128)S(1)}, f32[14,8,128]{2,1,0:T(8,128)S(1)}, f32[...) custom-call(f32[14,10,8,128]{3,2,1,0:T(8,128)S(1)} %get-tuple-elemen, ...), custom_call_target="tpu_custom_call" | custom-call | tf_op jit(solution)/shard_map/pallas_call | solution.py:759
  37.2 0.1 collective-permute-start.11
  37.3 0.6 %collective-permute-start.13 = (f32[4,8,128]{2,1,0:T(8,128)S(1)}, f32[4,8,128]{2,1,0:T(8,128)S(1)}, u32[]{:S(2)}, u32[]{:S(2)}) collective-permute-start(f32[4,8,128]{2,1,0:T(8,128)S(1)} %get-tuple-element.102), channel_id=1, source_target_pairs={{0,16},{16,0},{1,17},{17,1},{2,18},{18,2},{3,19},{19,3},{4,20},{20... | collective-permute-start | bytes 49160 | tf_op jit(solution)/shard_map/ppermute | solution.py:775
  37.9 0.7 %collective-permute-start.12 = (f32[28,8,128]{2,1,0:T(8,128)S(1)}, f32[28,8,128]{2,1,0:T(8,128)S(1)}, u32[]{:S(2)}, u32[]{:S(2)}) collective-permute-start(f32[28,8,128]{2,1,0:T(8,128)S(1)} %get-tuple-element.101), channel_id=1, source_target_pairs={{1,2},{3,4},{5,6},{7,8},{9,10},{11,12},{13,14},{2,1},{4,3},{6,5},{... | collective-permute-start | bytes 344072 | tf_op jit(solution)/shard_map/ppermute | solution.py:775
  38.5 0.1 collective-permute-done.11.refs_1_
  38.6 4.3 %collective-permute-start.14 = (f32[8,128]{1,0:T(8,128)S(1)}, f32[8,128]{1,0:T(8,128)S(1)}, u32[]{:S(2)}, u32[]{:S(2)}) collective-permute-start(f32[8,128]{1,0:T(8,128)S(1)} %fusion), channel_id=1, source_target_pairs={{0,8},{1,9},{2,10},{3,11},{4,12},{5,13},{6,14},{7,15},{8,0},{9,1},... | collective-permute-start | bytes 12296 | tf_op jit(solution)/shard_map/ppermute | solution.py:789
  42.9 1.2 %shard_map.75.refs_0_ = f32[14,8,8,128]{3,2,1,0:T(8,128)S(1)} custom-call(f32[14,12,8,128]{3,2,1,0:T(8,128)S(1)} %get-tuple-element.65.ext, s32[64,128]{1,0:T(8,128)S(1)} %get-tuple-element.54.words.refs_6_.refs_9_, f32[14,10,8,128]{3,2,1,0:T(8,128)S(1)} %get-tuple-element.86.a_ext, f32[14,8,8,128]{3,2,1,0:T(8,128)S(1)} %get-tuple-element.87.fvx, ...), custom_call_target="tpu_custom_call" | custom-call | tf_op jit(solution)/shard_map/pallas_call | solution.py:759
  44.1 1.1 %shard_map.76 = (f32[14,64,128]{2,1,0:T(8,128)}, f32[14,8,8,128]{3,2,1,0:T(8,128)S(1)}) custom-call(f32[14,8,8,128]{3,2,1,0:T(8,128)S(1)} %shard_map.75.refs_0_, f32[29,8,128]{2,1,0:T(8,128)S(1)} %collective-permute-done.11.refs_1_, f32[28,8,128]{2,1,0:T(8,128)S(1)} %collective-permute-done.12.refs_2_, ...), custom_call_target="tpu_custom_call", output_to_operand_aliasing={{1}: (0, {})} | custom-call | tf_op jit(solution)/shard_map/pallas_call | solution.py:759
  45.2 0.5 collective-permute-done.14
  45.7 0.5 %multiply_bitcast_fusion = f32[24]{0:T(128)} fusion(f32[8,128]{1,0:T(8,128)S(1)} %add.23), kind=kLoop, calls=%fused_computation.4 | loop fusion | flops 24 | bytes 192 | tf_op jit(solution)/shard_map/mul | solution.py:871
  (17 shorter events, 0.0 us)
Async XLA Ops:
  2.0 6.2 %collective-permute-start = (f32[29,8,128]{2,1,0:T(8,128)S(1)}, f32[29,8,128]{2,1,0:T(8,128)S(1)}, u32[]{:S(2)}, u32[]{:S(2)}) collective-permute-start(f32[29,8,128]{2,1,0:T(8,128)S(1)} %get-tuple-element.62), channel_id=1, source_target_pairs={{0,1},{2,3},{4,5},{6,7},{8,9},{10,11},{12,13},{14,15},{1,0},{3,2},... | collective-permute-start | bytes 356360 | tf_op jit(solution)/shard_map/ppermute | solution.py:775
  2.5 5.7 %collective-permute-start.1 = (f32[29,8,128]{2,1,0:T(8,128)S(1)}, f32[29,8,128]{2,1,0:T(8,128)S(1)}, u32[]{:S(2)}, u32[]{:S(2)}) collective-permute-start(f32[29,8,128]{2,1,0:T(8,128)S(1)} %get-tuple-element.63), channel_id=1, source_target_pairs={{1,2},{3,4},{5,6},{7,8},{9,10},{11,12},{13,14},{2,1},{4,3},{6,5},{... | collective-permute-start | bytes 356360 | tf_op jit(solution)/shard_map/ppermute | solution.py:775
  3.2 5.0 %collective-permute-start.2 = (f32[5,8,128]{2,1,0:T(8,128)S(1)}, f32[5,8,128]{2,1,0:T(8,128)S(1)}, u32[]{:S(2)}, u32[]{:S(2)}) collective-permute-start(f32[5,8,128]{2,1,0:T(8,128)S(1)} %get-tuple-element.64), channel_id=1, source_target_pairs={{0,16},{16,0},{1,17},{17,1},{2,18},{18,2},{3,19},{19,3},{4,20},{20... | collective-permute-start | bytes 61448 | tf_op jit(solution)/shard_map/ppermute | solution.py:775
  5.8 0.7 %copy-start.1 = (f32[24]{0:T(128)S(1)}, f32[24]{0:T(128)}, u32[]{:S(2)}) copy-start(f32[24]{0:T(128)} %refs_0_.1) | copy-start | bytes 292
  9.5 7.1 %copy-start = (f32[14,8,8,128]{3,2,1,0:T(8,128)S(1)}, f32[14,8,8,128]{3,2,1,0:T(8,128)}, u32[]{:S(2)}) copy-start(f32[14,8,8,128]{3,2,1,0:T(8,128)} %param.6) | copy-start | bytes 1376260
  9.5 7.1 %collective-permute-start.3 = (f32[28,8,128]{2,1,0:T(8,128)S(1)}, f32[28,8,128]{2,1,0:T(8,128)S(1)}, u32[]{:S(2)}, u32[]{:S(2)}) collective-permute-start(f32[28,8,128]{2,1,0:T(8,128)S(1)} %get-tuple-element.78), channel_id=1, source_target_pairs={{0,1},{2,3},{4,5},{6,7},{8,9},{10,11},{12,13},{14,15},{1,0},{3,2},... | collective-permute-start | bytes 344072 | tf_op jit(solution)/shard_map/ppermute | solution.py:775
  12.1 4.5 %collective-permute-start.4 = (f32[28,8,128]{2,1,0:T(8,128)S(1)}, f32[28,8,128]{2,1,0:T(8,128)S(1)}, u32[]{:S(2)}, u32[]{:S(2)}) collective-permute-start(f32[28,8,128]{2,1,0:T(8,128)S(1)} %get-tuple-element.79), channel_id=1, source_target_pairs={{1,2},{3,4},{5,6},{7,8},{9,10},{11,12},{13,14},{2,1},{4,3},{6,5},{... | collective-permute-start | bytes 344072 | tf_op jit(solution)/shard_map/ppermute | solution.py:775
  12.8 3.8 %collective-permute-start.5 = (f32[4,8,128]{2,1,0:T(8,128)S(1)}, f32[4,8,128]{2,1,0:T(8,128)S(1)}, u32[]{:S(2)}, u32[]{:S(2)}) collective-permute-start(f32[4,8,128]{2,1,0:T(8,128)S(1)} %get-tuple-element.80), channel_id=1, source_target_pairs={{0,16},{16,0},{1,17},{17,1},{2,18},{18,2},{3,19},{19,3},{4,20},{20... | collective-permute-start | bytes 49160 | tf_op jit(solution)/shard_map/ppermute | solution.py:775
  19.9 3.9 %collective-permute-start.8 = (f32[5,8,128]{2,1,0:T(8,128)S(1)}, f32[5,8,128]{2,1,0:T(8,128)S(1)}, u32[]{:S(2)}, u32[]{:S(2)}) collective-permute-start(f32[5,8,128]{2,1,0:T(8,128)S(1)} %get-tuple-element.85), channel_id=1, source_target_pairs={{0,16},{16,0},{1,17},{17,1},{2,18},{18,2},{3,19},{19,3},{4,20},{20... | collective-permute-start | bytes 61448 | tf_op jit(solution)/shard_map/ppermute | solution.py:775
  20.8 15.2 %collective-permute-start.6 = (f32[28,8,128]{2,1,0:T(8,128)S(1)}, f32[28,8,128]{2,1,0:T(8,128)S(1)}, u32[]{:S(2)}, u32[]{:S(2)}) collective-permute-start(f32[28,8,128]{2,1,0:T(8,128)S(1)} %get-tuple-element.83), channel_id=1, source_target_pairs={{0,1},{2,3},{4,5},{6,7},{8,9},{10,11},{12,13},{14,15},{1,0},{3,2},... | collective-permute-start | bytes 344072 | tf_op jit(solution)/shard_map/ppermute | solution.py:775
  23.1 12.9 %collective-permute-start.7 = (f32[28,8,128]{2,1,0:T(8,128)S(1)}, f32[28,8,128]{2,1,0:T(8,128)S(1)}, u32[]{:S(2)}, u32[]{:S(2)}) collective-permute-start(f32[28,8,128]{2,1,0:T(8,128)S(1)} %get-tuple-element.84), channel_id=1, source_target_pairs={{1,2},{3,4},{5,6},{7,8},{9,10},{11,12},{13,14},{2,1},{4,3},{6,5},{... | collective-permute-start | bytes 344072 | tf_op jit(solution)/shard_map/ppermute | solution.py:775
  23.8 6.5 %collective-permute-start.9 = (f32[8,128]{1,0:T(8,128)S(1)}, f32[8,128]{1,0:T(8,128)S(1)}, u32[]{:S(2)}, u32[]{:S(2)}) collective-permute-start(f32[8,128]{1,0:T(8,128)S(1)} %fusion.1), channel_id=1, source_target_pairs={{0,2},{1,3},{2,0},{3,1},{4,6},{5,7},{6,4},{7,5},{8,10},{9,11},{10,... | collective-permute-start | bytes 12296 | tf_op jit(solution)/shard_map/ppermute | solution.py:789
  30.3 5.7 %collective-permute-start.10 = (f32[8,128]{1,0:T(8,128)S(1)}, f32[8,128]{1,0:T(8,128)S(1)}, u32[]{:S(2)}, u32[]{:S(2)}) collective-permute-start(f32[8,128]{1,0:T(8,128)S(1)} %add.20), channel_id=1, source_target_pairs={{0,4},{1,5},{2,6},{3,7},{4,0},{5,1},{6,2},{7,3},{8,12},{9,13},{10,... | collective-permute-start | bytes 12296 | tf_op jit(solution)/shard_map/ppermute | solution.py:789
  37.2 1.4 %collective-permute-start.11 = (f32[29,8,128]{2,1,0:T(8,128)S(1)}, f32[29,8,128]{2,1,0:T(8,128)S(1)}, u32[]{:S(2)}, u32[]{:S(2)}) collective-permute-start(f32[29,8,128]{2,1,0:T(8,128)S(1)} %get-tuple-element.100), channel_id=1, source_target_pairs={{0,1},{2,3},{4,5},{6,7},{8,9},{10,11},{12,13},{14,15},{1,0},{3,2},... | collective-permute-start | bytes 356360 | tf_op jit(solution)/shard_map/ppermute | solution.py:775
  37.3 6.8 %collective-permute-start.13 = (f32[4,8,128]{2,1,0:T(8,128)S(1)}, f32[4,8,128]{2,1,0:T(8,128)S(1)}, u32[]{:S(2)}, u32[]{:S(2)}) collective-permute-start(f32[4,8,128]{2,1,0:T(8,128)S(1)} %get-tuple-element.102), channel_id=1, source_target_pairs={{0,16},{16,0},{1,17},{17,1},{2,18},{18,2},{3,19},{19,3},{4,20},{20... | collective-permute-start | bytes 49160 | tf_op jit(solution)/shard_map/ppermute | solution.py:775
  37.9 6.3 %collective-permute-start.12 = (f32[28,8,128]{2,1,0:T(8,128)S(1)}, f32[28,8,128]{2,1,0:T(8,128)S(1)}, u32[]{:S(2)}, u32[]{:S(2)}) collective-permute-start(f32[28,8,128]{2,1,0:T(8,128)S(1)} %get-tuple-element.101), channel_id=1, source_target_pairs={{1,2},{3,4},{5,6},{7,8},{9,10},{11,12},{13,14},{2,1},{4,3},{6,5},{... | collective-permute-start | bytes 344072 | tf_op jit(solution)/shard_map/ppermute | solution.py:775
  38.6 7.0 %collective-permute-start.14 = (f32[8,128]{1,0:T(8,128)S(1)}, f32[8,128]{1,0:T(8,128)S(1)}, u32[]{:S(2)}, u32[]{:S(2)}) collective-permute-start(f32[8,128]{1,0:T(8,128)S(1)} %fusion), channel_id=1, source_target_pairs={{0,8},{1,9},{2,10},{3,11},{4,12},{5,13},{6,14},{7,15},{8,0},{9,1},... | collective-permute-start | bytes 12296 | tf_op jit(solution)/shard_map/ppermute | solution.py:789

commit v4 on v3

--- a/solution.py
+++ b/solution.py
@@ -700,7 +700,8 @@
     return kernel
 
 
-def seam_kernel(a_ext, edges_a, ext, strip, fvy, vy, sfv, su, low_ref, left_ref, edge_words, words, grads, *outs):
+def seam_kernel(a_ext, edges_a, ext, strip, fvy, vy, sfv, su, *refs):
+    low_ref, left_ref, edge_words, words, grads, arriving, *outs = refs
     to_a, to_b, to_c, sdc, sdu, gl, gh, dvy = outs
     low_words, left_words = low_ref[...], left_ref[...]
     backward_strip(0, strip, edges_a, edge_words, left_words, sfv, su, sdc, sdu, to_c)
@@ -709,7 +710,7 @@
         put_ghost_rows(values, row, to_a, to_b)
 
     backward_faces(0, ext, words, low_words, a_ext, fvy, vy, gl, gh, dvy, put_ghost)
-    to_a[2 * FIELDS] = grads[...]
+    to_a[2 * FIELDS] = grads[...] + arriving[...]
 
 
 def own_kernel(ext, words, a_ext, fvx, ux, sdc, sdu, gl, gh, dvy, part):
@@ -785,8 +786,12 @@
     return (from_a, from_b, from_c) + (() if from_d is None else (from_d,))
 
 
+def from_partner(x, axis, distance):
+    return lax.ppermute(x, axis, [(i, i ^ distance) for i in range(lax.axis_size(axis))])
+
+
 def add_partner(x, axis, distance):
-    return x + lax.ppermute(x, axis, [(i, i ^ distance) for i in range(lax.axis_size(axis))])
+    return x + from_partner(x, axis, distance)
 
 
 def body(start_state, final_adjoint, face_words, terrain, drag_coef):
@@ -838,9 +843,11 @@
     got = exchange(*payload)
     grads = payload[2][4] + got[2][4]
     steps = [("gx", 2**k) for k in range(1, 32) if 2**k < nx] + [("gy", 2**k) for k in range(1, 32) if 2**k < ny]
-    early_steps = len(steps) - 1
-    for axis, distance in steps[:early_steps]:
+    steps = steps[::-1]
+    early_steps = 1
+    for axis, distance in steps[: early_steps - 1]:
         grads = add_partner(grads, axis, distance)
+    arriving = from_partner(grads, *steps[early_steps - 1])
     _, a_ext, edges_a = call(
         third_kernel(has_odd),
         [tiles(14, 8), tiles(14, 10), tiles(14)],
@@ -852,11 +859,11 @@
         seam_kernel,
         [tiles(29), tiles(28), tiles(4), tiles(14), tiles(4), tiles(14, 15), tiles(14, 15), tiles(4, 15)],
         [],
-        [a_ext, edges_a, ext, strip, fvy, vy, sfv, su, low_ref, left_ref, edge_words, words, grads],
+        [a_ext, edges_a, ext, strip, fvy, vy, sfv, su, low_ref, left_ref, edge_words, words, grads, arriving],
     )
     sdc, sdu, gl, gh, dvy = adjoints
     got = exchange(to_a, to_b, to_c)
-    grads = grads + got[0][2 * FIELDS]
+    grads = to_a[2 * FIELDS] + got[0][2 * FIELDS]
     for axis, distance in steps[early_steps:]:
         grads = add_partner(grads, axis, distance)
     (part,) = call(own_kernel, [tiles(14, 8)], [], [ext, words, a_ext, fvx, ux, sdc, sdu, gl, gh, dvy])

time: 46.4 us -> 45.1 us (0.972)
  starting transfers between devices: 25.4 us -> 23 us
  waiting for transfers between devices: 6.51 us -> 7.64 us
    ppermute x3, starting transfers between devices: 12.2 us -> 9.8 us  [from_partner(): lax.ppermute(x, axis, [(i, i ^ distance) for i in range(lax.axis_size(axi...]
    ppermute x3, waiting for transfers between devices: 4.74 us -> 5.87 us  [from_partner(): lax.ppermute(x, axis, [(i, i ^ distance) for i in range(lax.axis_size(axi...]
  transfers between devices with their start and end apart: 15 -> 15, of which waited for: 5 -> 5; matrix products, arithmetic and copies ran while one was open for 0% -> 0% of each run, Pallas kernels for 11% -> 13%
where the time goes in v4:
time: 45.1 us; the launch traced here: 44.9 us
  starting transfers between devices  23 us (51%)
  Pallas kernels  12.3 us (27%)
  waiting for transfers between devices  7.64 us (17%)
  between operations  0.8 us (2%)
  local copies, waits for them, and re-layouts  0.66 us (1%)
  other arithmetic  0.53 us (1%)
    ppermute x12, starting transfers between devices, swap(): return lax.ppermute(x, axis, pairs + [(j, i) for i, j in pairs])  13.2 us
    pallas_call x9, Pallas kernels, call(): pl.pallas_call(kernel, out_shape=outs, in_specs=[pl.BlockSpec(memory_spac...  12.3 us
    ppermute x3, starting transfers between devices, from_partner(): lax.ppermute(x, axis, [(i, i ^ distance) for i in range(lax.axis_size(axi...  9.8 us
    ppermute x3, waiting for transfers between devices, from_partner(): lax.ppermute(x, axis, [(i, i ^ distance) for i in range(lax.axis_size(axi...  5.87 us
    ppermute x12, waiting for transfers between devices, swap(): return lax.ppermute(x, axis, pairs + [(j, i) for i, j in pairs])  1.77 us
  transfers between devices with their start and end apart: 15, of which 5 were waited for; matrix products, arithmetic and copies ran while one was open for 0% of the time, Pallas kernels for 13%

profile of v4, /device:TPU:0, one launch (start us, length us, event | category | flops | bytes accessed | tf_op | source)
XLA Modules:
  0.0 44.9 jit_solution(14226658187109843587)
XLA Ops:
  0.6 1.3 %shard_map.68 = (s32[64,128]{1,0:T(8,128)S(1)}, s32[8,128]{1,0:T(8,128)S(1)}, f32[14,12,8,128]{3,2,1,0:T(8,128)S(1)}, f32[14,8,128]{2,1,0:T(8,128)S(1)}, s32[8,1...) custom-call(f32[14,64,128]{2,1,0:T(8,128)} %bitcast.11, ...), custom_call_target="tpu_custom_call" | custom-call | tf_op jit(solution)/shard_map/pallas_call | solution.py:760
  2.0 0.5 %collective-permute-start = (f32[29,8,128]{2,1,0:T(8,128)S(1)}, f32[29,8,128]{2,1,0:T(8,128)S(1)}, u32[]{:S(2)}, u32[]{:S(2)}) collective-permute-start(f32[29,8,128]{2,1,0:T(8,128)S(1)} %get-tuple-element.62), channel_id=1, source_target_pairs={{0,1},{2,3},{4,5},{6,7},{8,9},{10,11},{12,13},{14,15},{1,0},{3,2},... | collective-permute-start | bytes 356360 | tf_op jit(solution)/shard_map/ppermute | solution.py:776
  2.5 0.7 %collective-permute-start.1 = (f32[29,8,128]{2,1,0:T(8,128)S(1)}, f32[29,8,128]{2,1,0:T(8,128)S(1)}, u32[]{:S(2)}, u32[]{:S(2)}) collective-permute-start(f32[29,8,128]{2,1,0:T(8,128)S(1)} %get-tuple-element.63), channel_id=1, source_target_pairs={{1,2},{3,4},{5,6},{7,8},{9,10},{11,12},{13,14},{2,1},{4,3},{6,5},{... | collective-permute-start | bytes 356360 | tf_op jit(solution)/shard_map/ppermute | solution.py:776
  3.2 2.6 %collective-permute-start.2 = (f32[5,8,128]{2,1,0:T(8,128)S(1)}, f32[5,8,128]{2,1,0:T(8,128)S(1)}, u32[]{:S(2)}, u32[]{:S(2)}) collective-permute-start(f32[5,8,128]{2,1,0:T(8,128)S(1)} %get-tuple-element.64), channel_id=1, source_target_pairs={{0,16},{16,0},{1,17},{17,1},{2,18},{18,2},{3,19},{19,3},{4,20},{20... | collective-permute-start | bytes 61448 | tf_op jit(solution)/shard_map/ppermute | solution.py:776
  5.8 0.7 %copy-done.1 = f32[24]{0:T(128)S(1)} copy-done((f32[24]{0:T(128)S(1)}, f32[24]{0:T(128)}, u32[]{:S(2)}) %copy-start.1) | copy-done | bytes 120
  6.4 1.7 %shard_map.69 = (f32[14,8,8,128]{3,2,1,0:T(8,128)S(1)}, f32[4,8,8,128]{3,2,1,0:T(8,128)S(1)}, f32[14,8,8,128]{3,2,1,0:T(8,128)S(1)}, f32[14,9,8,128]{3,2,1,0:T(8...) custom-call(f32[14,12,8,128]{3,2,1,0:T(8,128)S(1)} %get-tuple-element.53.ext.refs_0_, ...), custom_call_target="tpu_custom_call" | custom-call | tf_op jit(solution)/shard_map/pallas_call | solution.py:760
  8.2 1.3 %shard_map.70 = (f32[14,12,8,128]{3,2,1,0:T(8,128)S(1)}, f32[14,9,8,128]{3,2,1,0:T(8,128)S(1)}, f32[4,9,8,128]{3,2,1,0:T(8,128)S(1)}, f32[14,8,128]{2,1,0:T(8,12...) custom-call(f32[14,12,8,128]{3,2,1,0:T(8,128)S(1)} %get-tuple-elemen, ...), custom_call_target="tpu_custom_call", output_to_operand_aliasing={{0}: (0, {}), {1}: (1, {}), {2}: (2, {})} | custom-call | tf_op jit(solution)/shard_map/pallas_call | solution.py:760
  9.5 0.0 copy-start
  9.5 2.6 %collective-permute-start.3 = (f32[28,8,128]{2,1,0:T(8,128)S(1)}, f32[28,8,128]{2,1,0:T(8,128)S(1)}, u32[]{:S(2)}, u32[]{:S(2)}) collective-permute-start(f32[28,8,128]{2,1,0:T(8,128)S(1)} %get-tuple-element.78), channel_id=1, source_target_pairs={{0,1},{2,3},{4,5},{6,7},{8,9},{10,11},{12,13},{14,15},{1,0},{3,2},... | collective-permute-start | bytes 344072 | tf_op jit(solution)/shard_map/ppermute | solution.py:776
  12.1 0.7 %collective-permute-start.4 = (f32[28,8,128]{2,1,0:T(8,128)S(1)}, f32[28,8,128]{2,1,0:T(8,128)S(1)}, u32[]{:S(2)}, u32[]{:S(2)}) collective-permute-start(f32[28,8,128]{2,1,0:T(8,128)S(1)} %get-tuple-element.79), channel_id=1, source_target_pairs={{1,2},{3,4},{5,6},{7,8},{9,10},{11,12},{13,14},{2,1},{4,3},{6,5},{... | collective-permute-start | bytes 344072 | tf_op jit(solution)/shard_map/ppermute | solution.py:776
  12.8 1.0 %collective-permute-start.5 = (f32[4,8,128]{2,1,0:T(8,128)S(1)}, f32[4,8,128]{2,1,0:T(8,128)S(1)}, u32[]{:S(2)}, u32[]{:S(2)}) collective-permute-start(f32[4,8,128]{2,1,0:T(8,128)S(1)} %get-tuple-element.80), channel_id=1, source_target_pairs={{0,16},{16,0},{1,17},{17,1},{2,18},{18,2},{3,19},{19,3},{4,20},{20... | collective-permute-start | bytes 49160 | tf_op jit(solution)/shard_map/ppermute | solution.py:776
  13.7 1.2 %shard_map.71 = (f32[14,8,8,128]{3,2,1,0:T(8,128)S(1)}, f32[4,8,8,128]{3,2,1,0:T(8,128)S(1)}, f32[14,8,8,128]{3,2,1,0:T(8,128)S(1)}, f32[14,9,8,128]{3,2,1,0:T(8,128)S(1)}, f32[4,9,8,128]{3,2,1,0:T(8,128)S(1)}) custom-call(f32[14,12,8,128]{3,2,1,0:T(8,128)S(1)} %get-tuple-element.66.ext.refs_0_, s32[64,128]{1,0:T(8,128)S(1)} %get-tuple-element.54.words.refs_6_.refs_9_.refs_3_), custom_call_target="tpu_custom_call" | custom-call | tf_op jit(solution)/shard_map/pallas_call | solution.py:760
  14.9 1.7 %collective-permute-done.5.refs_17_ = f32[4,8,128]{2,1,0:T(8,128)S(1)} collective-permute-done((f32[4,8,128]{2,1,0:T(8,128)S(1)}, f32[4,8,128]{2,1,0:T(8,128)S(1)}, u32[]{:S(2)}, u32[]{:S(2)}) %collective-permute-start.5) | collective-permute-done | bytes 16416 | tf_op jit(solution)/shard_map/ppermute | solution.py:776
  16.6 3.4 %shard_map.72 = (f32[14,12,8,128]{3,2,1,0:T(8,128)S(1)}, f32[14,12,8,128]{3,2,1,0:T(8,128)S(1)}, f32[14,9,8,128]{3,2,1,0:T(8,128)S(1)}, f32[4,9,8,128]{3,2,1,0:T...) custom-call(f32[14,12,8,128]{3,2,1,0:T(8,128)S(1)} %get-tuple-elemen, ...), custom_call_target="tpu_custom_call", output_to_operand_aliasing={{0}: (0, {}), {1}: (1, {}), {2}: (2, {}), {3}: (3, {})} | custom-call | tf_op jit(solution)/shard_map/pallas_call | solution.py:760
  19.9 0.9 %collective-permute-start.8 = (f32[5,8,128]{2,1,0:T(8,128)S(1)}, f32[5,8,128]{2,1,0:T(8,128)S(1)}, u32[]{:S(2)}, u32[]{:S(2)}) collective-permute-start(f32[5,8,128]{2,1,0:T(8,128)S(1)} %get-tuple-element.85), channel_id=1, source_target_pairs={{0,16},{16,0},{1,17},{17,1},{2,18},{18,2},{3,19},{19,3},{4,20},{20... | collective-permute-start | bytes 61448 | tf_op jit(solution)/shard_map/ppermute | solution.py:776
  20.8 2.3 %collective-permute-start.6 = (f32[28,8,128]{2,1,0:T(8,128)S(1)}, f32[28,8,128]{2,1,0:T(8,128)S(1)}, u32[]{:S(2)}, u32[]{:S(2)}) collective-permute-start(f32[28,8,128]{2,1,0:T(8,128)S(1)} %get-tuple-element.83), channel_id=1, source_target_pairs={{0,1},{2,3},{4,5},{6,7},{8,9},{10,11},{12,13},{14,15},{1,0},{3,2},... | collective-permute-start | bytes 344072 | tf_op jit(solution)/shard_map/ppermute | solution.py:776
  23.1 0.7 %collective-permute-start.7 = (f32[28,8,128]{2,1,0:T(8,128)S(1)}, f32[28,8,128]{2,1,0:T(8,128)S(1)}, u32[]{:S(2)}, u32[]{:S(2)}) collective-permute-start(f32[28,8,128]{2,1,0:T(8,128)S(1)} %get-tuple-element.84), channel_id=1, source_target_pairs={{1,2},{3,4},{5,6},{7,8},{9,10},{11,12},{13,14},{2,1},{4,3},{6,5},{... | collective-permute-start | bytes 344072 | tf_op jit(solution)/shard_map/ppermute | solution.py:776
  23.8 5.9 %collective-permute-start.9 = (f32[8,128]{1,0:T(8,128)S(1)}, f32[8,128]{1,0:T(8,128)S(1)}, u32[]{:S(2)}, u32[]{:S(2)}) collective-permute-start(f32[8,128]{1,0:T(8,128)S(1)} %fusion.1.refs_4_), channel_id=1, source_target_pairs={{0,8},{1,9},{2,10},{3,11},{4,12},{5,13},{6,14},{7,15},{8,0},{9,1},... | collective-permute-start | bytes 12296 | tf_op jit(solution)/shard_map/ppermute | solution.py:790
  29.7 0.7 %shard_map.73 = (f32[14,8,8,128]{3,2,1,0:T(8,128)S(1)}, f32[14,10,8,128]{3,2,1,0:T(8,128)S(1)}, f32[14,8,128]{2,1,0:T(8,128)S(1)}) custom-call(f32[14,8,8,128]{3,2,1,0:T(8,128)S(1)} %get-tuple-element.81.refs_0_, f32[14,8,8,128]{3,2,1,0:T(8,128)S(1)} %get-tuple-element.82.refs_1_, ...), custom_call_target="tpu_custom_call", output_to_operand_aliasing={{0}: (0, {})} | custom-call | tf_op jit(solution)/shard_map/pallas_call | solution.py:760
  30.4 2.1 %collective-permute-done.9.refs_5_ = f32[8,128]{1,0:T(8,128)S(1)} collective-permute-done((f32[8,128]{1,0:T(8,128)S(1)}, f32[8,128]{1,0:T(8,128)S(1)}, u32[]{:S(2)}, u32[]{:S(2)}) %collective-permute-start.9) | collective-permute-done | bytes 4128 | tf_op jit(solution)/shard_map/ppermute | solution.py:790
  32.5 0.5 %shard_map.74 = (f32[29,8,128]{2,1,0:T(8,128)S(1)}, f32[28,8,128]{2,1,0:T(8,128)S(1)}, f32[4,8,128]{2,1,0:T(8,128)S(1)}, f32[14,8,128]{2,1,0:T(8,128)S(1)}, f32[...) custom-call(f32[14,10,8,128]{3,2,1,0:T(8,128)S(1)} %get-tuple-elemen, ...), custom_call_target="tpu_custom_call" | custom-call | tf_op jit(solution)/shard_map/pallas_call | solution.py:760
  33.0 0.1 collective-permute-start.10
  33.1 0.6 %collective-permute-start.12 = (f32[4,8,128]{2,1,0:T(8,128)S(1)}, f32[4,8,128]{2,1,0:T(8,128)S(1)}, u32[]{:S(2)}, u32[]{:S(2)}) collective-permute-start(f32[4,8,128]{2,1,0:T(8,128)S(1)} %get-tuple-element.102), channel_id=1, source_target_pairs={{0,16},{16,0},{1,17},{17,1},{2,18},{18,2},{3,19},{19,3},{4,20},{20... | collective-permute-start | bytes 49160 | tf_op jit(solution)/shard_map/ppermute | solution.py:776
  33.7 0.7 %collective-permute-start.11 = (f32[28,8,128]{2,1,0:T(8,128)S(1)}, f32[28,8,128]{2,1,0:T(8,128)S(1)}, u32[]{:S(2)}, u32[]{:S(2)}) collective-permute-start(f32[28,8,128]{2,1,0:T(8,128)S(1)} %get-tuple-element.101), channel_id=1, source_target_pairs={{1,2},{3,4},{5,6},{7,8},{9,10},{11,12},{13,14},{2,1},{4,3},{6,5},{... | collective-permute-start | bytes 344072 | tf_op jit(solution)/shard_map/ppermute | solution.py:776
  34.3 0.1 collective-permute-done.10.refs_1_
  34.4 3.6 %collective-permute-start.13 = (f32[8,128]{1,0:T(8,128)S(1)}, f32[8,128]{1,0:T(8,128)S(1)}, u32[]{:S(2)}, u32[]{:S(2)}) collective-permute-start(f32[8,128]{1,0:T(8,128)S(1)} %fusion), channel_id=1, source_target_pairs={{0,4},{1,5},{2,6},{3,7},{4,0},{5,1},{6,2},{7,3},{8,12},{9,13},{10,... | collective-permute-start | bytes 12296 | tf_op jit(solution)/shard_map/ppermute | solution.py:790
  38.0 2.7 %collective-permute-done.13 = f32[8,128]{1,0:T(8,128)S(1)} collective-permute-done((f32[8,128]{1,0:T(8,128)S(1)}, f32[8,128]{1,0:T(8,128)S(1)}, u32[]{:S(2)}, u32[]{:S(2)}) %collective-permute-start.13) | collective-permute-done | bytes 4128 | tf_op jit(solution)/shard_map/ppermute | solution.py:790
  40.8 0.3 collective-permute-start.14
  41.1 1.2 %shard_map.75.refs_0_ = f32[14,8,8,128]{3,2,1,0:T(8,128)S(1)} custom-call(f32[14,12,8,128]{3,2,1,0:T(8,128)S(1)} %get-tuple-element.65.ext, s32[64,128]{1,0:T(8,128)S(1)} %get-tuple-element.54.words.refs_6_.refs_9_.refs_3_, f32[14,10,8,128]{3,2,1,0:T(8,128)S(1)} %get-tuple-element.86.a_ext, f32[14,8,8,128]{3,2,1,0:T(8,128)S(1)} %get-tuple-element.87.fvx, ...), custom_call_target="tpu_custom_call" | custom-call | tf_op jit(solution)/shard_map/pallas_call | solution.py:760
  42.3 1.1 %shard_map.76 = (f32[14,64,128]{2,1,0:T(8,128)}, f32[14,8,8,128]{3,2,1,0:T(8,128)S(1)}) custom-call(f32[14,8,8,128]{3,2,1,0:T(8,128)S(1)} %shard_map.75.refs_0_, f32[29,8,128]{2,1,0:T(8,128)S(1)} %collective-permute-done.10.refs_1_, f32[28,8,128]{2,1,0:T(8,128)S(1)} %collective-permute-done.11.refs_2_, ...), custom_call_target="tpu_custom_call", output_to_operand_aliasing={{1}: (0, {})} | custom-call | tf_op jit(solution)/shard_map/pallas_call | solution.py:760
  43.4 1.0 %collective-permute-done.14 = f32[8,128]{1,0:T(8,128)S(1)} collective-permute-done((f32[8,128]{1,0:T(8,128)S(1)}, f32[8,128]{1,0:T(8,128)S(1)}, u32[]{:S(2)}, u32[]{:S(2)}) %collective-permute-start.14) | collective-permute-done | bytes 4128 | tf_op jit(solution)/shard_map/ppermute | solution.py:790
  44.4 0.5 %multiply_bitcast_fusion = f32[24]{0:T(128)} fusion(f32[8,128]{1,0:T(8,128)S(1)} %add.22), kind=kLoop, calls=%fused_computation.4 | loop fusion | flops 24 | bytes 192 | tf_op jit(solution)/shard_map/mul | solution.py:878
  (16 shorter events, 0.0 us)
Async XLA Ops:
  2.0 6.2 %collective-permute-start = (f32[29,8,128]{2,1,0:T(8,128)S(1)}, f32[29,8,128]{2,1,0:T(8,128)S(1)}, u32[]{:S(2)}, u32[]{:S(2)}) collective-permute-start(f32[29,8,128]{2,1,0:T(8,128)S(1)} %get-tuple-element.62), channel_id=1, source_target_pairs={{0,1},{2,3},{4,5},{6,7},{8,9},{10,11},{12,13},{14,15},{1,0},{3,2},... | collective-permute-start | bytes 356360 | tf_op jit(solution)/shard_map/ppermute | solution.py:776
  2.5 5.7 %collective-permute-start.1 = (f32[29,8,128]{2,1,0:T(8,128)S(1)}, f32[29,8,128]{2,1,0:T(8,128)S(1)}, u32[]{:S(2)}, u32[]{:S(2)}) collective-permute-start(f32[29,8,128]{2,1,0:T(8,128)S(1)} %get-tuple-element.63), channel_id=1, source_target_pairs={{1,2},{3,4},{5,6},{7,8},{9,10},{11,12},{13,14},{2,1},{4,3},{6,5},{... | collective-permute-start | bytes 356360 | tf_op jit(solution)/shard_map/ppermute | solution.py:776
  3.2 5.0 %collective-permute-start.2 = (f32[5,8,128]{2,1,0:T(8,128)S(1)}, f32[5,8,128]{2,1,0:T(8,128)S(1)}, u32[]{:S(2)}, u32[]{:S(2)}) collective-permute-start(f32[5,8,128]{2,1,0:T(8,128)S(1)} %get-tuple-element.64), channel_id=1, source_target_pairs={{0,16},{16,0},{1,17},{17,1},{2,18},{18,2},{3,19},{19,3},{4,20},{20... | collective-permute-start | bytes 61448 | tf_op jit(solution)/shard_map/ppermute | solution.py:776
  5.8 0.7 %copy-start.1 = (f32[24]{0:T(128)S(1)}, f32[24]{0:T(128)}, u32[]{:S(2)}) copy-start(f32[24]{0:T(128)} %refs_0_.1) | copy-start | bytes 292
  9.5 7.1 %copy-start = (f32[14,8,8,128]{3,2,1,0:T(8,128)S(1)}, f32[14,8,8,128]{3,2,1,0:T(8,128)}, u32[]{:S(2)}) copy-start(f32[14,8,8,128]{3,2,1,0:T(8,128)} %param.6) | copy-start | bytes 1376260
  9.5 7.1 %collective-permute-start.3 = (f32[28,8,128]{2,1,0:T(8,128)S(1)}, f32[28,8,128]{2,1,0:T(8,128)S(1)}, u32[]{:S(2)}, u32[]{:S(2)}) collective-permute-start(f32[28,8,128]{2,1,0:T(8,128)S(1)} %get-tuple-element.78), channel_id=1, source_target_pairs={{0,1},{2,3},{4,5},{6,7},{8,9},{10,11},{12,13},{14,15},{1,0},{3,2},... | collective-permute-start | bytes 344072 | tf_op jit(solution)/shard_map/ppermute | solution.py:776
  12.1 4.5 %collective-permute-start.4 = (f32[28,8,128]{2,1,0:T(8,128)S(1)}, f32[28,8,128]{2,1,0:T(8,128)S(1)}, u32[]{:S(2)}, u32[]{:S(2)}) collective-permute-start(f32[28,8,128]{2,1,0:T(8,128)S(1)} %get-tuple-element.79), channel_id=1, source_target_pairs={{1,2},{3,4},{5,6},{7,8},{9,10},{11,12},{13,14},{2,1},{4,3},{6,5},{... | collective-permute-start | bytes 344072 | tf_op jit(solution)/shard_map/ppermute | solution.py:776
  12.8 3.8 %collective-permute-start.5 = (f32[4,8,128]{2,1,0:T(8,128)S(1)}, f32[4,8,128]{2,1,0:T(8,128)S(1)}, u32[]{:S(2)}, u32[]{:S(2)}) collective-permute-start(f32[4,8,128]{2,1,0:T(8,128)S(1)} %get-tuple-element.80), channel_id=1, source_target_pairs={{0,16},{16,0},{1,17},{17,1},{2,18},{18,2},{3,19},{19,3},{4,20},{20... | collective-permute-start | bytes 49160 | tf_op jit(solution)/shard_map/ppermute | solution.py:776
  19.9 3.9 %collective-permute-start.8 = (f32[5,8,128]{2,1,0:T(8,128)S(1)}, f32[5,8,128]{2,1,0:T(8,128)S(1)}, u32[]{:S(2)}, u32[]{:S(2)}) collective-permute-start(f32[5,8,128]{2,1,0:T(8,128)S(1)} %get-tuple-element.85), channel_id=1, source_target_pairs={{0,16},{16,0},{1,17},{17,1},{2,18},{18,2},{3,19},{19,3},{4,20},{20... | collective-permute-start | bytes 61448 | tf_op jit(solution)/shard_map/ppermute | solution.py:776
  20.8 8.9 %collective-permute-start.6 = (f32[28,8,128]{2,1,0:T(8,128)S(1)}, f32[28,8,128]{2,1,0:T(8,128)S(1)}, u32[]{:S(2)}, u32[]{:S(2)}) collective-permute-start(f32[28,8,128]{2,1,0:T(8,128)S(1)} %get-tuple-element.83), channel_id=1, source_target_pairs={{0,1},{2,3},{4,5},{6,7},{8,9},{10,11},{12,13},{14,15},{1,0},{3,2},... | collective-permute-start | bytes 344072 | tf_op jit(solution)/shard_map/ppermute | solution.py:776
  23.1 6.6 %collective-permute-start.7 = (f32[28,8,128]{2,1,0:T(8,128)S(1)}, f32[28,8,128]{2,1,0:T(8,128)S(1)}, u32[]{:S(2)}, u32[]{:S(2)}) collective-permute-start(f32[28,8,128]{2,1,0:T(8,128)S(1)} %get-tuple-element.84), channel_id=1, source_target_pairs={{1,2},{3,4},{5,6},{7,8},{9,10},{11,12},{13,14},{2,1},{4,3},{6,5},{... | collective-permute-start | bytes 344072 | tf_op jit(solution)/shard_map/ppermute | solution.py:776
  23.8 8.7 %collective-permute-start.9 = (f32[8,128]{1,0:T(8,128)S(1)}, f32[8,128]{1,0:T(8,128)S(1)}, u32[]{:S(2)}, u32[]{:S(2)}) collective-permute-start(f32[8,128]{1,0:T(8,128)S(1)} %fusion.1.refs_4_), channel_id=1, source_target_pairs={{0,8},{1,9},{2,10},{3,11},{4,12},{5,13},{6,14},{7,15},{8,0},{9,1},... | collective-permute-start | bytes 12296 | tf_op jit(solution)/shard_map/ppermute | solution.py:790
  33.0 1.4 %collective-permute-start.10 = (f32[29,8,128]{2,1,0:T(8,128)S(1)}, f32[29,8,128]{2,1,0:T(8,128)S(1)}, u32[]{:S(2)}, u32[]{:S(2)}) collective-permute-start(f32[29,8,128]{2,1,0:T(8,128)S(1)} %get-tuple-element.100), channel_id=1, source_target_pairs={{0,1},{2,3},{4,5},{6,7},{8,9},{10,11},{12,13},{14,15},{1,0},{3,2},... | collective-permute-start | bytes 356360 | tf_op jit(solution)/shard_map/ppermute | solution.py:776
  33.1 9.2 %collective-permute-start.12 = (f32[4,8,128]{2,1,0:T(8,128)S(1)}, f32[4,8,128]{2,1,0:T(8,128)S(1)}, u32[]{:S(2)}, u32[]{:S(2)}) collective-permute-start(f32[4,8,128]{2,1,0:T(8,128)S(1)} %get-tuple-element.102), channel_id=1, source_target_pairs={{0,16},{16,0},{1,17},{17,1},{2,18},{18,2},{3,19},{19,3},{4,20},{20... | collective-permute-start | bytes 49160 | tf_op jit(solution)/shard_map/ppermute | solution.py:776
  33.7 8.6 %collective-permute-start.11 = (f32[28,8,128]{2,1,0:T(8,128)S(1)}, f32[28,8,128]{2,1,0:T(8,128)S(1)}, u32[]{:S(2)}, u32[]{:S(2)}) collective-permute-start(f32[28,8,128]{2,1,0:T(8,128)S(1)} %get-tuple-element.101), channel_id=1, source_target_pairs={{1,2},{3,4},{5,6},{7,8},{9,10},{11,12},{13,14},{2,1},{4,3},{6,5},{... | collective-permute-start | bytes 344072 | tf_op jit(solution)/shard_map/ppermute | solution.py:776
  34.4 6.3 %collective-permute-start.13 = (f32[8,128]{1,0:T(8,128)S(1)}, f32[8,128]{1,0:T(8,128)S(1)}, u32[]{:S(2)}, u32[]{:S(2)}) collective-permute-start(f32[8,128]{1,0:T(8,128)S(1)} %fusion), channel_id=1, source_target_pairs={{0,4},{1,5},{2,6},{3,7},{4,0},{5,1},{6,2},{7,3},{8,12},{9,13},{10,... | collective-permute-start | bytes 12296 | tf_op jit(solution)/shard_map/ppermute | solution.py:790
  40.8 3.6 %collective-permute-start.14 = (f32[8,128]{1,0:T(8,128)S(1)}, f32[8,128]{1,0:T(8,128)S(1)}, u32[]{:S(2)}, u32[]{:S(2)}) collective-permute-start(f32[8,128]{1,0:T(8,128)S(1)} %add.21), channel_id=1, source_target_pairs={{0,2},{1,3},{2,0},{3,1},{4,6},{5,7},{6,4},{7,5},{8,10},{9,11},{10,... | collective-permute-start | bytes 12296 | tf_op jit(solution)/shard_map/ppermute | solution.py:790

commit v5 on v4

--- a/solution.py
+++ b/solution.py
@@ -12,6 +12,7 @@
 FIELDS = 14
 ROWS = 8
 LANES = 128
+HALVES = (range(7), range(7, FIELDS))
 PHASES = ((0, 5), (5, 3), (8, 3), (11, 3))
 FACE = 0.3 * 0.5 * 0.5
 COUPLING = 0.5
@@ -725,18 +726,22 @@
     def kernel(*refs):
         _, from_a, from_b, from_c = refs[:4]
         from_d = refs[4] if has_odd else None
-        out, part, incoming = refs[4 + has_odd :]
+        out, part, incoming, staged, sems = refs[4 + has_odd :]
         pick = side_payloads(from_c, from_d)
         collect(part, from_a, from_b, pick, incoming)
         edges = edge_lanes()
 
-        def one_row(r, carry):
-            for f in range(FIELDS):
-                value = part[f, r] + jnp.where(edges, roll(incoming[f], (124 - 16 * r) % LANES), 0.0)
-                out[f, pl.ds(r, 8, stride=8), :] = value
-            return carry
-
-        lax.fori_loop(0, ROWS, one_row, 0, unroll=8)
+        copies = []
+        for k, fields in enumerate(HALVES):
+            for r in range(ROWS):
+                for f in fields:
+                    value = part[f, r] + jnp.where(edges, roll(incoming[f], (124 - 16 * r) % LANES), 0.0)
+                    staged[f, pl.ds(r, 8, stride=8), :] = value
+            span = pl.ds(fields[0], len(fields))
+            copies.append(pltpu.make_async_copy(staged.at[span], out.at[span], sems.at[k]))
+            copies[-1].start()
+        for copy in copies:
+            copy.wait()
 
     return kernel
 
@@ -753,7 +758,7 @@
     return pltpu.VMEM((*shape, 8, LANES), dtype)
 
 
-def call(kernel, outs, scratches, args, smem=(), hbm=(), aliases=None):
+def call(kernel, outs, scratches, args, smem=(), hbm=(), aliases=None, hbm_outs=()):
     def space(k):
         return pltpu.SMEM if k in smem else pltpu.HBM if k in hbm else pltpu.VMEM
 
@@ -761,7 +766,7 @@
         kernel,
         out_shape=outs,
         in_specs=[pl.BlockSpec(memory_space=space(k)) for k in range(len(args))],
-        out_specs=[pl.BlockSpec(memory_space=pltpu.VMEM)] * len(outs),
+        out_specs=[pl.BlockSpec(memory_space=pltpu.HBM if k in hbm_outs else pltpu.VMEM) for k in range(len(outs))],
         scratch_shapes=scratches,
         input_output_aliases=aliases or {},
         compiler_params=pltpu.CompilerParams(vmem_limit_bytes=32 << 20),
@@ -864,15 +869,18 @@
     sdc, sdu, gl, gh, dvy = adjoints
     got = exchange(to_a, to_b, to_c)
     grads = to_a[2 * FIELDS] + got[0][2 * FIELDS]
-    for axis, distance in steps[early_steps:]:
+    for axis, distance in steps[early_steps:-1]:
         grads = add_partner(grads, axis, distance)
     (part,) = call(own_kernel, [tiles(14, 8)], [], [ext, words, a_ext, fvx, ux, sdc, sdu, gl, gh, dvy])
+    grads, part = lax.optimization_barrier((grads, part))
+    grads = add_partner(grads, *steps[-1])
     out, _ = call(
         last_kernel(has_odd),
         [shaped(FIELDS, LEV * ROWS, LANES), tiles(14, 8)],
-        [scratch(14)],
+        [scratch(14), pltpu.VMEM(start.shape, jnp.float32), pltpu.SemaphoreType.DMA((2,))],
         [part, *got],
         aliases={0: 1},
+        hbm_outs=(0,),
     )
     grad_scale = math.sqrt(NCLASS / (terrain.size * nx * ny * LEV))
     return (out.reshape(start_state.shape), grads[0, :NCLASS] * grad_scale)

time: 45.1 us -> 45.1 us (level)
  no operation moved by 1% of the time
where the time goes in v5:
time: 45.1 us; the launch traced here: 44.9 us
  starting transfers between devices  23 us (51%)
  Pallas kernels  12.2 us (27%)
  waiting for transfers between devices  7.71 us (17%)
  between operations  0.79 us (2%)
  local copies, waits for them, and re-layouts  0.66 us (1%)
  other arithmetic  0.53 us (1%)
    ppermute x12, starting transfers between devices, swap(): return lax.ppermute(x, axis, pairs + [(j, i) for i, j in pairs])  13.2 us
    pallas_call x9, Pallas kernels, call(): pl.pallas_call(kernel, out_shape=outs, in_specs=[pl.BlockSpec(memory_spac...  12.2 us
    ppermute x3, starting transfers between devices, from_partner(): lax.ppermute(x, axis, [(i, i ^ distance) for i in range(lax.axis_size(axi...  9.8 us
    ppermute x3, waiting for transfers between devices, from_partner(): lax.ppermute(x, axis, [(i, i ^ distance) for i in range(lax.axis_size(axi...  5.95 us
    ppermute x12, waiting for transfers between devices, swap(): return lax.ppermute(x, axis, pairs + [(j, i) for i, j in pairs])  1.77 us
  transfers between devices with their start and end apart: 15, of which 5 were waited for; matrix products, arithmetic and copies ran while one was open for 0% of the time, Pallas kernels for 13%

profile of v5, /device:TPU:0, one launch (start us, length us, event | category | flops | bytes accessed | tf_op | source)
XLA Modules:
  0.0 44.9 jit_solution(3014507186976818955)
XLA Ops:
  0.6 1.3 %shard_map.68 = (s32[64,128]{1,0:T(8,128)S(1)}, s32[8,128]{1,0:T(8,128)S(1)}, f32[14,12,8,128]{3,2,1,0:T(8,128)S(1)}, f32[14,8,128]{2,1,0:T(8,128)S(1)}, s32[8,1...) custom-call(f32[14,64,128]{2,1,0:T(8,128)} %bitcast.11, ...), custom_call_target="tpu_custom_call" | custom-call | tf_op jit(solution)/shard_map/pallas_call | solution.py:765
  2.0 0.5 %collective-permute-start = (f32[29,8,128]{2,1,0:T(8,128)S(1)}, f32[29,8,128]{2,1,0:T(8,128)S(1)}, u32[]{:S(2)}, u32[]{:S(2)}) collective-permute-start(f32[29,8,128]{2,1,0:T(8,128)S(1)} %get-tuple-element.64), channel_id=1, source_target_pairs={{0,1},{2,3},{4,5},{6,7},{8,9},{10,11},{12,13},{14,15},{1,0},{3,2},... | collective-permute-start | bytes 356360 | tf_op jit(solution)/shard_map/ppermute | solution.py:781
  2.5 0.7 %collective-permute-start.1 = (f32[29,8,128]{2,1,0:T(8,128)S(1)}, f32[29,8,128]{2,1,0:T(8,128)S(1)}, u32[]{:S(2)}, u32[]{:S(2)}) collective-permute-start(f32[29,8,128]{2,1,0:T(8,128)S(1)} %get-tuple-element.65), channel_id=1, source_target_pairs={{1,2},{3,4},{5,6},{7,8},{9,10},{11,12},{13,14},{2,1},{4,3},{6,5},{... | collective-permute-start | bytes 356360 | tf_op jit(solution)/shard_map/ppermute | solution.py:781
  3.2 2.6 %collective-permute-start.2 = (f32[5,8,128]{2,1,0:T(8,128)S(1)}, f32[5,8,128]{2,1,0:T(8,128)S(1)}, u32[]{:S(2)}, u32[]{:S(2)}) collective-permute-start(f32[5,8,128]{2,1,0:T(8,128)S(1)} %get-tuple-element.66), channel_id=1, source_target_pairs={{0,16},{16,0},{1,17},{17,1},{2,18},{18,2},{3,19},{19,3},{4,20},{20... | collective-permute-start | bytes 61448 | tf_op jit(solution)/shard_map/ppermute | solution.py:781
  5.8 0.7 %copy-done.1 = f32[24]{0:T(128)S(1)} copy-done((f32[24]{0:T(128)S(1)}, f32[24]{0:T(128)}, u32[]{:S(2)}) %copy-start.1) | copy-done | bytes 120
  6.4 1.7 %shard_map.69 = (f32[14,8,8,128]{3,2,1,0:T(8,128)S(1)}, f32[4,8,8,128]{3,2,1,0:T(8,128)S(1)}, f32[14,8,8,128]{3,2,1,0:T(8,128)S(1)}, f32[14,9,8,128]{3,2,1,0:T(8...) custom-call(f32[14,12,8,128]{3,2,1,0:T(8,128)S(1)} %get-tuple-element.55.ext.refs_0_, ...), custom_call_target="tpu_custom_call" | custom-call | tf_op jit(solution)/shard_map/pallas_call | solution.py:765
  8.2 1.3 %shard_map.70 = (f32[14,12,8,128]{3,2,1,0:T(8,128)S(1)}, f32[14,9,8,128]{3,2,1,0:T(8,128)S(1)}, f32[4,9,8,128]{3,2,1,0:T(8,128)S(1)}, f32[14,8,128]{2,1,0:T(8,12...) custom-call(f32[14,12,8,128]{3,2,1,0:T(8,128)S(1)} %get-tuple-elemen, ...), custom_call_target="tpu_custom_call", output_to_operand_aliasing={{0}: (0, {}), {1}: (1, {}), {2}: (2, {})} | custom-call | tf_op jit(solution)/shard_map/pallas_call | solution.py:765
  9.5 0.0 copy-start
  9.5 2.6 %collective-permute-start.3 = (f32[28,8,128]{2,1,0:T(8,128)S(1)}, f32[28,8,128]{2,1,0:T(8,128)S(1)}, u32[]{:S(2)}, u32[]{:S(2)}) collective-permute-start(f32[28,8,128]{2,1,0:T(8,128)S(1)} %get-tuple-element.79), channel_id=1, source_target_pairs={{0,1},{2,3},{4,5},{6,7},{8,9},{10,11},{12,13},{14,15},{1,0},{3,2},... | collective-permute-start | bytes 344072 | tf_op jit(solution)/shard_map/ppermute | solution.py:781
  12.1 0.7 %collective-permute-start.4 = (f32[28,8,128]{2,1,0:T(8,128)S(1)}, f32[28,8,128]{2,1,0:T(8,128)S(1)}, u32[]{:S(2)}, u32[]{:S(2)}) collective-permute-start(f32[28,8,128]{2,1,0:T(8,128)S(1)} %get-tuple-element.80), channel_id=1, source_target_pairs={{1,2},{3,4},{5,6},{7,8},{9,10},{11,12},{13,14},{2,1},{4,3},{6,5},{... | collective-permute-start | bytes 344072 | tf_op jit(solution)/shard_map/ppermute | solution.py:781
  12.8 1.0 %collective-permute-start.5 = (f32[4,8,128]{2,1,0:T(8,128)S(1)}, f32[4,8,128]{2,1,0:T(8,128)S(1)}, u32[]{:S(2)}, u32[]{:S(2)}) collective-permute-start(f32[4,8,128]{2,1,0:T(8,128)S(1)} %get-tuple-element.81), channel_id=1, source_target_pairs={{0,16},{16,0},{1,17},{17,1},{2,18},{18,2},{3,19},{19,3},{4,20},{20... | collective-permute-start | bytes 49160 | tf_op jit(solution)/shard_map/ppermute | solution.py:781
  13.7 1.2 %shard_map.71 = (f32[14,8,8,128]{3,2,1,0:T(8,128)S(1)}, f32[4,8,8,128]{3,2,1,0:T(8,128)S(1)}, f32[14,8,8,128]{3,2,1,0:T(8,128)S(1)}, f32[14,9,8,128]{3,2,1,0:T(8,128)S(1)}, f32[4,9,8,128]{3,2,1,0:T(8,128)S(1)}) custom-call(f32[14,12,8,128]{3,2,1,0:T(8,128)S(1)} %get-tuple-element.67.ext.refs_0_, s32[64,128]{1,0:T(8,128)S(1)} %get-tuple-element.56.words.refs_6_.refs_9_.refs_3_), custom_call_target="tpu_custom_call" | custom-call | tf_op jit(solution)/shard_map/pallas_call | solution.py:765
  14.9 1.7 %collective-permute-done.5.refs_17_ = f32[4,8,128]{2,1,0:T(8,128)S(1)} collective-permute-done((f32[4,8,128]{2,1,0:T(8,128)S(1)}, f32[4,8,128]{2,1,0:T(8,128)S(1)}, u32[]{:S(2)}, u32[]{:S(2)}) %collective-permute-start.5) | collective-permute-done | bytes 16416 | tf_op jit(solution)/shard_map/ppermute | solution.py:781
  16.6 3.4 %shard_map.72 = (f32[14,12,8,128]{3,2,1,0:T(8,128)S(1)}, f32[14,12,8,128]{3,2,1,0:T(8,128)S(1)}, f32[14,9,8,128]{3,2,1,0:T(8,128)S(1)}, f32[4,9,8,128]{3,2,1,0:T...) custom-call(f32[14,12,8,128]{3,2,1,0:T(8,128)S(1)} %get-tuple-elemen, ...), custom_call_target="tpu_custom_call", output_to_operand_aliasing={{0}: (0, {}), {1}: (1, {}), {2}: (2, {}), {3}: (3, {})} | custom-call | tf_op jit(solution)/shard_map/pallas_call | solution.py:765
  19.9 0.9 %collective-permute-start.8 = (f32[5,8,128]{2,1,0:T(8,128)S(1)}, f32[5,8,128]{2,1,0:T(8,128)S(1)}, u32[]{:S(2)}, u32[]{:S(2)}) collective-permute-start(f32[5,8,128]{2,1,0:T(8,128)S(1)} %get-tuple-element.86), channel_id=1, source_target_pairs={{0,16},{16,0},{1,17},{17,1},{2,18},{18,2},{3,19},{19,3},{4,20},{20... | collective-permute-start | bytes 61448 | tf_op jit(solution)/shard_map/ppermute | solution.py:781
  20.8 2.3 %collective-permute-start.6 = (f32[28,8,128]{2,1,0:T(8,128)S(1)}, f32[28,8,128]{2,1,0:T(8,128)S(1)}, u32[]{:S(2)}, u32[]{:S(2)}) collective-permute-start(f32[28,8,128]{2,1,0:T(8,128)S(1)} %get-tuple-element.84), channel_id=1, source_target_pairs={{0,1},{2,3},{4,5},{6,7},{8,9},{10,11},{12,13},{14,15},{1,0},{3,2},... | collective-permute-start | bytes 344072 | tf_op jit(solution)/shard_map/ppermute | solution.py:781
  23.1 0.7 %collective-permute-start.7 = (f32[28,8,128]{2,1,0:T(8,128)S(1)}, f32[28,8,128]{2,1,0:T(8,128)S(1)}, u32[]{:S(2)}, u32[]{:S(2)}) collective-permute-start(f32[28,8,128]{2,1,0:T(8,128)S(1)} %get-tuple-element.85), channel_id=1, source_target_pairs={{1,2},{3,4},{5,6},{7,8},{9,10},{11,12},{13,14},{2,1},{4,3},{6,5},{... | collective-permute-start | bytes 344072 | tf_op jit(solution)/shard_map/ppermute | solution.py:781
  23.8 5.9 %collective-permute-start.9 = (f32[8,128]{1,0:T(8,128)S(1)}, f32[8,128]{1,0:T(8,128)S(1)}, u32[]{:S(2)}, u32[]{:S(2)}) collective-permute-start(f32[8,128]{1,0:T(8,128)S(1)} %fusion.1.refs_4_), channel_id=1, source_target_pairs={{0,8},{1,9},{2,10},{3,11},{4,12},{5,13},{6,14},{7,15},{8,0},{9,1},... | collective-permute-start | bytes 12296 | tf_op jit(solution)/shard_map/ppermute | solution.py:795
  29.7 0.7 %shard_map.73 = (f32[14,8,8,128]{3,2,1,0:T(8,128)S(1)}, f32[14,10,8,128]{3,2,1,0:T(8,128)S(1)}, f32[14,8,128]{2,1,0:T(8,128)S(1)}) custom-call(f32[14,8,8,128]{3,2,1,0:T(8,128)S(1)} %get-tuple-element.82.refs_0_, f32[14,8,8,128]{3,2,1,0:T(8,128)S(1)} %get-tuple-element.83.refs_1_, ...), custom_call_target="tpu_custom_call", output_to_operand_aliasing={{0}: (0, {})} | custom-call | tf_op jit(solution)/shard_map/pallas_call | solution.py:765
  30.4 2.1 %collective-permute-done.9.refs_5_ = f32[8,128]{1,0:T(8,128)S(1)} collective-permute-done((f32[8,128]{1,0:T(8,128)S(1)}, f32[8,128]{1,0:T(8,128)S(1)}, u32[]{:S(2)}, u32[]{:S(2)}) %collective-permute-start.9) | collective-permute-done | bytes 4128 | tf_op jit(solution)/shard_map/ppermute | solution.py:795
  32.5 0.5 %shard_map.74 = (f32[29,8,128]{2,1,0:T(8,128)S(1)}, f32[28,8,128]{2,1,0:T(8,128)S(1)}, f32[4,8,128]{2,1,0:T(8,128)S(1)}, f32[14,8,128]{2,1,0:T(8,128)S(1)}, f32[...) custom-call(f32[14,10,8,128]{3,2,1,0:T(8,128)S(1)} %get-tuple-elemen, ...), custom_call_target="tpu_custom_call" | custom-call | tf_op jit(solution)/shard_map/pallas_call | solution.py:765
  33.0 0.1 collective-permute-start.10
  33.1 0.6 %collective-permute-start.13 = (f32[4,8,128]{2,1,0:T(8,128)S(1)}, f32[4,8,128]{2,1,0:T(8,128)S(1)}, u32[]{:S(2)}, u32[]{:S(2)}) collective-permute-start(f32[4,8,128]{2,1,0:T(8,128)S(1)} %get-tuple-element.105), channel_id=1, source_target_pairs={{0,16},{16,0},{1,17},{17,1},{2,18},{18,2},{3,19},{19,3},{4,20},{20... | collective-permute-start | bytes 49160 | tf_op jit(solution)/shard_map/ppermute | solution.py:781
  33.7 0.7 %collective-permute-start.12 = (f32[28,8,128]{2,1,0:T(8,128)S(1)}, f32[28,8,128]{2,1,0:T(8,128)S(1)}, u32[]{:S(2)}, u32[]{:S(2)}) collective-permute-start(f32[28,8,128]{2,1,0:T(8,128)S(1)} %get-tuple-element.104), channel_id=1, source_target_pairs={{1,2},{3,4},{5,6},{7,8},{9,10},{11,12},{13,14},{2,1},{4,3},{6,5},{... | collective-permute-start | bytes 344072 | tf_op jit(solution)/shard_map/ppermute | solution.py:781
  34.3 0.1 collective-permute-done.10.refs_1_
  34.4 3.6 %collective-permute-start.11 = (f32[8,128]{1,0:T(8,128)S(1)}, f32[8,128]{1,0:T(8,128)S(1)}, u32[]{:S(2)}, u32[]{:S(2)}) collective-permute-start(f32[8,128]{1,0:T(8,128)S(1)} %fusion), channel_id=1, source_target_pairs={{0,4},{1,5},{2,6},{3,7},{4,0},{5,1},{6,2},{7,3},{8,12},{9,13},{10,... | collective-permute-start | bytes 12296 | tf_op jit(solution)/shard_map/ppermute | solution.py:795
  38.0 1.2 %shard_map.75.refs_0_ = f32[14,8,8,128]{3,2,1,0:T(8,128)S(1)} custom-call(f32[14,12,8,128]{3,2,1,0:T(8,128)S(1)} %get-tuple-element.89.ext, s32[64,128]{1,0:T(8,128)S(1)} %get-tuple-element.56.words.refs_6_.refs_9_.refs_3_, f32[14,10,8,128]{3,2,1,0:T(8,128)S(1)} %get-tuple-element.87.a_ext, f32[14,8,8,128]{3,2,1,0:T(8,128)S(1)} %get-tuple-element.96.fvx, ...), custom_call_target="tpu_custom_call" | custom-call | tf_op jit(solution)/shard_map/pallas_call | solution.py:765
  39.2 1.5 %collective-permute-done.11 = f32[8,128]{1,0:T(8,128)S(1)} collective-permute-done((f32[8,128]{1,0:T(8,128)S(1)}, f32[8,128]{1,0:T(8,128)S(1)}, u32[]{:S(2)}, u32[]{:S(2)}) %collective-permute-start.11) | collective-permute-done | bytes 4128 | tf_op jit(solution)/shard_map/ppermute | solution.py:795
  40.8 0.3 collective-permute-start.14
  41.1 1.0 %shard_map.76 = (f32[14,64,128]{2,1,0:T(8,128)}, f32[14,8,8,128]{3,2,1,0:T(8,128)S(1)}) custom-call(f32[14,8,8,128]{3,2,1,0:T(8,128)S(1)} %shard_map.75.refs_0_, f32[29,8,128]{2,1,0:T(8,128)S(1)} %collective-permute-done.10.refs_1_, f32[28,8,128]{2,1,0:T(8,128)S(1)} %collective-permute-done.12.refs_2_, ...), custom_call_target="tpu_custom_call", output_to_operand_aliasing={{1}: (0, {})} | custom-call | tf_op jit(solution)/shard_map/pallas_call | solution.py:765
  42.1 2.3 %collective-permute-done.14 = f32[8,128]{1,0:T(8,128)S(1)} collective-permute-done((f32[8,128]{1,0:T(8,128)S(1)}, f32[8,128]{1,0:T(8,128)S(1)}, u32[]{:S(2)}, u32[]{:S(2)}) %collective-permute-start.14) | collective-permute-done | bytes 4128 | tf_op jit(solution)/shard_map/ppermute | solution.py:795
  44.4 0.5 %multiply_bitcast_fusion = f32[24]{0:T(128)} fusion(f32[8,128]{1,0:T(8,128)S(1)} %add.22), kind=kLoop, calls=%fused_computation.4 | loop fusion | flops 24 | bytes 192 | tf_op jit(solution)/shard_map/mul | solution.py:886
  (16 shorter events, 0.0 us)
Async XLA Ops:
  2.0 6.2 %collective-permute-start = (f32[29,8,128]{2,1,0:T(8,128)S(1)}, f32[29,8,128]{2,1,0:T(8,128)S(1)}, u32[]{:S(2)}, u32[]{:S(2)}) collective-permute-start(f32[29,8,128]{2,1,0:T(8,128)S(1)} %get-tuple-element.64), channel_id=1, source_target_pairs={{0,1},{2,3},{4,5},{6,7},{8,9},{10,11},{12,13},{14,15},{1,0},{3,2},... | collective-permute-start | bytes 356360 | tf_op jit(solution)/shard_map/ppermute | solution.py:781
  2.5 5.7 %collective-permute-start.1 = (f32[29,8,128]{2,1,0:T(8,128)S(1)}, f32[29,8,128]{2,1,0:T(8,128)S(1)}, u32[]{:S(2)}, u32[]{:S(2)}) collective-permute-start(f32[29,8,128]{2,1,0:T(8,128)S(1)} %get-tuple-element.65), channel_id=1, source_target_pairs={{1,2},{3,4},{5,6},{7,8},{9,10},{11,12},{13,14},{2,1},{4,3},{6,5},{... | collective-permute-start | bytes 356360 | tf_op jit(solution)/shard_map/ppermute | solution.py:781
  3.2 5.0 %collective-permute-start.2 = (f32[5,8,128]{2,1,0:T(8,128)S(1)}, f32[5,8,128]{2,1,0:T(8,128)S(1)}, u32[]{:S(2)}, u32[]{:S(2)}) collective-permute-start(f32[5,8,128]{2,1,0:T(8,128)S(1)} %get-tuple-element.66), channel_id=1, source_target_pairs={{0,16},{16,0},{1,17},{17,1},{2,18},{18,2},{3,19},{19,3},{4,20},{20... | collective-permute-start | bytes 61448 | tf_op jit(solution)/shard_map/ppermute | solution.py:781
  5.8 0.7 %copy-start.1 = (f32[24]{0:T(128)S(1)}, f32[24]{0:T(128)}, u32[]{:S(2)}) copy-start(f32[24]{0:T(128)} %refs_0_.1) | copy-start | bytes 292
  9.5 7.1 %copy-start = (f32[14,8,8,128]{3,2,1,0:T(8,128)S(1)}, f32[14,8,8,128]{3,2,1,0:T(8,128)}, u32[]{:S(2)}) copy-start(f32[14,8,8,128]{3,2,1,0:T(8,128)} %param.6) | copy-start | bytes 1376260
  9.5 7.1 %collective-permute-start.3 = (f32[28,8,128]{2,1,0:T(8,128)S(1)}, f32[28,8,128]{2,1,0:T(8,128)S(1)}, u32[]{:S(2)}, u32[]{:S(2)}) collective-permute-start(f32[28,8,128]{2,1,0:T(8,128)S(1)} %get-tuple-element.79), channel_id=1, source_target_pairs={{0,1},{2,3},{4,5},{6,7},{8,9},{10,11},{12,13},{14,15},{1,0},{3,2},... | collective-permute-start | bytes 344072 | tf_op jit(solution)/shard_map/ppermute | solution.py:781
  12.1 4.5 %collective-permute-start.4 = (f32[28,8,128]{2,1,0:T(8,128)S(1)}, f32[28,8,128]{2,1,0:T(8,128)S(1)}, u32[]{:S(2)}, u32[]{:S(2)}) collective-permute-start(f32[28,8,128]{2,1,0:T(8,128)S(1)} %get-tuple-element.80), channel_id=1, source_target_pairs={{1,2},{3,4},{5,6},{7,8},{9,10},{11,12},{13,14},{2,1},{4,3},{6,5},{... | collective-permute-start | bytes 344072 | tf_op jit(solution)/shard_map/ppermute | solution.py:781
  12.8 3.8 %collective-permute-start.5 = (f32[4,8,128]{2,1,0:T(8,128)S(1)}, f32[4,8,128]{2,1,0:T(8,128)S(1)}, u32[]{:S(2)}, u32[]{:S(2)}) collective-permute-start(f32[4,8,128]{2,1,0:T(8,128)S(1)} %get-tuple-element.81), channel_id=1, source_target_pairs={{0,16},{16,0},{1,17},{17,1},{2,18},{18,2},{3,19},{19,3},{4,20},{20... | collective-permute-start | bytes 49160 | tf_op jit(solution)/shard_map/ppermute | solution.py:781
  19.9 3.9 %collective-permute-start.8 = (f32[5,8,128]{2,1,0:T(8,128)S(1)}, f32[5,8,128]{2,1,0:T(8,128)S(1)}, u32[]{:S(2)}, u32[]{:S(2)}) collective-permute-start(f32[5,8,128]{2,1,0:T(8,128)S(1)} %get-tuple-element.86), channel_id=1, source_target_pairs={{0,16},{16,0},{1,17},{17,1},{2,18},{18,2},{3,19},{19,3},{4,20},{20... | collective-permute-start | bytes 61448 | tf_op jit(solution)/shard_map/ppermute | solution.py:781
  20.8 8.9 %collective-permute-start.6 = (f32[28,8,128]{2,1,0:T(8,128)S(1)}, f32[28,8,128]{2,1,0:T(8,128)S(1)}, u32[]{:S(2)}, u32[]{:S(2)}) collective-permute-start(f32[28,8,128]{2,1,0:T(8,128)S(1)} %get-tuple-element.84), channel_id=1, source_target_pairs={{0,1},{2,3},{4,5},{6,7},{8,9},{10,11},{12,13},{14,15},{1,0},{3,2},... | collective-permute-start | bytes 344072 | tf_op jit(solution)/shard_map/ppermute | solution.py:781
  23.1 6.6 %collective-permute-start.7 = (f32[28,8,128]{2,1,0:T(8,128)S(1)}, f32[28,8,128]{2,1,0:T(8,128)S(1)}, u32[]{:S(2)}, u32[]{:S(2)}) collective-permute-start(f32[28,8,128]{2,1,0:T(8,128)S(1)} %get-tuple-element.85), channel_id=1, source_target_pairs={{1,2},{3,4},{5,6},{7,8},{9,10},{11,12},{13,14},{2,1},{4,3},{6,5},{... | collective-permute-start | bytes 344072 | tf_op jit(solution)/shard_map/ppermute | solution.py:781
  23.8 8.7 %collective-permute-start.9 = (f32[8,128]{1,0:T(8,128)S(1)}, f32[8,128]{1,0:T(8,128)S(1)}, u32[]{:S(2)}, u32[]{:S(2)}) collective-permute-start(f32[8,128]{1,0:T(8,128)S(1)} %fusion.1.refs_4_), channel_id=1, source_target_pairs={{0,8},{1,9},{2,10},{3,11},{4,12},{5,13},{6,14},{7,15},{8,0},{9,1},... | collective-permute-start | bytes 12296 | tf_op jit(solution)/shard_map/ppermute | solution.py:795
  33.0 1.4 %collective-permute-start.10 = (f32[29,8,128]{2,1,0:T(8,128)S(1)}, f32[29,8,128]{2,1,0:T(8,128)S(1)}, u32[]{:S(2)}, u32[]{:S(2)}) collective-permute-start(f32[29,8,128]{2,1,0:T(8,128)S(1)} %get-tuple-element.95), channel_id=1, source_target_pairs={{0,1},{2,3},{4,5},{6,7},{8,9},{10,11},{12,13},{14,15},{1,0},{3,2},... | collective-permute-start | bytes 356360 | tf_op jit(solution)/shard_map/ppermute | solution.py:781
  33.1 8.0 %collective-permute-start.13 = (f32[4,8,128]{2,1,0:T(8,128)S(1)}, f32[4,8,128]{2,1,0:T(8,128)S(1)}, u32[]{:S(2)}, u32[]{:S(2)}) collective-permute-start(f32[4,8,128]{2,1,0:T(8,128)S(1)} %get-tuple-element.105), channel_id=1, source_target_pairs={{0,16},{16,0},{1,17},{17,1},{2,18},{18,2},{3,19},{19,3},{4,20},{20... | collective-permute-start | bytes 49160 | tf_op jit(solution)/shard_map/ppermute | solution.py:781
  33.7 7.4 %collective-permute-start.12 = (f32[28,8,128]{2,1,0:T(8,128)S(1)}, f32[28,8,128]{2,1,0:T(8,128)S(1)}, u32[]{:S(2)}, u32[]{:S(2)}) collective-permute-start(f32[28,8,128]{2,1,0:T(8,128)S(1)} %get-tuple-element.104), channel_id=1, source_target_pairs={{1,2},{3,4},{5,6},{7,8},{9,10},{11,12},{13,14},{2,1},{4,3},{6,5},{... | collective-permute-start | bytes 344072 | tf_op jit(solution)/shard_map/ppermute | solution.py:781
  34.4 6.3 %collective-permute-start.11 = (f32[8,128]{1,0:T(8,128)S(1)}, f32[8,128]{1,0:T(8,128)S(1)}, u32[]{:S(2)}, u32[]{:S(2)}) collective-permute-start(f32[8,128]{1,0:T(8,128)S(1)} %fusion), channel_id=1, source_target_pairs={{0,4},{1,5},{2,6},{3,7},{4,0},{5,1},{6,2},{7,3},{8,12},{9,13},{10,... | collective-permute-start | bytes 12296 | tf_op jit(solution)/shard_map/ppermute | solution.py:795
  40.8 3.6 %collective-permute-start.14 = (f32[8,128]{1,0:T(8,128)S(1)}, f32[8,128]{1,0:T(8,128)S(1)}, u32[]{:S(2)}, u32[]{:S(2)}) collective-permute-start(f32[8,128]{1,0:T(8,128)S(1)} %add.21), channel_id=1, source_target_pairs={{0,2},{1,3},{2,0},{3,1},{4,6},{5,7},{6,4},{7,5},{8,10},{9,11},{10,... | collective-permute-start | bytes 12296 | tf_op jit(solution)/shard_map/ppermute | solution.py:795

commit v6 on v4

--- a/solution.py
+++ b/solution.py
@@ -202,12 +202,15 @@
 
 def early_kernel(step):
     def kernel(ext, words, *refs):
-        fvx, ux, along, fvy, vy = refs[-6:-1] if step == 0 else refs
+        extra, fvx, ux, along, fvy, vy, extra_rows = refs
         bits = level_bits()
         if step == 0:
-            coef, coef_rows = refs[0], refs[-1]
             for k in range(NCLASS):
-                coef_rows[pl.ds(k, 1), :] = jnp.full((1, LANES), coef[k], jnp.float32)
+                extra_rows[pl.ds(k, 1), :] = jnp.full((1, LANES), extra[k], jnp.float32)
+        else:
+            for f in range(FIELDS):
+                for r in range(ROWS):
+                    extra_rows[f, r] = extra[f, pl.ds(r, 8, stride=8), :]
 
         def one_row(r, carry):
             for p, (lead, members) in enumerate(PHASES):
@@ -606,7 +609,7 @@
 
         def one_row(r, carry):
             c = carried_row(r, seams, ext, sdx, along, fvy, vy)
-            a = [adjoint[f, pl.ds(r, 8, stride=8), :] for f in range(FIELDS)]
+            a = [adjoint[f, r] for f in range(FIELDS)]
             a, terms = stepped_back(c, weight * spread(drag_ref, r + 2), a, True)
             cells[pl.ds(r + 2, 1), :] = level_sum(weight * terms)
             for f in range(FIELDS):
@@ -830,14 +833,16 @@
     ext, fvy, vy, strip, carried_ref, sfv, su, drag_ref, class_ref, low_ref, left_ref = res[:11]
     middle, before, before_edges, *payload = res[11:]
     got = exchange(*payload)
-    fvx2, ux2, along2, fvy2, vy2 = call(early_kernel(1), early, [], [middle, words])
+    fvx2, ux2, along2, fvy2, vy2, adjoint_rows = call(
+        early_kernel(1), [*early, tiles(14, 8)], [], [middle, words, adjoint]
+    )
     kept = [scratch(14, 10), scratch(14), scratch(14), scratch(4), scratch(14, 15), scratch(14, 15), scratch(4, 15)]
     part, *payload = call(
         second_kernel(has_odd),
         [tiles(14, 12), tiles(14, 12), tiles(14, 9), tiles(4, 9), tiles(14, 8), tiles(28), tiles(28), tiles(5)],
         [scratch(14), scratch(14), scratch(4), scratch(14), *kept, scratch(14), pltpu.VMEM((16, LANES), jnp.float32)],
         [middle, before, fvy2, vy2, before_edges, edge_words, along2, fvx2, ux2, words]
-        + [drag_ref, class_ref, low_ref, left_ref, adjoint, *got],
+        + [drag_ref, class_ref, low_ref, left_ref, adjoint_rows, *got],
         aliases={0: 0, 1: 1, 2: 2, 3: 3},
     )[4:]
     got = exchange(*payload)

time: 45.1 us -> 45.3 us (level)
  starting transfers between devices: 23 us -> 23.9 us
  waiting for transfers between devices: 7.64 us -> 6.87 us
    ppermute x3, starting transfers between devices: 9.8 us -> 10.7 us  [from_partner(): lax.ppermute(x, axis, [(i, i ^ distance) for i in range(lax.axis_size(axi...]
    ppermute x3, waiting for transfers between devices: 5.87 us -> 5.19 us  [from_partner(): lax.ppermute(x, axis, [(i, i ^ distance) for i in range(lax.axis_size(axi...]
where the time goes in v6:
time: 45.3 us; the launch traced here: 45.1 us
  starting transfers between devices  23.9 us (53%)
  Pallas kernels  12.3 us (27%)
  waiting for transfers between devices  6.87 us (15%)
  between operations  0.8 us (2%)
  local copies, waits for them, and re-layouts  0.66 us (1%)
  other arithmetic  0.53 us (1%)
    ppermute x12, starting transfers between devices, swap(): return lax.ppermute(x, axis, pairs + [(j, i) for i, j in pairs])  13.2 us
    pallas_call x9, Pallas kernels, call(): pl.pallas_call(kernel, out_shape=outs, in_specs=[pl.BlockSpec(memory_spac...  12.3 us
    ppermute x3, starting transfers between devices, from_partner(): lax.ppermute(x, axis, [(i, i ^ distance) for i in range(lax.axis_size(axi...  10.7 us
    ppermute x3, waiting for transfers between devices, from_partner(): lax.ppermute(x, axis, [(i, i ^ distance) for i in range(lax.axis_size(axi...  5.19 us
    ppermute x12, waiting for transfers between devices, swap(): return lax.ppermute(x, axis, pairs + [(j, i) for i, j in pairs])  1.69 us
  transfers between devices with their start and end apart: 15, of which 5 were waited for; matrix products, arithmetic and copies ran while one was open for 0% of the time, Pallas kernels for 13%

profile of v6, /device:TPU:0, one launch (start us, length us, event | category | flops | bytes accessed | tf_op | source)
XLA Modules:
  0.0 45.1 jit_solution(10837660036223018001)
XLA Ops:
  0.6 1.3 %shard_map.68 = (s32[64,128]{1,0:T(8,128)S(1)}, s32[8,128]{1,0:T(8,128)S(1)}, f32[14,12,8,128]{3,2,1,0:T(8,128)S(1)}, f32[14,8,128]{2,1,0:T(8,128)S(1)}, s32[8,1...) custom-call(f32[14,64,128]{2,1,0:T(8,128)} %bitcast.11, ...), custom_call_target="tpu_custom_call" | custom-call | tf_op jit(solution)/shard_map/pallas_call | solution.py:763
  2.0 0.5 %collective-permute-start = (f32[29,8,128]{2,1,0:T(8,128)S(1)}, f32[29,8,128]{2,1,0:T(8,128)S(1)}, u32[]{:S(2)}, u32[]{:S(2)}) collective-permute-start(f32[29,8,128]{2,1,0:T(8,128)S(1)} %get-tuple-element.63), channel_id=1, source_target_pairs={{0,1},{2,3},{4,5},{6,7},{8,9},{10,11},{12,13},{14,15},{1,0},{3,2},... | collective-permute-start | bytes 356360 | tf_op jit(solution)/shard_map/ppermute | solution.py:779
  2.5 0.7 %collective-permute-start.1 = (f32[29,8,128]{2,1,0:T(8,128)S(1)}, f32[29,8,128]{2,1,0:T(8,128)S(1)}, u32[]{:S(2)}, u32[]{:S(2)}) collective-permute-start(f32[29,8,128]{2,1,0:T(8,128)S(1)} %get-tuple-element.64), channel_id=1, source_target_pairs={{1,2},{3,4},{5,6},{7,8},{9,10},{11,12},{13,14},{2,1},{4,3},{6,5},{... | collective-permute-start | bytes 356360 | tf_op jit(solution)/shard_map/ppermute | solution.py:779
  3.2 2.6 %collective-permute-start.2 = (f32[5,8,128]{2,1,0:T(8,128)S(1)}, f32[5,8,128]{2,1,0:T(8,128)S(1)}, u32[]{:S(2)}, u32[]{:S(2)}) collective-permute-start(f32[5,8,128]{2,1,0:T(8,128)S(1)} %get-tuple-element.65), channel_id=1, source_target_pairs={{0,16},{16,0},{1,17},{17,1},{2,18},{18,2},{3,19},{19,3},{4,20},{20... | collective-permute-start | bytes 61448 | tf_op jit(solution)/shard_map/ppermute | solution.py:779
  5.8 0.7 %copy-done.1 = f32[24]{0:T(128)S(1)} copy-done((f32[24]{0:T(128)S(1)}, f32[24]{0:T(128)}, u32[]{:S(2)}) %copy-start.1) | copy-done | bytes 120
  6.4 1.7 %shard_map.69 = (f32[14,8,8,128]{3,2,1,0:T(8,128)S(1)}, f32[4,8,8,128]{3,2,1,0:T(8,128)S(1)}, f32[14,8,8,128]{3,2,1,0:T(8,128)S(1)}, f32[14,9,8,128]{3,2,1,0:T(8...) custom-call(f32[14,12,8,128]{3,2,1,0:T(8,128)S(1)} %get-tuple-element.54.ext.refs_0_, ...), custom_call_target="tpu_custom_call" | custom-call | tf_op jit(solution)/shard_map/pallas_call | solution.py:763
  8.2 0.0 copy-start
  8.2 1.3 %shard_map.70 = (f32[14,12,8,128]{3,2,1,0:T(8,128)S(1)}, f32[14,9,8,128]{3,2,1,0:T(8,128)S(1)}, f32[4,9,8,128]{3,2,1,0:T(8,128)S(1)}, f32[14,8,128]{2,1,0:T(8,12...) custom-call(f32[14,12,8,128]{3,2,1,0:T(8,128)S(1)} %get-tuple-elemen, ...), custom_call_target="tpu_custom_call", output_to_operand_aliasing={{0}: (0, {}), {1}: (1, {}), {2}: (2, {})} | custom-call | tf_op jit(solution)/shard_map/pallas_call | solution.py:763
  9.5 2.6 %collective-permute-start.3 = (f32[28,8,128]{2,1,0:T(8,128)S(1)}, f32[28,8,128]{2,1,0:T(8,128)S(1)}, u32[]{:S(2)}, u32[]{:S(2)}) collective-permute-start(f32[28,8,128]{2,1,0:T(8,128)S(1)} %get-tuple-element.80), channel_id=1, source_target_pairs={{0,1},{2,3},{4,5},{6,7},{8,9},{10,11},{12,13},{14,15},{1,0},{3,2},... | collective-permute-start | bytes 344072 | tf_op jit(solution)/shard_map/ppermute | solution.py:779
  12.1 0.7 %collective-permute-start.4 = (f32[28,8,128]{2,1,0:T(8,128)S(1)}, f32[28,8,128]{2,1,0:T(8,128)S(1)}, u32[]{:S(2)}, u32[]{:S(2)}) collective-permute-start(f32[28,8,128]{2,1,0:T(8,128)S(1)} %get-tuple-element.81), channel_id=1, source_target_pairs={{1,2},{3,4},{5,6},{7,8},{9,10},{11,12},{13,14},{2,1},{4,3},{6,5},{... | collective-permute-start | bytes 344072 | tf_op jit(solution)/shard_map/ppermute | solution.py:779
  12.8 1.0 %collective-permute-start.5 = (f32[4,8,128]{2,1,0:T(8,128)S(1)}, f32[4,8,128]{2,1,0:T(8,128)S(1)}, u32[]{:S(2)}, u32[]{:S(2)}) collective-permute-start(f32[4,8,128]{2,1,0:T(8,128)S(1)} %get-tuple-element.82), channel_id=1, source_target_pairs={{0,16},{16,0},{1,17},{17,1},{2,18},{18,2},{3,19},{19,3},{4,20},{20... | collective-permute-start | bytes 49160 | tf_op jit(solution)/shard_map/ppermute | solution.py:779
  13.7 1.3 %shard_map.71 = (f32[14,8,8,128]{3,2,1,0:T(8,128)S(1)}, f32[4,8,8,128]{3,2,1,0:T(8,128)S(1)}, f32[14,8,8,128]{3,2,1,0:T(8,128)S(1)}, f32[14,9,8,128]{3,2,1,0:T(8...) custom-call(f32[14,12,8,128]{3,2,1,0:T(8,128)S(1)} %get-tuple-element.67.ext.refs_0_, ...), custom_call_target="tpu_custom_call" | custom-call | tf_op jit(solution)/shard_map/pallas_call | solution.py:763
  15.0 1.6 %collective-permute-done.5.refs_17_ = f32[4,8,128]{2,1,0:T(8,128)S(1)} collective-permute-done((f32[4,8,128]{2,1,0:T(8,128)S(1)}, f32[4,8,128]{2,1,0:T(8,128)S(1)}, u32[]{:S(2)}, u32[]{:S(2)}) %collective-permute-start.5) | collective-permute-done | bytes 16416 | tf_op jit(solution)/shard_map/ppermute | solution.py:779
  16.6 3.3 %shard_map.72 = (f32[14,12,8,128]{3,2,1,0:T(8,128)S(1)}, f32[14,12,8,128]{3,2,1,0:T(8,128)S(1)}, f32[14,9,8,128]{3,2,1,0:T(8,128)S(1)}, f32[4,9,8,128]{3,2,1,0:T...) custom-call(f32[14,12,8,128]{3,2,1,0:T(8,128)S(1)} %get-tuple-elemen, ...), custom_call_target="tpu_custom_call", output_to_operand_aliasing={{0}: (0, {}), {1}: (1, {}), {2}: (2, {}), {3}: (3, {})} | custom-call | tf_op jit(solution)/shard_map/pallas_call | solution.py:763
  19.9 0.9 %collective-permute-start.8 = (f32[5,8,128]{2,1,0:T(8,128)S(1)}, f32[5,8,128]{2,1,0:T(8,128)S(1)}, u32[]{:S(2)}, u32[]{:S(2)}) collective-permute-start(f32[5,8,128]{2,1,0:T(8,128)S(1)} %get-tuple-element.87), channel_id=1, source_target_pairs={{0,16},{16,0},{1,17},{17,1},{2,18},{18,2},{3,19},{19,3},{4,20},{20... | collective-permute-start | bytes 61448 | tf_op jit(solution)/shard_map/ppermute | solution.py:779
  20.8 2.3 %collective-permute-start.6 = (f32[28,8,128]{2,1,0:T(8,128)S(1)}, f32[28,8,128]{2,1,0:T(8,128)S(1)}, u32[]{:S(2)}, u32[]{:S(2)}) collective-permute-start(f32[28,8,128]{2,1,0:T(8,128)S(1)} %get-tuple-element.85), channel_id=1, source_target_pairs={{0,1},{2,3},{4,5},{6,7},{8,9},{10,11},{12,13},{14,15},{1,0},{3,2},... | collective-permute-start | bytes 344072 | tf_op jit(solution)/shard_map/ppermute | solution.py:779
  23.1 0.7 %collective-permute-start.7 = (f32[28,8,128]{2,1,0:T(8,128)S(1)}, f32[28,8,128]{2,1,0:T(8,128)S(1)}, u32[]{:S(2)}, u32[]{:S(2)}) collective-permute-start(f32[28,8,128]{2,1,0:T(8,128)S(1)} %get-tuple-element.86), channel_id=1, source_target_pairs={{1,2},{3,4},{5,6},{7,8},{9,10},{11,12},{13,14},{2,1},{4,3},{6,5},{... | collective-permute-start | bytes 344072 | tf_op jit(solution)/shard_map/ppermute | solution.py:779
  23.8 6.8 %collective-permute-start.9 = (f32[8,128]{1,0:T(8,128)S(1)}, f32[8,128]{1,0:T(8,128)S(1)}, u32[]{:S(2)}, u32[]{:S(2)}) collective-permute-start(f32[8,128]{1,0:T(8,128)S(1)} %fusion.1.refs_4_), channel_id=1, source_target_pairs={{0,8},{1,9},{2,10},{3,11},{4,12},{5,13},{6,14},{7,15},{8,0},{9,1},... | collective-permute-start | bytes 12296 | tf_op jit(solution)/shard_map/ppermute | solution.py:793
  30.6 0.7 %shard_map.73 = (f32[14,8,8,128]{3,2,1,0:T(8,128)S(1)}, f32[14,10,8,128]{3,2,1,0:T(8,128)S(1)}, f32[14,8,128]{2,1,0:T(8,128)S(1)}) custom-call(f32[14,8,8,128]{3,2,1,0:T(8,128)S(1)} %get-tuple-element.83.refs_0_, f32[14,8,8,128]{3,2,1,0:T(8,128)S(1)} %get-tuple-element.84.refs_1_, ...), custom_call_target="tpu_custom_call", output_to_operand_aliasing={{0}: (0, {})} | custom-call | tf_op jit(solution)/shard_map/pallas_call | solution.py:763
  31.3 2.1 %collective-permute-done.9.refs_5_ = f32[8,128]{1,0:T(8,128)S(1)} collective-permute-done((f32[8,128]{1,0:T(8,128)S(1)}, f32[8,128]{1,0:T(8,128)S(1)}, u32[]{:S(2)}, u32[]{:S(2)}) %collective-permute-start.9) | collective-permute-done | bytes 4128 | tf_op jit(solution)/shard_map/ppermute | solution.py:793
  33.4 0.5 %shard_map.74 = (f32[29,8,128]{2,1,0:T(8,128)S(1)}, f32[28,8,128]{2,1,0:T(8,128)S(1)}, f32[4,8,128]{2,1,0:T(8,128)S(1)}, f32[14,8,128]{2,1,0:T(8,128)S(1)}, f32[...) custom-call(f32[14,10,8,128]{3,2,1,0:T(8,128)S(1)} %get-tuple-elemen, ...), custom_call_target="tpu_custom_call" | custom-call | tf_op jit(solution)/shard_map/pallas_call | solution.py:763
  33.9 0.1 collective-permute-start.10
  34.0 0.6 %collective-permute-start.12 = (f32[4,8,128]{2,1,0:T(8,128)S(1)}, f32[4,8,128]{2,1,0:T(8,128)S(1)}, u32[]{:S(2)}, u32[]{:S(2)}) collective-permute-start(f32[4,8,128]{2,1,0:T(8,128)S(1)} %get-tuple-element.104), channel_id=1, source_target_pairs={{0,16},{16,0},{1,17},{17,1},{2,18},{18,2},{3,19},{19,3},{4,20},{20... | collective-permute-start | bytes 49160 | tf_op jit(solution)/shard_map/ppermute | solution.py:779
  34.5 0.7 %collective-permute-start.11 = (f32[28,8,128]{2,1,0:T(8,128)S(1)}, f32[28,8,128]{2,1,0:T(8,128)S(1)}, u32[]{:S(2)}, u32[]{:S(2)}) collective-permute-start(f32[28,8,128]{2,1,0:T(8,128)S(1)} %get-tuple-element.103), channel_id=1, source_target_pairs={{1,2},{3,4},{5,6},{7,8},{9,10},{11,12},{13,14},{2,1},{4,3},{6,5},{... | collective-permute-start | bytes 344072 | tf_op jit(solution)/shard_map/ppermute | solution.py:779
  35.2 0.1 collective-permute-done.10.refs_1_
  35.3 2.9 %collective-permute-start.13 = (f32[8,128]{1,0:T(8,128)S(1)}, f32[8,128]{1,0:T(8,128)S(1)}, u32[]{:S(2)}, u32[]{:S(2)}) collective-permute-start(f32[8,128]{1,0:T(8,128)S(1)} %fusion), channel_id=1, source_target_pairs={{0,4},{1,5},{2,6},{3,7},{4,0},{5,1},{6,2},{7,3},{8,12},{9,13},{10,... | collective-permute-start | bytes 12296 | tf_op jit(solution)/shard_map/ppermute | solution.py:793
  38.2 2.7 %collective-permute-done.13 = f32[8,128]{1,0:T(8,128)S(1)} collective-permute-done((f32[8,128]{1,0:T(8,128)S(1)}, f32[8,128]{1,0:T(8,128)S(1)}, u32[]{:S(2)}, u32[]{:S(2)}) %collective-permute-start.13) | collective-permute-done | bytes 4128 | tf_op jit(solution)/shard_map/ppermute | solution.py:793
  41.0 1.0 %collective-permute-start.14 = (f32[8,128]{1,0:T(8,128)S(1)}, f32[8,128]{1,0:T(8,128)S(1)}, u32[]{:S(2)}, u32[]{:S(2)}) collective-permute-start(f32[8,128]{1,0:T(8,128)S(1)} %add.21), channel_id=1, source_target_pairs={{0,2},{1,3},{2,0},{3,1},{4,6},{5,7},{6,4},{7,5},{8,10},{9,11},{10,... | collective-permute-start | bytes 12296 | tf_op jit(solution)/shard_map/ppermute | solution.py:793
  41.9 1.2 %shard_map.75.refs_0_ = f32[14,8,8,128]{3,2,1,0:T(8,128)S(1)} custom-call(f32[14,12,8,128]{3,2,1,0:T(8,128)S(1)} %get-tuple-element.66.ext, s32[64,128]{1,0:T(8,128)S(1)} %get-tuple-element.55.words.refs_6_.refs_9_.refs_3_, f32[14,10,8,128]{3,2,1,0:T(8,128)S(1)} %get-tuple-element.88.a_ext, f32[14,8,8,128]{3,2,1,0:T(8,128)S(1)} %get-tuple-element.89.fvx, ...), custom_call_target="tpu_custom_call" | custom-call | tf_op jit(solution)/shard_map/pallas_call | solution.py:763
  43.2 1.1 %shard_map.76 = (f32[14,64,128]{2,1,0:T(8,128)}, f32[14,8,8,128]{3,2,1,0:T(8,128)S(1)}) custom-call(f32[14,8,8,128]{3,2,1,0:T(8,128)S(1)} %shard_map.75.refs_0_, f32[29,8,128]{2,1,0:T(8,128)S(1)} %collective-permute-done.10.refs_1_, f32[28,8,128]{2,1,0:T(8,128)S(1)} %collective-permute-done.11.refs_2_, ...), custom_call_target="tpu_custom_call", output_to_operand_aliasing={{1}: (0, {})} | custom-call | tf_op jit(solution)/shard_map/pallas_call | solution.py:763
  44.2 0.4 collective-permute-done.14
  44.6 0.5 %multiply_bitcast_fusion = f32[24]{0:T(128)} fusion(f32[8,128]{1,0:T(8,128)S(1)} %add.22), kind=kLoop, calls=%fused_computation.4 | loop fusion | flops 24 | bytes 192 | tf_op jit(solution)/shard_map/mul | solution.py:883
  (16 shorter events, 0.0 us)
Async XLA Ops:
  2.0 6.2 %collective-permute-start = (f32[29,8,128]{2,1,0:T(8,128)S(1)}, f32[29,8,128]{2,1,0:T(8,128)S(1)}, u32[]{:S(2)}, u32[]{:S(2)}) collective-permute-start(f32[29,8,128]{2,1,0:T(8,128)S(1)} %get-tuple-element.63), channel_id=1, source_target_pairs={{0,1},{2,3},{4,5},{6,7},{8,9},{10,11},{12,13},{14,15},{1,0},{3,2},... | collective-permute-start | bytes 356360 | tf_op jit(solution)/shard_map/ppermute | solution.py:779
  2.5 5.7 %collective-permute-start.1 = (f32[29,8,128]{2,1,0:T(8,128)S(1)}, f32[29,8,128]{2,1,0:T(8,128)S(1)}, u32[]{:S(2)}, u32[]{:S(2)}) collective-permute-start(f32[29,8,128]{2,1,0:T(8,128)S(1)} %get-tuple-element.64), channel_id=1, source_target_pairs={{1,2},{3,4},{5,6},{7,8},{9,10},{11,12},{13,14},{2,1},{4,3},{6,5},{... | collective-permute-start | bytes 356360 | tf_op jit(solution)/shard_map/ppermute | solution.py:779
  3.2 5.0 %collective-permute-start.2 = (f32[5,8,128]{2,1,0:T(8,128)S(1)}, f32[5,8,128]{2,1,0:T(8,128)S(1)}, u32[]{:S(2)}, u32[]{:S(2)}) collective-permute-start(f32[5,8,128]{2,1,0:T(8,128)S(1)} %get-tuple-element.65), channel_id=1, source_target_pairs={{0,16},{16,0},{1,17},{17,1},{2,18},{18,2},{3,19},{19,3},{4,20},{20... | collective-permute-start | bytes 61448 | tf_op jit(solution)/shard_map/ppermute | solution.py:779
  5.8 0.7 %copy-start.1 = (f32[24]{0:T(128)S(1)}, f32[24]{0:T(128)}, u32[]{:S(2)}) copy-start(f32[24]{0:T(128)} %refs_0_.1) | copy-start | bytes 292
  8.2 5.5 %copy-start = (f32[14,8,8,128]{3,2,1,0:T(8,128)S(1)}, f32[14,8,8,128]{3,2,1,0:T(8,128)}, u32[]{:S(2)}) copy-start(f32[14,8,8,128]{3,2,1,0:T(8,128)} %param.6) | copy-start | bytes 1376260
  9.5 7.1 %collective-permute-start.3 = (f32[28,8,128]{2,1,0:T(8,128)S(1)}, f32[28,8,128]{2,1,0:T(8,128)S(1)}, u32[]{:S(2)}, u32[]{:S(2)}) collective-permute-start(f32[28,8,128]{2,1,0:T(8,128)S(1)} %get-tuple-element.80), channel_id=1, source_target_pairs={{0,1},{2,3},{4,5},{6,7},{8,9},{10,11},{12,13},{14,15},{1,0},{3,2},... | collective-permute-start | bytes 344072 | tf_op jit(solution)/shard_map/ppermute | solution.py:779
  12.1 4.5 %collective-permute-start.4 = (f32[28,8,128]{2,1,0:T(8,128)S(1)}, f32[28,8,128]{2,1,0:T(8,128)S(1)}, u32[]{:S(2)}, u32[]{:S(2)}) collective-permute-start(f32[28,8,128]{2,1,0:T(8,128)S(1)} %get-tuple-element.81), channel_id=1, source_target_pairs={{1,2},{3,4},{5,6},{7,8},{9,10},{11,12},{13,14},{2,1},{4,3},{6,5},{... | collective-permute-start | bytes 344072 | tf_op jit(solution)/shard_map/ppermute | solution.py:779
  12.8 3.8 %collective-permute-start.5 = (f32[4,8,128]{2,1,0:T(8,128)S(1)}, f32[4,8,128]{2,1,0:T(8,128)S(1)}, u32[]{:S(2)}, u32[]{:S(2)}) collective-permute-start(f32[4,8,128]{2,1,0:T(8,128)S(1)} %get-tuple-element.82), channel_id=1, source_target_pairs={{0,16},{16,0},{1,17},{17,1},{2,18},{18,2},{3,19},{19,3},{4,20},{20... | collective-permute-start | bytes 49160 | tf_op jit(solution)/shard_map/ppermute | solution.py:779
  19.9 3.9 %collective-permute-start.8 = (f32[5,8,128]{2,1,0:T(8,128)S(1)}, f32[5,8,128]{2,1,0:T(8,128)S(1)}, u32[]{:S(2)}, u32[]{:S(2)}) collective-permute-start(f32[5,8,128]{2,1,0:T(8,128)S(1)} %get-tuple-element.87), channel_id=1, source_target_pairs={{0,16},{16,0},{1,17},{17,1},{2,18},{18,2},{3,19},{19,3},{4,20},{20... | collective-permute-start | bytes 61448 | tf_op jit(solution)/shard_map/ppermute | solution.py:779
  20.8 9.8 %collective-permute-start.6 = (f32[28,8,128]{2,1,0:T(8,128)S(1)}, f32[28,8,128]{2,1,0:T(8,128)S(1)}, u32[]{:S(2)}, u32[]{:S(2)}) collective-permute-start(f32[28,8,128]{2,1,0:T(8,128)S(1)} %get-tuple-element.85), channel_id=1, source_target_pairs={{0,1},{2,3},{4,5},{6,7},{8,9},{10,11},{12,13},{14,15},{1,0},{3,2},... | collective-permute-start | bytes 344072 | tf_op jit(solution)/shard_map/ppermute | solution.py:779
  23.1 7.5 %collective-permute-start.7 = (f32[28,8,128]{2,1,0:T(8,128)S(1)}, f32[28,8,128]{2,1,0:T(8,128)S(1)}, u32[]{:S(2)}, u32[]{:S(2)}) collective-permute-start(f32[28,8,128]{2,1,0:T(8,128)S(1)} %get-tuple-element.86), channel_id=1, source_target_pairs={{1,2},{3,4},{5,6},{7,8},{9,10},{11,12},{13,14},{2,1},{4,3},{6,5},{... | collective-permute-start | bytes 344072 | tf_op jit(solution)/shard_map/ppermute | solution.py:779
  23.8 9.6 %collective-permute-start.9 = (f32[8,128]{1,0:T(8,128)S(1)}, f32[8,128]{1,0:T(8,128)S(1)}, u32[]{:S(2)}, u32[]{:S(2)}) collective-permute-start(f32[8,128]{1,0:T(8,128)S(1)} %fusion.1.refs_4_), channel_id=1, source_target_pairs={{0,8},{1,9},{2,10},{3,11},{4,12},{5,13},{6,14},{7,15},{8,0},{9,1},... | collective-permute-start | bytes 12296 | tf_op jit(solution)/shard_map/ppermute | solution.py:793
  33.9 1.4 %collective-permute-start.10 = (f32[29,8,128]{2,1,0:T(8,128)S(1)}, f32[29,8,128]{2,1,0:T(8,128)S(1)}, u32[]{:S(2)}, u32[]{:S(2)}) collective-permute-start(f32[29,8,128]{2,1,0:T(8,128)S(1)} %get-tuple-element.102), channel_id=1, source_target_pairs={{0,1},{2,3},{4,5},{6,7},{8,9},{10,11},{12,13},{14,15},{1,0},{3,2},... | collective-permute-start | bytes 356360 | tf_op jit(solution)/shard_map/ppermute | solution.py:779
  34.0 9.2 %collective-permute-start.12 = (f32[4,8,128]{2,1,0:T(8,128)S(1)}, f32[4,8,128]{2,1,0:T(8,128)S(1)}, u32[]{:S(2)}, u32[]{:S(2)}) collective-permute-start(f32[4,8,128]{2,1,0:T(8,128)S(1)} %get-tuple-element.104), channel_id=1, source_target_pairs={{0,16},{16,0},{1,17},{17,1},{2,18},{18,2},{3,19},{19,3},{4,20},{20... | collective-permute-start | bytes 49160 | tf_op jit(solution)/shard_map/ppermute | solution.py:779
  34.5 8.6 %collective-permute-start.11 = (f32[28,8,128]{2,1,0:T(8,128)S(1)}, f32[28,8,128]{2,1,0:T(8,128)S(1)}, u32[]{:S(2)}, u32[]{:S(2)}) collective-permute-start(f32[28,8,128]{2,1,0:T(8,128)S(1)} %get-tuple-element.103), channel_id=1, source_target_pairs={{1,2},{3,4},{5,6},{7,8},{9,10},{11,12},{13,14},{2,1},{4,3},{6,5},{... | collective-permute-start | bytes 344072 | tf_op jit(solution)/shard_map/ppermute | solution.py:779
  35.3 5.7 %collective-permute-start.13 = (f32[8,128]{1,0:T(8,128)S(1)}, f32[8,128]{1,0:T(8,128)S(1)}, u32[]{:S(2)}, u32[]{:S(2)}) collective-permute-start(f32[8,128]{1,0:T(8,128)S(1)} %fusion), channel_id=1, source_target_pairs={{0,4},{1,5},{2,6},{3,7},{4,0},{5,1},{6,2},{7,3},{8,12},{9,13},{10,... | collective-permute-start | bytes 12296 | tf_op jit(solution)/shard_map/ppermute | solution.py:793
  41.0 3.6 %collective-permute-start.14 = (f32[8,128]{1,0:T(8,128)S(1)}, f32[8,128]{1,0:T(8,128)S(1)}, u32[]{:S(2)}, u32[]{:S(2)}) collective-permute-start(f32[8,128]{1,0:T(8,128)S(1)} %add.21), channel_id=1, source_target_pairs={{0,2},{1,3},{2,0},{3,1},{4,6},{5,7},{6,4},{7,5},{8,10},{9,11},{10,... | collective-permute-start | bytes 12296 | tf_op jit(solution)/shard_map/ppermute | solution.py:793
